TPU v7x, 32 devices: a whole 2x2x4 slice. The times are simulated.
32 devices in a mesh: beam: 2 (over y), chan: 16 (over z, x, core).
Axes of the slice: x: 2, y: 2, z: 4, core: 2. Of those that a mesh axis runs over, the one named last changes fastest.
Arguments:
- filterbank: bfloat16 [2048, 4096], P(('beam', 'chan')), parts along dimension 0
- shift_table: int32 [511], replicated, may hold values from 0 to 511, as said below
- box_widths: int32 [8], replicated, may hold values from 1 to 255, as said below
Outputs:
- dedispersed: bfloat16 [512, 4096], P(('beam', 'chan')), parts along dimension 0
- peaks: float32 [16, 256], P('beam', 'chan'), parts along dimension 0
There are 2 independent parts, one for each index of `beam`. A program takes and returns all parts, laid end to end along the dimension named above; an argument that names none is the same for every part. Nothing has to cross between parts.
Inputs may be any that keep to these rules, and one draw needn't show every extreme that they name: `shift_table`: entry k - 1 + j, for k a power of two up to 256 and j < k, is the delay for merged trial j of a section with k trials; it equals 2 j or 2 j + 1. `box_widths`: entry i lies between 2**i and 2**(i+1) - 1.
All inputs are finite; a program needn't handle non-finite values.
Results may differ from a plain program's by a relative error of at most 0.001.
Values sent between devices are 32-bit elements; how exact they have to be, the bound alone decides.
No kernel may reach another device: no remote copies, remote signals or barrier semaphores. Data moves between devices by JAX's collectives and lax.ppermute only.
A program may use at most 64 MiB of HBM per device.

v0:
```python
import jax
import jax.numpy as jnp
from jax import lax
from jax.sharding import PartitionSpec as P

ROWS = 16


epsilon = 1e-05


def swapped(block, axis, bit):
    count = lax.axis_size(axis)
    route = []
    for low in range(count):
        high = low | 1 << bit
        if high != low and high < count:
            route += [(low, high), (high, low)]
    return lax.ppermute(block, axis, route)


def advance(rows_in, shifts, start):
    length = rows_in.shape[-1]
    count = rows_in.shape[-2]
    leading = rows_in.shape[:-2]
    last_axis = rows_in.ndim - 1
    padded = jnp.concatenate([rows_in, jnp.zeros_like(rows_in)], axis=last_axis)
    base = jnp.minimum(2 * start, length)
    moved = lax.dynamic_slice_in_dim(padded, base, length, last_axis)
    width = length + 2 * count
    wide = jnp.concatenate(
        [moved, jnp.zeros(leading + (count, 2 * count), moved.dtype)], axis=last_axis
    )
    flat = wide.reshape(leading + (count * width,))
    flat = jnp.concatenate(
        [flat, jnp.zeros(leading + (2 * count,), moved.dtype)], axis=last_axis - 1
    )
    skewed = flat.reshape(leading + (count, width + 2))[..., :length]
    odd_moved = jnp.concatenate(
        [skewed[..., 1:], jnp.zeros(leading + (count, 1), moved.dtype)], axis=last_axis
    )
    parity = shifts - 2 * (start + jnp.arange(count, dtype=jnp.int32))
    return jnp.where((parity == 1)[:, None], odd_moved, skewed)


def merge_pairs(subbands, shift_table, trials_now):
    paired = subbands.reshape(subbands.shape[0] // 2, 2, subbands.shape[1], subbands.shape[2])
    lower_rows = paired[:, 0]
    upper_rows = paired[:, 1]
    if trials_now > subbands.shape[1]:
        lower_rows = jnp.repeat(lower_rows, 2, axis=1)
        upper_rows = jnp.repeat(upper_rows, 2, axis=1)
    return lower_rows + advance(upper_rows, shift_table[trials_now - 1 : 2 * trials_now - 1], 0)


def local_tree(spectra, shift_table):
    chan_count = spectra.shape[0]
    subbands = spectra[:, None, :]
    band_span = 1
    while band_span < chan_count:
        band_span *= 2
        subbands = merge_pairs(subbands, shift_table, max(1, band_span * ROWS // chan_count))
    return subbands[0]


def flat_tree(channel_mean, shift_table, chan_count):
    subband = channel_mean[None, :]
    band_span = 1
    while band_span < chan_count:
        band_span *= 2
        trials_now = max(1, band_span * ROWS // chan_count)
        if trials_now > subband.shape[0]:
            subband = jnp.repeat(subband, 2, axis=0)
        subband = subband + advance(subband, shift_table[trials_now - 1 : 2 * trials_now - 1], 0)
    return subband


def normalize(channel_block):
    values = channel_block.astype(jnp.float32)
    centre = jnp.mean(values, axis=1, keepdims=True)
    spread = jnp.mean(jnp.square(values - centre), axis=1, keepdims=True)
    return (values - centre) * lax.rsqrt(spread + epsilon)


def boxcar_peaks(scaled, box_widths):
    length = scaled.shape[1]
    running = jnp.cumsum(scaled, axis=1)
    padded = jnp.concatenate([jnp.zeros_like(running), running], axis=1)

    def single(box_width):
        earlier = lax.dynamic_slice_in_dim(padded, length - box_width, length, 1)
        box_sums = (running - earlier) * lax.rsqrt(box_width.astype(jnp.float32))
        return jnp.max(box_sums, axis=1)

    return lax.map(single, box_widths)


def shards(filterbank, shift_table, box_widths):
    chan_count = filterbank.shape[0]
    half_rows = ROWS // 2
    section_count = lax.axis_size("chan").bit_length() - 1
    normal = normalize(filterbank)
    partial_value = jnp.sum(normal, axis=0)
    current = local_tree(normal, shift_table)
    device_index = lax.axis_index("chan")
    position = jnp.zeros((), jnp.int32)
    for bit_number in range(section_count):
        upper_side = device_index >> bit_number & 1
        trials_now = 2 * ROWS * (1 << bit_number)
        payload = jnp.concatenate([current, partial_value[None, :]], axis=0)
        arrived = swapped(payload, "chan", bit_number)
        received = arrived[:ROWS]
        partial_value = partial_value + arrived[ROWS]
        lower_all = jnp.where(upper_side == 0, current, received)
        upper_all = jnp.where(upper_side == 0, received, current)
        lower_rows = lax.dynamic_slice_in_dim(lower_all, upper_side * half_rows, half_rows, 0)
        upper_rows = lax.dynamic_slice_in_dim(upper_all, upper_side * half_rows, half_rows, 0)
        first_trial = 2 * (position * ROWS + upper_side * half_rows)
        shifts = lax.dynamic_slice_in_dim(shift_table, trials_now - 1 + first_trial, ROWS)
        current = jnp.repeat(lower_rows, 2, axis=0) + advance(
            jnp.repeat(upper_rows, 2, axis=0), shifts, first_trial
        )
        position = 2 * position + upper_side
    channel_mean = partial_value / (chan_count * lax.axis_size("chan"))
    mean_rows = flat_tree(channel_mean, shift_table, chan_count)
    place = jnp.zeros((), jnp.int32)
    for bit_number in range(section_count):
        side = device_index >> bit_number & 1
        trials_now = 2 * ROWS * (1 << bit_number)
        mean_half = lax.dynamic_slice_in_dim(mean_rows, side * half_rows, half_rows, 0)
        first_trial = 2 * (place * ROWS + side * half_rows)
        shifts = lax.dynamic_slice_in_dim(shift_table, trials_now - 1 + first_trial, ROWS)
        doubled = jnp.repeat(mean_half, 2, axis=0)
        mean_rows = doubled + advance(doubled, shifts, first_trial)
        place = 2 * place + side
    current = current - mean_rows
    centre = jnp.mean(current, axis=1, keepdims=True)
    spread = jnp.mean(jnp.square(current - centre), axis=1, keepdims=True)
    scaled = (current - centre) * lax.rsqrt(spread + epsilon)
    dedispersed = scaled.astype(jnp.bfloat16)
    peaks = boxcar_peaks(scaled, box_widths)
    return (dedispersed, peaks)


def solution(mesh):
    placed = (P(("beam", "chan"), None), P(), P())
    return jax.shard_map(
        shards,
        mesh=mesh,
        in_specs=placed,
        out_specs=(P(("beam", "chan"), None), P("beam", "chan")),
        check_vma=False,
    )
```

profile of v0, /device:TPU:0, one launch (start us, length us, event | category | flops | bytes accessed | tf_op | source)
XLA Modules:
  0.0 118.3 jit_solution(13654196649057623181)
XLA Ops:
  0.7 1.3 %slice.229 = s32[1]{0:T(128)} slice(s32[511]{0:T(512)} %param.6), slice={[0:1]} | slice | bytes 8 | tf_op jit(solution)/shard_map/slice | solution.py:53
  1.9 0.8 subtract_compare_fusion.7
  2.8 1.2 %convert_reduce_fusion = f32[64]{0:T(128)S(1)} fusion(bf16[64,4096]{1,0:T(8,128)(2,1)} %param.5), kind=kLoop, calls=%fused_computation.2 | loop fusion | flops 524224 | bytes 524544 | tf_op jit(solution)/shard_map/reduce_sum | solution.py:80
  4.1 0.3 fusion.2
  4.4 0.2 fusion
  4.6 0.6 reshape_broadcast_in_dim.3
  5.2 0.6 slice.296
  5.8 0.3 copy.31
  6.2 0.4 reshape.282
  6.6 1.2 slice.297
  8.4 0.8 fusion.3
  9.8 0.3 reshape.286
  10.4 0.2 reshape.289
  10.7 0.2 reshape.290
  10.9 0.3 slice.305
  11.4 0.2 fusion.15
  11.7 0.2 reshape.292
  12.1 0.2 reshape.293
  12.4 0.3 reshape.294
  12.7 0.3 reshape.295
  13.9 0.4 reshape.299
  14.4 0.3 reshape.300
  15.6 0.4 reshape.302
  16.0 0.7 pad_reduce_fusion
  17.4 0.5 collective-permute-start
  17.9 1.3 %collective-permute-done = f32[17,4096]{1,0:T(8,128)S(1)} collective-permute-done((f32[17,4096]{1,0:T(8,128)S(1)}, f32[17,4096]{1,0:T(8,128)S(1)}, u32[]{:S(2)}, u32[]{:S(2)}) %collective-permute-start) | collective-permute-done | bytes 278560 | tf_op jit(solution)/shard_map/ppermute | solution.py:19
  20.9 2.9 %collective-permute-start.1 = (f32[17,4096]{1,0:T(8,128)S(1)}, f32[17,4096]{1,0:T(8,128)S(1)}, u32[]{:S(2)}, u32[]{:S(2)}) collective-permute-start(f32[17,4096]{1,0:T(8,128)S(1)} %pad_maximum_fusion.1), channel_id=1, source_target_pairs={{0,2},{2,0},{1,3},{3,1},{4,6},{6,4},{5,7},{7,5},{8,10},{10,8},{9,1... | collective-permute-start | bytes 835592 | tf_op jit(solution)/shard_map/ppermute | solution.py:19
  23.8 9.4 %collective-permute-done.1 = f32[17,4096]{1,0:T(8,128)S(1)} collective-permute-done((f32[17,4096]{1,0:T(8,128)S(1)}, f32[17,4096]{1,0:T(8,128)S(1)}, u32[]{:S(2)}, u32[]{:S(2)}) %collective-permute-start.1) | collective-permute-done | bytes 278560 | tf_op jit(solution)/shard_map/ppermute | solution.py:19
  34.8 1.9 %collective-permute-start.2 = (f32[17,4096]{1,0:T(8,128)S(1)}, f32[17,4096]{1,0:T(8,128)S(1)}, u32[]{:S(2)}, u32[]{:S(2)}) collective-permute-start(f32[17,4096]{1,0:T(8,128)S(1)} %pad_maximum_fusion.2), channel_id=1, source_target_pairs={{0,4},{4,0},{1,5},{5,1},{2,6},{6,2},{3,7},{7,3},{8,12},{12,8},{9,1... | collective-permute-start | bytes 835592 | tf_op jit(solution)/shard_map/ppermute | solution.py:19
  36.6 8.8 %collective-permute-done.2 = f32[17,4096]{1,0:T(8,128)S(1)} collective-permute-done((f32[17,4096]{1,0:T(8,128)S(1)}, f32[17,4096]{1,0:T(8,128)S(1)}, u32[]{:S(2)}, u32[]{:S(2)}) %collective-permute-start.2) | collective-permute-done | bytes 278560 | tf_op jit(solution)/shard_map/ppermute | solution.py:19
  47.0 2.6 %collective-permute-start.3 = (f32[17,4096]{1,0:T(8,128)S(1)}, f32[17,4096]{1,0:T(8,128)S(1)}, u32[]{:S(2)}, u32[]{:S(2)}) collective-permute-start(f32[17,4096]{1,0:T(8,128)S(1)} %pad_maximum_fusion.3), channel_id=1, source_target_pairs={{0,8},{8,0},{1,9},{9,1},{2,10},{10,2},{3,11},{11,3},{4,12},{12,4},... | collective-permute-start | bytes 835592 | tf_op jit(solution)/shard_map/ppermute | solution.py:19
  49.9 16.2 %collective-permute-done.3 = f32[17,4096]{1,0:T(8,128)S(1)} collective-permute-done((f32[17,4096]{1,0:T(8,128)S(1)}, f32[17,4096]{1,0:T(8,128)S(1)}, u32[]{:S(2)}, u32[]{:S(2)}) %collective-permute-start.3) | collective-permute-done | bytes 278560 | tf_op jit(solution)/shard_map/ppermute | solution.py:19
  72.2 0.7 copy-done.1
  73.0 0.9 slice-done
  76.3 0.3 fusion.32
  76.8 0.8 multiply_bitcast_fusion
  77.6 4.6 %reduce-window.6 = f32[16,32,128]{2,1,0:T(8,128)S(1)} reduce-window(f32[16,32,128]{2,1,0:T(8,128)S(1)} %bitcast.76, f32[]{:T(128)} %constant.50.clone.1), window={size=1x1x128 pad=0_0x0_0x127_0}, to_apply=%region_5.6 | reduce-window | flops 8323072 | bytes 524292 | tf_op jit(solution)/shard_map/reduce-window
  82.2 0.3 slice_reduce_fusion
  83.0 0.6 copy-done.3
  83.6 34.6 %while.12 = (s32[]{:T(128)}, f32[8,16]{1,0:T(8,128)}, s32[8]{0:T(128)S(1)}, f32[16,8192]{1,0:T(8,128)S(1)}, f32[16,4096]{1,0:T(8,128)S(1)}, /*index=5*/s32[]{:T(128)}, s32[1]{0:T(128)}, s32[]{:T(128)}, s32[1]{0:T(128)}) while((s32[]{:T(128)}, f32[8,16]{1,0:T(8,128)}, s32[8]{0:T(128)S(1)}, f32[16,8192]{1,0:T(8,128)S(1)}, ...), condition=%wide.region_9.10_spmd, body=%wide.region_7.9_spmd.sunk | while | flops 196599 | bytes 524667 | solution.py:95
  83.6 0.7 dynamic_slice.201
  86.4 0.2 multiply_reduce_fusion.3
  86.7 1.3 %dynamic_update_slice.8 = f32[8,16]{1,0:T(8,128)} dynamic-update-slice(f32[8,16]{1,0:T(8,128)} %get-tuple-element.149, f32[1,16]{1,0:T(1,128)S(1)} %bitcast.85, s32[]{:T(128)S(6)} %copy.38, s32[]{:T(128)} %constant.48.clone.1..sunk) | dynamic-update-slice | bytes 132 | tf_op jit(solution)/shard_map/while/body/jit(dynamic_update_index_in_dim)/dynamic_update_slice | solution.py:95
  88.0 0.7 dynamic_slice.201
  90.8 0.2 multiply_reduce_fusion.3
  91.0 1.3 %dynamic_update_slice.8 = f32[8,16]{1,0:T(8,128)} dynamic-update-slice(f32[8,16]{1,0:T(8,128)} %get-tuple-element.149, f32[1,16]{1,0:T(1,128)S(1)} %bitcast.85, s32[]{:T(128)S(6)} %copy.38, s32[]{:T(128)} %constant.48.clone.1..sunk) | dynamic-update-slice | bytes 132 | tf_op jit(solution)/shard_map/while/body/jit(dynamic_update_index_in_dim)/dynamic_update_slice | solution.py:95
  92.3 0.7 dynamic_slice.201
  95.1 0.2 multiply_reduce_fusion.3
  95.3 1.3 %dynamic_update_slice.8 = f32[8,16]{1,0:T(8,128)} dynamic-update-slice(f32[8,16]{1,0:T(8,128)} %get-tuple-element.149, f32[1,16]{1,0:T(1,128)S(1)} %bitcast.85, s32[]{:T(128)S(6)} %copy.38, s32[]{:T(128)} %constant.48.clone.1..sunk) | dynamic-update-slice | bytes 132 | tf_op jit(solution)/shard_map/while/body/jit(dynamic_update_index_in_dim)/dynamic_update_slice | solution.py:95
  96.6 0.7 dynamic_slice.201
  99.4 0.2 multiply_reduce_fusion.3
  99.7 1.3 %dynamic_update_slice.8 = f32[8,16]{1,0:T(8,128)} dynamic-update-slice(f32[8,16]{1,0:T(8,128)} %get-tuple-element.149, f32[1,16]{1,0:T(1,128)S(1)} %bitcast.85, s32[]{:T(128)S(6)} %copy.38, s32[]{:T(128)} %constant.48.clone.1..sunk) | dynamic-update-slice | bytes 132 | tf_op jit(solution)/shard_map/while/body/jit(dynamic_update_index_in_dim)/dynamic_update_slice | solution.py:95
  101.0 0.7 dynamic_slice.201
  103.7 0.2 multiply_reduce_fusion.3
  104.0 1.3 %dynamic_update_slice.8 = f32[8,16]{1,0:T(8,128)} dynamic-update-slice(f32[8,16]{1,0:T(8,128)} %get-tuple-element.149, f32[1,16]{1,0:T(1,128)S(1)} %bitcast.85, s32[]{:T(128)S(6)} %copy.38, s32[]{:T(128)} %constant.48.clone.1..sunk) | dynamic-update-slice | bytes 132 | tf_op jit(solution)/shard_map/while/body/jit(dynamic_update_index_in_dim)/dynamic_update_slice | solution.py:95
  105.3 0.7 dynamic_slice.201
  108.1 0.2 multiply_reduce_fusion.3
  108.3 1.3 %dynamic_update_slice.8 = f32[8,16]{1,0:T(8,128)} dynamic-update-slice(f32[8,16]{1,0:T(8,128)} %get-tuple-element.149, f32[1,16]{1,0:T(1,128)S(1)} %bitcast.85, s32[]{:T(128)S(6)} %copy.38, s32[]{:T(128)} %constant.48.clone.1..sunk) | dynamic-update-slice | bytes 132 | tf_op jit(solution)/shard_map/while/body/jit(dynamic_update_index_in_dim)/dynamic_update_slice | solution.py:95
  109.6 0.7 dynamic_slice.201
  112.4 0.2 multiply_reduce_fusion.3
  112.7 1.3 %dynamic_update_slice.8 = f32[8,16]{1,0:T(8,128)} dynamic-update-slice(f32[8,16]{1,0:T(8,128)} %get-tuple-element.149, f32[1,16]{1,0:T(1,128)S(1)} %bitcast.85, s32[]{:T(128)S(6)} %copy.38, s32[]{:T(128)} %constant.48.clone.1..sunk) | dynamic-update-slice | bytes 132 | tf_op jit(solution)/shard_map/while/body/jit(dynamic_update_index_in_dim)/dynamic_update_slice | solution.py:95
  114.0 0.7 dynamic_slice.201
  116.7 0.3 multiply_reduce_fusion.3
  117.0 1.3 %dynamic_update_slice.8 = f32[8,16]{1,0:T(8,128)} dynamic-update-slice(f32[8,16]{1,0:T(8,128)} %get-tuple-element.149, f32[1,16]{1,0:T(1,128)S(1)} %bitcast.85, s32[]{:T(128)S(6)} %copy.38, s32[]{:T(128)} %constant.48.clone.1..sunk) | dynamic-update-slice | bytes 132 | tf_op jit(solution)/shard_map/while/body/jit(dynamic_update_index_in_dim)/dynamic_update_slice | solution.py:95
  (201 shorter events, 17.1 us)
Async XLA Ops:
  0.6 2.0 %copy-start.2 = (s32[511]{0:T(512)S(1)}, s32[511]{0:T(512)}, u32[]{:S(2)}) copy-start(s32[511]{0:T(512)} %param.6) | copy-start | bytes 6136
  0.6 3.4 %copy-start = (bf16[64,4096]{1,0:T(8,128)(2,1)S(1)}, bf16[64,4096]{1,0:T(8,128)(2,1)}, u32[]{:S(2)}) copy-start(bf16[64,4096]{1,0:T(8,128)(2,1)} %param.5) | copy-start | bytes 1572868
  17.4 1.9 %collective-permute-start = (f32[17,4096]{1,0:T(8,128)S(1)}, f32[17,4096]{1,0:T(8,128)S(1)}, u32[]{:S(2)}, u32[]{:S(2)}) collective-permute-start(f32[17,4096]{1,0:T(8,128)S(1)} %pad_maximum_fusion), channel_id=1, source_target_pairs={{0,1},{1,0},{2,3},{3,2},{4,5},{5,4},{6,7},{7,6},{8,9},{9,8},{10,11... | collective-permute-start | bytes 835592 | tf_op jit(solution)/shard_map/ppermute | solution.py:19
  20.9 12.3 %collective-permute-start.1 = (f32[17,4096]{1,0:T(8,128)S(1)}, f32[17,4096]{1,0:T(8,128)S(1)}, u32[]{:S(2)}, u32[]{:S(2)}) collective-permute-start(f32[17,4096]{1,0:T(8,128)S(1)} %pad_maximum_fusion.1), channel_id=1, source_target_pairs={{0,2},{2,0},{1,3},{3,1},{4,6},{6,4},{5,7},{7,5},{8,10},{10,8},{9,1... | collective-permute-start | bytes 835592 | tf_op jit(solution)/shard_map/ppermute | solution.py:19
  34.8 10.7 %collective-permute-start.2 = (f32[17,4096]{1,0:T(8,128)S(1)}, f32[17,4096]{1,0:T(8,128)S(1)}, u32[]{:S(2)}, u32[]{:S(2)}) collective-permute-start(f32[17,4096]{1,0:T(8,128)S(1)} %pad_maximum_fusion.2), channel_id=1, source_target_pairs={{0,4},{4,0},{1,5},{5,1},{2,6},{6,2},{3,7},{7,3},{8,12},{12,8},{9,1... | collective-permute-start | bytes 835592 | tf_op jit(solution)/shard_map/ppermute | solution.py:19
  47.0 19.1 %collective-permute-start.3 = (f32[17,4096]{1,0:T(8,128)S(1)}, f32[17,4096]{1,0:T(8,128)S(1)}, u32[]{:S(2)}, u32[]{:S(2)}) collective-permute-start(f32[17,4096]{1,0:T(8,128)S(1)} %pad_maximum_fusion.3), channel_id=1, source_target_pairs={{0,8},{8,0},{1,9},{9,1},{2,10},{10,2},{3,11},{11,3},{4,12},{12,4},... | collective-permute-start | bytes 835592 | tf_op jit(solution)/shard_map/ppermute | solution.py:19
  72.2 0.7 copy-start.1
  73.0 1.0 slice-start
  83.0 0.7 copy-start.3
where the time goes:
time: 119 us; the launch traced here: 118 us
  local copies, waits for them, and re-layouts  40.6 us (34%)
  waiting for transfers between devices  35.8 us (30%)
  loops' own time  16.9 us (14%)
  other arithmetic  14.1 us (12%)
  starting transfers between devices  7.92 us (7%)
  between operations  2.95 us (2%)
    ppermute x4, waiting for transfers between devices, swapped(): return lax.ppermute(block, axis, route)  35.8 us
    another operation x1, loops' own time, boxcar_peaks(): return lax.map(single, box_widths)  16.9 us
    dynamic_update_slice x8, local copies, waits for them, and re-layouts, boxcar_peaks(): return lax.map(single, box_widths)  10.4 us
    ppermute x4, starting transfers between devices, swapped(): return lax.ppermute(block, axis, route)  7.92 us
    dynamic_slice x8, local copies, waits for them, and re-layouts, boxcar_peaks(): return lax.map(single, box_widths)  5.3 us
    another operation x4, other arithmetic  4.95 us
    slice x20, local copies, waits for them, and re-layouts, advance(): skewed[..., 1:]  3.63 us
    reshape x20, local copies, waits for them, and re-layouts, advance(): skewed = flat.reshape(leading + (count, width + 2))[..., :length]  3.42 us
  transfers between devices with their start and end apart: 4, of which 4 were waited for; matrix products, arithmetic and copies ran while one was open for 0% of the time, Pallas kernels for 0%

commit v1 on v0

v1 whole, which is shorter than its diff:
```python
import functools

import jax
import jax.numpy as jnp
from jax import lax
from jax.experimental import pallas as pl
from jax.experimental.pallas import tpu as pltpu
from jax.sharding import PartitionSpec as P

ROWS = 16
LANES = 128
PAD = 8

epsilon = 1e-05


def reverse4(value):
    return (value & 1) << 3 | (value & 2) << 1 | (value & 4) >> 1 | (value & 8) >> 3


def lane_index(blocks):
    return lax.broadcasted_iota(jnp.int32, (blocks, LANES), 1)


def later(ref, row, blocks, lane, whole, part):
    here = ref[row, pl.ds(whole, blocks), :]
    beyond = ref[row, pl.ds(whole + 1, blocks), :]
    return pltpu.roll(jnp.where(lane >= part, here, beyond), (LANES - part) % LANES, axis=1)


def clear_tail(ref, count, blocks):
    for row in range(count):
        ref[row, pl.ds(blocks, PAD), :] = jnp.zeros((PAD, LANES), jnp.float32)


def tree_section(source, target, blocks, lane, subbands, trials_in, trials_out, shift_of):
    for trial in range(trials_out):
        shift = shift_of(trial)
        whole, part = shift // LANES, shift % LANES
        old = trial * trials_in // trials_out
        for band in range(subbands // 2):
            low = source[2 * band * trials_in + old, pl.ds(0, blocks), :]
            high = later(source, (2 * band + 1) * trials_in + old, blocks, lane, whole, part)
            target[band * trials_out + trial, pl.ds(0, blocks), :] = low + high


def local_kernel(me_ref, table_ref, x_ref, keep_ref, send_ref, normal, first, second):
    channels, length = x_ref.shape
    blocks = length // LANES
    stride = blocks + PAD
    lane = lane_index(blocks)
    flat = normal.reshape(channels * stride, LANES)
    for group in range(channels // 16):
        rows = pl.ds(16 * group, 16)

        def piece(block):
            return x_ref[rows, pl.ds(block * LANES, LANES)].astype(jnp.float32)

        total = piece(0)
        for block in range(1, blocks):
            total = total + piece(block)
        centre = jnp.sum(total, axis=1, keepdims=True) / length
        centre = jnp.broadcast_to(centre, (16, LANES))
        total = jnp.square(piece(0) - centre)
        for block in range(1, blocks):
            total = total + jnp.square(piece(block) - centre)
        spread = jnp.sum(total, axis=1, keepdims=True) / length
        gain = jnp.broadcast_to(lax.rsqrt(spread + epsilon), (16, LANES))
        for block in range(blocks):
            value = (piece(block) - centre) * gain
            for half in range(2):
                start = (16 * group + 8 * half) * stride + block
                flat[pl.ds(start, 8, stride=stride), :] = value[8 * half : 8 * half + 8]
    clear_tail(normal, channels, blocks)
    clear_tail(first, channels // 2, blocks)
    clear_tail(second, channels // 4, blocks)

    partial = normal[0, pl.ds(0, blocks), :]
    for channel in range(1, channels):
        partial = partial + normal[channel, pl.ds(0, blocks), :]
    send_ref[8] = partial

    bands, trials = channels, 1
    source = normal
    buffers = (first, second)
    step = 0
    while bands > 2:
        fresh = max(1, 2 * channels // bands * ROWS // channels)
        target = buffers[step % 2]
        tree_section(
            source, target, blocks, lane, bands, trials, fresh, lambda trial: table_ref[fresh - 1 + trial]
        )
        source = target
        bands, trials = bands // 2, fresh
        step += 1
    mine = reverse4(me_ref[0] % 16)
    for trial in range(ROWS):
        shift = table_ref[ROWS - 1 + trial]
        old = trial * trials // ROWS
        high = later(source, trials + old, blocks, lane, shift // LANES, shift % LANES)
        value = source[old, pl.ds(0, blocks), :] + high
        place = mine ^ trial
        keep_ref[place] = value
    for place in range(8):
        send_ref[place] = keep_ref[8 + place]


def local_rows(filterbank, shift_table, me):
    channels, length = filterbank.shape
    blocks = length // LANES
    stride = blocks + PAD
    smem = pl.BlockSpec(memory_space=pltpu.SMEM)
    vmem = pl.BlockSpec(memory_space=pltpu.VMEM)
    return pl.pallas_call(
        local_kernel,
        out_shape=(
            jax.ShapeDtypeStruct((ROWS, blocks, LANES), jnp.float32),
            jax.ShapeDtypeStruct((9, blocks, LANES), jnp.float32),
        ),
        in_specs=[smem, smem, vmem],
        out_specs=(vmem, vmem),
        scratch_shapes=[
            pltpu.VMEM((channels, stride, LANES), jnp.float32),
            pltpu.VMEM((channels // 2, stride, LANES), jnp.float32),
            pltpu.VMEM((channels // 4, stride, LANES), jnp.float32),
        ],
        compiler_params=pltpu.CompilerParams(vmem_limit_bytes=32 << 20),
        name="local_tree",
    )(me, shift_table, filterbank)


def mean_path(mean, table_ref, scratch, blocks, lane, channels, row):
    clear_tail(scratch, 2, blocks)
    bands = channels
    value = mean
    step = 0
    while bands > 1:
        bands //= 2
        trials = max(1, channels // bands * ROWS // channels)
        shift = table_ref[trials - 1 + row * trials // ROWS]
        scratch[step % 2, pl.ds(0, blocks), :] = value
        value = value + later(scratch, step % 2, blocks, lane, shift // LANES, shift % LANES)
        step += 1
    return value


def cross_tree(me, table_ref, first, second, blocks, lane):
    row = reverse4(me % 16)
    bands, trials = ROWS, 1
    source, target = first, second
    while bands > 1:
        fresh = 2 * trials
        base = ROWS * fresh - 1 + row * fresh
        tree_section(
            source, target, blocks, lane, bands, trials, fresh, lambda trial: table_ref[base + trial]
        )
        source, target = target, source
        bands, trials = bands // 2, fresh
    return source


def split_bf16(value):
    high = value.astype(jnp.bfloat16)
    rest = value - high.astype(jnp.float32)
    middle = rest.astype(jnp.bfloat16)
    low = (rest - middle.astype(jnp.float32)).astype(jnp.bfloat16)
    return high, middle, low


def finish(rows, width_ref, out_ref, peaks_ref, prefix, blocks):
    length = blocks * LANES
    stride = blocks + PAD
    lane = lane_index(blocks)
    upper = lax.broadcasted_iota(jnp.int32, (LANES, LANES), 0)
    right = lax.broadcasted_iota(jnp.int32, (LANES, LANES), 1)
    running = jnp.where(upper <= right, 1.0, 0.0).astype(jnp.bfloat16)
    ones = jnp.ones((LANES, LANES), jnp.bfloat16)
    row_i = lax.broadcasted_iota(jnp.int32, (blocks, blocks), 0)
    row_j = lax.broadcasted_iota(jnp.int32, (blocks, blocks), 1)
    before = jnp.where(row_j < row_i, 1.0, 0.0).astype(jnp.bfloat16)

    def dots(left, right_side):
        return jnp.dot(left, right_side, preferred_element_type=jnp.float32)

    for trial in range(ROWS):
        value = rows[trial, pl.ds(0, blocks), :]
        centre = jnp.sum(value, axis=(0, 1), keepdims=True) / length
        value = value - centre
        spread = jnp.sum(jnp.square(value), axis=(0, 1), keepdims=True) / length
        value = value * lax.rsqrt(spread + epsilon)
        rows[trial, pl.ds(0, blocks), :] = value
        parts = split_bf16(value)
        within = sum(dots(part, running) for part in parts)
        totals = split_bf16(sum(dots(part, ones) for part in parts))
        offset = sum(dots(before, part) for part in totals)
        prefix[trial, pl.ds(PAD, blocks), :] = within + offset
        prefix[trial, pl.ds(0, PAD), :] = jnp.zeros((PAD, LANES), jnp.float32)
    flat = rows.reshape(ROWS * stride, LANES)
    for block in range(blocks):
        top = flat[pl.ds(block, 8, stride=stride), :]
        bottom = flat[pl.ds(block + 8 * stride, 8, stride=stride), :]
        both = jnp.concatenate([top, bottom], axis=0)
        out_ref[:, pl.ds(block * LANES, LANES)] = both.astype(jnp.bfloat16)
    widths = peaks_ref.shape[0]
    for index in range(widths):
        width = width_ref[index]
        back = PAD * LANES - width
        whole, part = back // LANES, back % LANES
        best = []
        for trial in range(ROWS):
            here = prefix[trial, pl.ds(whole, blocks), :]
            beyond = prefix[trial, pl.ds(whole + 1, blocks), :]
            earlier = pltpu.roll(jnp.where(lane >= part, here, beyond), (LANES - part) % LANES, axis=1)
            gap = prefix[trial, pl.ds(PAD, blocks), :] - earlier
            best.append(jnp.max(gap, axis=0, keepdims=True))
        best = jnp.max(jnp.concatenate(best, axis=0), axis=1, keepdims=True)
        scale = lax.rsqrt(jnp.full((ROWS, 1), width, jnp.int32).astype(jnp.float32))
        peaks_ref[index : index + 1, :] = jnp.transpose(best * scale)


def cross_kernel(
    channels, count, finishing, me_ref, table_ref, width_ref,
    keep_ref, core_ref, x_ref, z1_ref, z2_ref, z3_ref, mean_ref,
    *rest,
):
    blocks = keep_ref.shape[1]
    lane = lane_index(blocks)
    if finishing:
        out_ref, peaks_ref, first, second, prefix = rest
    else:
        series_ref, first, second, prefix = rest
    me = me_ref[0]
    here = me % 16
    mean = mean_ref[0]
    if finishing:
        mean = mean + z1_ref[4] + z2_ref[4] + z3_ref[4]
    mean = mean / (channels * count)
    dropped = mean_path(mean, table_ref, prefix, blocks, lane, channels, reverse4(here))
    clear_tail(first, ROWS, blocks)
    clear_tail(second, ROWS, blocks)

    def place(offset, value):
        first[here ^ offset, pl.ds(0, blocks), :] = value - dropped

    place(0, keep_ref[0])
    place(1, core_ref[0])
    place(2, x_ref[0])
    place(3, x_ref[4])
    for step, ref in ((1, z1_ref), (2, z2_ref), (3, z3_ref)):
        for inner in range(4):
            place(4 * step + inner, ref[inner])
    rows = cross_tree(me, table_ref, first, second, blocks, lane)
    if finishing:
        finish(rows, width_ref, out_ref, peaks_ref, prefix, blocks)
    else:
        for trial in range(ROWS):
            series_ref[trial] = rows[trial, pl.ds(0, blocks), :]


def finish_kernel(width_ref, series_ref, out_ref, peaks_ref, rows, prefix):
    blocks = series_ref.shape[1]
    for trial in range(ROWS):
        rows[trial, pl.ds(0, blocks), :] = series_ref[trial]
    finish(rows, width_ref, out_ref, peaks_ref, prefix, blocks)


def row_scratch(blocks):
    return pltpu.VMEM((ROWS, blocks + PAD, LANES), jnp.float32)


def final_shapes(blocks, widths):
    return (
        jax.ShapeDtypeStruct((ROWS, blocks * LANES), jnp.bfloat16),
        jax.ShapeDtypeStruct((widths, ROWS), jnp.float32),
    )


def swapped(block, distance):
    count = lax.axis_size("chan")
    return lax.ppermute(block, "chan", [(device, device ^ distance) for device in range(count)])


def advance(rows_in, shifts, start):
    count, length = rows_in.shape
    padded = jnp.concatenate([rows_in, jnp.zeros_like(rows_in)], axis=1)
    moved = lax.dynamic_slice_in_dim(padded, jnp.minimum(2 * start, length), length, 1)
    moved = jnp.concatenate([moved, jnp.zeros((count, 2 * count), moved.dtype)], axis=1)
    width = length + 2 * count
    flat = jnp.concatenate([moved.reshape(-1), jnp.zeros((2 * count,), moved.dtype)])
    skewed = flat.reshape(count, width + 2)[:, :length]
    odd = jnp.concatenate([skewed[:, 1:], jnp.zeros((count, 1), moved.dtype)], axis=1)
    parity = shifts - 2 * (start + jnp.arange(count, dtype=jnp.int32))
    return jnp.where((parity == 1)[:, None], odd, skewed)


def wider_sections(current, shift_table, me, section_count):
    half = ROWS // 2
    position = reverse4(me % 16)
    for bit in range(4, section_count):
        side = me >> bit & 1
        trials_now = 2 * ROWS << bit
        theirs = lax.dynamic_slice_in_dim(current, (1 - side) * half, half, 0)
        ours = lax.dynamic_slice_in_dim(current, side * half, half, 0)
        arrived = swapped(theirs, 1 << bit)
        lower = jnp.where(side == 0, ours, arrived)
        upper = jnp.where(side == 0, arrived, ours)
        first_trial = 2 * (position * ROWS + side * half)
        shifts = lax.dynamic_slice_in_dim(shift_table, trials_now - 1 + first_trial, ROWS)
        current = jnp.repeat(lower, 2, axis=0) + advance(jnp.repeat(upper, 2, axis=0), shifts, first_trial)
        position = 2 * position + side
    return current


def shards(filterbank, shift_table, box_widths):
    channels, length = filterbank.shape
    blocks = length // LANES
    widths = box_widths.shape[0]
    count = lax.axis_size("chan")
    section_count = count.bit_length() - 1
    me = lax.axis_index("chan")
    me_array = jnp.reshape(me, (1,)).astype(jnp.int32)
    keep, send = local_rows(filterbank, shift_table, me_array)
    small = section_count == 4

    core = swapped(send, 1)
    mean = send[8:] + core[8:]
    across = swapped(jnp.concatenate([keep[4:8], core[4:8], mean], axis=0), 2)
    mean = mean + across[8:]
    arrived = []
    for step in (1, 2, 3):
        low = (0, 2, 1, 3)[step]
        parts = [rows[low : low + 1] for rows in (keep, core, across, across[4:8])]
        if small:
            parts.append(mean)
        arrived.append(swapped(jnp.concatenate(parts, axis=0), 4 * step))
    if not small:
        mean = lax.psum(send[8:], "chan")

    smem = pl.BlockSpec(memory_space=pltpu.SMEM)
    vmem = pl.BlockSpec(memory_space=pltpu.VMEM)
    params = pltpu.CompilerParams(vmem_limit_bytes=32 << 20)
    call = pl.pallas_call(
        functools.partial(cross_kernel, channels, count, small),
        out_shape=final_shapes(blocks, widths)
        if small
        else jax.ShapeDtypeStruct((ROWS, blocks, LANES), jnp.float32),
        in_specs=[smem] * 3 + [vmem] * 7,
        out_specs=(vmem, vmem) if small else vmem,
        scratch_shapes=[row_scratch(blocks)] * 3,
        compiler_params=params,
        name="cross_tree",
    )
    result = call(me_array, shift_table, box_widths, keep, core, across, *arrived, mean)
    if small:
        return tuple(result)
    current = wider_sections(result.reshape(ROWS, length), shift_table, me, section_count)
    return tuple(
        pl.pallas_call(
            finish_kernel,
            out_shape=final_shapes(blocks, widths),
            in_specs=[smem, vmem],
            out_specs=(vmem, vmem),
            scratch_shapes=[row_scratch(blocks)] * 2,
            compiler_params=params,
            name="finish",
        )(box_widths, current.reshape(ROWS, blocks, LANES))
    )


def solution(mesh):
    placed = (P(("beam", "chan"), None), P(), P())
    return jax.shard_map(
        shards,
        mesh=mesh,
        in_specs=placed,
        out_specs=(P(("beam", "chan"), None), P("beam", "chan")),
        check_vma=False,
    )
```

time: 119 us -> 30.7 us (0.26)
  local copies, waits for them, and re-layouts: 40.6 us -> 1.75 us
  waiting for transfers between devices: 35.8 us -> 11.5 us
  loops' own time: 16.9 us -> 0 us
  other arithmetic: 14.1 us -> 0.03 us
  Pallas kernels: 0 us -> 8.66 us
  between operations: 2.95 us -> 0.69 us
    ppermute x4 -> x5, waiting for transfers between devices: 35.8 us -> 11.5 us  [swapped(): lax.ppermute(block, 'chan', [(device, device ^ distance) for device in ra...]
    another operation x1 -> x0, loops' own time: 16.9 us -> none  [boxcar_peaks(): return lax.map(single, box_widths)]
    dynamic_update_slice x8 -> x0, local copies, waits for them, and re-layouts: 10.4 us -> none  [boxcar_peaks(): return lax.map(single, box_widths)]
    reshape x58 -> x0, local copies, waits for them, and re-layouts: 9.94 us -> none  [the longest x20 3.42 us: advance(): skewed = flat.reshape(leading + (count, width + 2))[..., :length]]
    pallas_call x0 -> x2, Pallas kernels: none -> 8.66 us  [the longest x1 6.7 us: shards(): call(me_array, shift_table, box_widths, keep, core, across, *arrived, mean)]
    slice x34 -> x2, local copies, waits for them, and re-layouts: 6.81 us -> 0.01 us  [shards(): across = swapped(jnp.concatenate([keep[4:8], core[4:8], mean], axis=0), 2)]
    dynamic_slice x20 -> x0, local copies, waits for them, and re-layouts: 6.69 us -> none  [the longest x8 5.3 us: boxcar_peaks(): return lax.map(single, box_widths)]
    another operation x4 -> x0, other arithmetic: 4.95 us -> none
  transfers between devices with their start and end apart: 4 -> 5, of which waited for: 4 -> 4; matrix products, arithmetic and copies ran while one was open for 0% -> 0% of each run, Pallas kernels for 0% -> 0%
where the time goes in v1:
time: 30.7 us; the launch traced here: 30.5 us
  waiting for transfers between devices  11.5 us (37%)
  Pallas kernels  8.66 us (28%)
  starting transfers between devices  7.92 us (26%)
  local copies, waits for them, and re-layouts  1.75 us (6%)
  between operations  0.69 us (2%)
    ppermute x5, waiting for transfers between devices, swapped(): lax.ppermute(block, 'chan', [(device, device ^ distance) for device in ra...  11.5 us
    ppermute x5, starting transfers between devices, swapped(): lax.ppermute(block, 'chan', [(device, device ^ distance) for device in ra...  7.92 us
    pallas_call x1, Pallas kernels, shards(): call(me_array, shift_table, box_widths, keep, core, across, *arrived, mean)  6.7 us
    pallas_call x1, Pallas kernels, local_rows(): pl.pallas_call(local_kernel, out_shape=(jax.ShapeDtypeStruct((ROWS, block...  1.96 us
    unnamed x9, local copies, waits for them, and re-layouts  1.73 us
  transfers between devices with their start and end apart: 5, of which 4 were waited for; matrix products, arithmetic and copies ran while one was open for 0% of the time, Pallas kernels for 0%

profile of v1, /device:TPU:0, one launch (start us, length us, event | category | flops | bytes accessed | tf_op | source)
XLA Modules:
  0.0 30.5 jit_solution(6900758279048863063)
XLA Ops:
  0.6 0.0 copy-start.1
  0.6 0.7 %copy-done.1 = s32[511]{0:T(512)S(1)} copy-done((s32[511]{0:T(512)S(1)}, s32[511]{0:T(512)}, u32[]{:S(2)}) %copy-start.1) | copy-done | bytes 2068
  1.3 0.0 copy-start
  1.3 1.0 %copy-done = bf16[64,4096]{1,0:T(8,128)(2,1)S(1)} copy-done((bf16[64,4096]{1,0:T(8,128)(2,1)S(1)}, bf16[64,4096]{1,0:T(8,128)(2,1)}, u32[]{:S(2)}) %copy-start) | copy-done | bytes 524312
  2.4 2.0 %local_tree.1 = (f32[16,32,128]{2,1,0:T(8,128)S(1)}, f32[9,32,128]{2,1,0:T(8,128)S(1)}) custom-call(s32[1]{0:T(128)} %bitcast.me_ref, s32[511]{0:T(512)S(1)} %copy-done.1, bf16[64,4096]{1,0:T(8,128)(2,1)S(1)} %copy-done), custom_call_target="tpu_custom_call" | custom-call | tf_op jit(solution)/shard_map/local_tree/pallas_call | solution.py:114
  4.3 0.5 %collective-permute-start = (f32[9,32,128]{2,1,0:T(8,128)S(1)}, f32[9,32,128]{2,1,0:T(8,128)S(1)}, u32[]{:S(2)}, u32[]{:S(2)}) collective-permute-start(f32[9,32,128]{2,1,0:T(8,128)S(1)} %get-tuple-element.5), channel_id=1, source_target_pairs={{0,1},{1,0},{2,3},{3,2},{4,5},{5,4},{6,7},{7,6},{8,9},{9,8},{10,11... | collective-permute-start | bytes 442376 | tf_op jit(solution)/shard_map/ppermute | solution.py:280
  4.9 1.0 %collective-permute-done.core_ref = f32[9,32,128]{2,1,0:T(8,128)S(1)} collective-permute-done((f32[9,32,128]{2,1,0:T(8,128)S(1)}, f32[9,32,128]{2,1,0:T(8,128)S(1)}, u32[]{:S(2)}, u32[]{:S(2)}) %collective-permute-start) | collective-permute-done | bytes 147488 | tf_op jit(solution)/shard_map/ppermute | solution.py:280
  5.9 2.9 %collective-permute-start.1 = (f32[9,32,128]{2,1,0:T(8,128)S(1)}, f32[9,32,128]{2,1,0:T(8,128)S(1)}, u32[]{:S(2)}, u32[]{:S(2)}) collective-permute-start(f32[9,32,128]{2,1,0:T(8,128)S(1)} %pad_maximum_fusion), channel_id=1, source_target_pairs={{0,2},{1,3},{2,0},{3,1},{4,6},{5,7},{6,4},{7,5},{8,10},{9,11},{10,... | collective-permute-start | bytes 442376 | tf_op jit(solution)/shard_map/ppermute | solution.py:280
  8.8 4.2 %collective-permute-done.1.x_ref = f32[9,32,128]{2,1,0:T(8,128)S(1)} collective-permute-done((f32[9,32,128]{2,1,0:T(8,128)S(1)}, f32[9,32,128]{2,1,0:T(8,128)S(1)}, u32[]{:S(2)}, u32[]{:S(2)}) %collective-permute-start.1) | collective-permute-done | bytes 147488 | tf_op jit(solution)/shard_map/ppermute | solution.py:280
  13.0 1.9 %collective-permute-start.2 = (f32[5,32,128]{2,1,0:T(8,128)S(1)}, f32[5,32,128]{2,1,0:T(8,128)S(1)}, u32[]{:S(2)}, u32[]{:S(2)}) collective-permute-start(f32[5,32,128]{2,1,0:T(8,128)S(1)} %get-tuple-element.22), channel_id=1, source_target_pairs={{0,4},{1,5},{2,6},{3,7},{4,0},{5,1},{6,2},{7,3},{8,12},{9,13},{10,... | collective-permute-start | bytes 245768 | tf_op jit(solution)/shard_map/ppermute | solution.py:280
  14.9 0.0 copy-start.2
  14.9 2.6 %collective-permute-start.3 = (f32[5,32,128]{2,1,0:T(8,128)S(1)}, f32[5,32,128]{2,1,0:T(8,128)S(1)}, u32[]{:S(2)}, u32[]{:S(2)}) collective-permute-start(f32[5,32,128]{2,1,0:T(8,128)S(1)} %get-tuple-element.21), channel_id=1, source_target_pairs={{0,8},{1,9},{2,10},{3,11},{4,12},{5,13},{6,14},{7,15},{8,0},{9,1},... | collective-permute-start | bytes 245768 | tf_op jit(solution)/shard_map/ppermute | solution.py:280
  17.5 0.0 collective-permute-start.4
  17.5 0.0 collective-permute-done.2.z1_ref
  17.5 5.2 %collective-permute-done.3.z2_ref = f32[5,32,128]{2,1,0:T(8,128)S(1)} collective-permute-done((f32[5,32,128]{2,1,0:T(8,128)S(1)}, f32[5,32,128]{2,1,0:T(8,128)S(1)}, u32[]{:S(2)}, u32[]{:S(2)}) %collective-permute-start.3) | collective-permute-done | bytes 81952 | tf_op jit(solution)/shard_map/ppermute | solution.py:280
  22.7 1.1 %collective-permute-done.4.z3_ref = f32[5,32,128]{2,1,0:T(8,128)S(1)} collective-permute-done((f32[5,32,128]{2,1,0:T(8,128)S(1)}, f32[5,32,128]{2,1,0:T(8,128)S(1)}, u32[]{:S(2)}, u32[]{:S(2)}) %collective-permute-start.4) | collective-permute-done | bytes 81952 | tf_op jit(solution)/shard_map/ppermute | solution.py:280
  23.8 0.0 copy-done.2
  23.8 6.7 %cross_tree.1 = (bf16[16,4096]{1,0:T(8,128)(2,1)}, f32[8,16]{1,0:T(8,128)}) custom-call(s32[1]{0:T(128)} %bitcast.me_ref, s32[511]{0:T(512)S(1)} %copy-done.1, s32[8]{0:T(128)S(1)} %copy-done.2, f32[16,32,128]{2,1,0:T(8,128)S(1)} %get-tuple-element.4.keep_ref, f32[9,32,128]{2,1,0:T(8,128)S(1)} %collective-permute-done.core_ref, ...), custom_call_target="tpu_custom_call" | custom-call | tf_op jit(solution)/shard_map/cross_tree/pallas_call | solution.py:353
  (9 shorter events, 0.1 us)
Async XLA Ops:
  0.6 0.7 %copy-start.1 = (s32[511]{0:T(512)S(1)}, s32[511]{0:T(512)}, u32[]{:S(2)}) copy-start(s32[511]{0:T(512)} %table_ref.3) | copy-start | bytes 6136
  1.3 1.0 %copy-start = (bf16[64,4096]{1,0:T(8,128)(2,1)S(1)}, bf16[64,4096]{1,0:T(8,128)(2,1)}, u32[]{:S(2)}) copy-start(bf16[64,4096]{1,0:T(8,128)(2,1)} %x_ref.1) | copy-start | bytes 1572868
  4.3 1.5 %collective-permute-start = (f32[9,32,128]{2,1,0:T(8,128)S(1)}, f32[9,32,128]{2,1,0:T(8,128)S(1)}, u32[]{:S(2)}, u32[]{:S(2)}) collective-permute-start(f32[9,32,128]{2,1,0:T(8,128)S(1)} %get-tuple-element.5), channel_id=1, source_target_pairs={{0,1},{1,0},{2,3},{3,2},{4,5},{5,4},{6,7},{7,6},{8,9},{9,8},{10,11... | collective-permute-start | bytes 442376 | tf_op jit(solution)/shard_map/ppermute | solution.py:280
  5.9 7.1 %collective-permute-start.1 = (f32[9,32,128]{2,1,0:T(8,128)S(1)}, f32[9,32,128]{2,1,0:T(8,128)S(1)}, u32[]{:S(2)}, u32[]{:S(2)}) collective-permute-start(f32[9,32,128]{2,1,0:T(8,128)S(1)} %pad_maximum_fusion), channel_id=1, source_target_pairs={{0,2},{1,3},{2,0},{3,1},{4,6},{5,7},{6,4},{7,5},{8,10},{9,11},{10,... | collective-permute-start | bytes 442376 | tf_op jit(solution)/shard_map/ppermute | solution.py:280
  13.0 4.5 %collective-permute-start.2 = (f32[5,32,128]{2,1,0:T(8,128)S(1)}, f32[5,32,128]{2,1,0:T(8,128)S(1)}, u32[]{:S(2)}, u32[]{:S(2)}) collective-permute-start(f32[5,32,128]{2,1,0:T(8,128)S(1)} %get-tuple-element.22), channel_id=1, source_target_pairs={{0,4},{1,5},{2,6},{3,7},{4,0},{5,1},{6,2},{7,3},{8,12},{9,13},{10,... | collective-permute-start | bytes 245768 | tf_op jit(solution)/shard_map/ppermute | solution.py:280
  14.9 8.9 %copy-start.2 = (s32[8]{0:T(128)S(1)}, s32[8]{0:T(128)}, u32[]{:S(2)}) copy-start(s32[8]{0:T(128)} %width_ref.1) | copy-start | bytes 100
  14.9 7.8 %collective-permute-start.3 = (f32[5,32,128]{2,1,0:T(8,128)S(1)}, f32[5,32,128]{2,1,0:T(8,128)S(1)}, u32[]{:S(2)}, u32[]{:S(2)}) collective-permute-start(f32[5,32,128]{2,1,0:T(8,128)S(1)} %get-tuple-element.21), channel_id=1, source_target_pairs={{0,8},{1,9},{2,10},{3,11},{4,12},{5,13},{6,14},{7,15},{8,0},{9,1},... | collective-permute-start | bytes 245768 | tf_op jit(solution)/shard_map/ppermute | solution.py:280
  17.5 6.3 %collective-permute-start.4 = (f32[5,32,128]{2,1,0:T(8,128)S(1)}, f32[5,32,128]{2,1,0:T(8,128)S(1)}, u32[]{:S(2)}, u32[]{:S(2)}) collective-permute-start(f32[5,32,128]{2,1,0:T(8,128)S(1)} %get-tuple-element.6), channel_id=1, source_target_pairs={{0,12},{1,13},{2,14},{3,15},{4,8},{5,9},{6,10},{7,11},{8,4},{9,5},... | collective-permute-start | bytes 245768 | tf_op jit(solution)/shard_map/ppermute | solution.py:280

commit v2 on v1

v2 whole, which is shorter than its diff:
```python
import functools

import jax
import jax.numpy as jnp
from jax import lax
from jax.experimental import pallas as pl
from jax.experimental.pallas import tpu as pltpu
from jax.sharding import PartitionSpec as P

ROWS = 16
LANES = 128
PAD = 8

epsilon = 1e-05


def reverse4(value):
    return (value & 1) << 3 | (value & 2) << 1 | (value & 4) >> 1 | (value & 8) >> 3


def lane_index(blocks):
    return lax.broadcasted_iota(jnp.int32, (blocks, LANES), 1)


def later(ref, row, blocks, lane, shift):
    whole, part = shift >> 7, shift & 127
    here = ref[row, pl.ds(whole, blocks), :]
    beyond = ref[row, pl.ds(whole + 1, blocks), :]
    return pltpu.roll(jnp.where(lane >= part, here, beyond), (LANES - part) & 127, axis=1)


def clear_tail(ref, count, blocks):
    for row in range(count):
        ref[row, pl.ds(blocks, PAD), :] = jnp.zeros((PAD, LANES), jnp.float32)


def tree_section(source, target, blocks, lane, subbands, trials_in, trials_out, shift_of, taken=None):
    for trial in range(trials_out):
        shift = shift_of(trial)
        old = trial * trials_in // trials_out
        for band in range(subbands // 2):
            low = source[2 * band * trials_in + old, pl.ds(0, blocks), :]
            high = later(source, (2 * band + 1) * trials_in + old, blocks, lane, shift)
            value = low + high
            if taken is not None:
                value = value - taken[trial]
            target[band * trials_out + trial, pl.ds(0, blocks), :] = value


def local_kernel(table_hbm, x_hbm, rows_ref, table_ref, x_ref, normal, first, second, table_sem, x_sem):
    channels, length = x_ref.shape
    blocks = length // LANES
    stride = blocks + PAD
    groups = channels // 16
    table_copy = pltpu.make_async_copy(table_hbm, table_ref, table_sem)
    copies = [
        pltpu.make_async_copy(x_hbm.at[pl.ds(16 * group, 16)], x_ref.at[pl.ds(16 * group, 16)], x_sem.at[group])
        for group in range(groups)
    ]
    for copy in copies:
        copy.start()
    table_copy.start()
    lane = lane_index(blocks)
    flat = normal.reshape(channels * stride, LANES)
    clear_tail(normal, channels, blocks)
    clear_tail(first, channels // 2, blocks)
    clear_tail(second, channels // 4, blocks)
    for group in range(groups):
        rows = pl.ds(16 * group, 16)

        def piece(block):
            return x_ref[rows, pl.ds(block * LANES, LANES)].astype(jnp.float32)

        copies[group].wait()
        total = piece(0)
        for block in range(1, blocks):
            total = total + piece(block)
        centre = jnp.sum(total, axis=1, keepdims=True) / length
        centre = jnp.broadcast_to(centre, (16, LANES))
        total = jnp.square(piece(0) - centre)
        for block in range(1, blocks):
            total = total + jnp.square(piece(block) - centre)
        spread = jnp.sum(total, axis=1, keepdims=True) / length
        gain = jnp.broadcast_to(lax.rsqrt(spread + epsilon), (16, LANES))
        for block in range(blocks):
            value = (piece(block) - centre) * gain
            for half in range(2):
                start = (16 * group + 8 * half) * stride + block
                flat[pl.ds(start, 8, stride=stride), :] = value[8 * half : 8 * half + 8]

    partial = normal[0, pl.ds(0, blocks), :]
    for channel in range(1, channels):
        partial = partial + normal[channel, pl.ds(0, blocks), :]
    rows_ref[ROWS] = partial
    table_copy.wait()

    bands, trials = channels, 1
    source = normal
    buffers = (first, second)
    step = 0
    while bands > 2:
        fresh = max(1, 2 * channels // bands * ROWS // channels)
        target = buffers[step % 2]
        tree_section(
            source, target, blocks, lane, bands, trials, fresh, lambda trial: table_ref[fresh - 1 + trial]
        )
        source = target
        bands, trials = bands // 2, fresh
        step += 1
    mine = reverse4(lax.axis_index("chan") & 15)
    for trial in range(ROWS):
        shift = table_ref[ROWS - 1 + trial]
        old = trial * trials // ROWS
        high = later(source, trials + old, blocks, lane, shift)
        rows_ref[mine ^ trial] = source[old, pl.ds(0, blocks), :] + high


def local_rows(filterbank, shift_table):
    channels, length = filterbank.shape
    blocks = length // LANES
    stride = blocks + PAD
    hbm = pl.BlockSpec(memory_space=pltpu.HBM)
    return pl.pallas_call(
        local_kernel,
        out_shape=jax.ShapeDtypeStruct((ROWS + 1, blocks, LANES), jnp.float32),
        in_specs=[hbm, hbm],
        out_specs=pl.BlockSpec(memory_space=pltpu.VMEM),
        scratch_shapes=[
            pltpu.SMEM(shift_table.shape, jnp.int32),
            pltpu.VMEM(filterbank.shape, filterbank.dtype),
            pltpu.VMEM((channels, stride, LANES), jnp.float32),
            pltpu.VMEM((channels // 2, stride, LANES), jnp.float32),
            pltpu.VMEM((channels // 4, stride, LANES), jnp.float32),
            pltpu.SemaphoreType.DMA,
            pltpu.SemaphoreType.DMA((channels // 16,)),
        ],
        compiler_params=pltpu.CompilerParams(vmem_limit_bytes=32 << 20),
        name="local_tree",
    )(shift_table, filterbank)


def mean_path(mean, table_ref, scratch, blocks, lane, channels, row):
    bands = channels
    value = mean
    step = 0
    while bands > 1:
        bands //= 2
        trials = max(1, channels // bands * ROWS // channels)
        shift = table_ref[trials - 1 + (row >> (ROWS // trials).bit_length() - 1)]
        scratch[step, pl.ds(0, blocks), :] = value
        value = value + later(scratch, step, blocks, lane, shift)
        step += 1
    return value


def cross_tree(me, mean, table_ref, first, second, spare, blocks, lane, channels):
    row = reverse4(me & 15)
    clear_tail(spare, ROWS, blocks)
    clear_tail(first, ROWS, blocks)
    clear_tail(second, ROWS, blocks)
    mean = mean_path(mean, table_ref, spare, blocks, lane, channels, row)
    spare[ROWS - 1, pl.ds(0, blocks), :] = mean
    bands, trials = ROWS, 1
    source, target = first, second
    while bands > 1:
        fresh = 2 * trials
        base = ROWS * fresh - 1 + row * fresh

        def shift_of(trial):
            return table_ref[base + trial]

        taken = None
        if bands == ROWS:
            taken = [mean + later(spare, ROWS - 1, blocks, lane, shift_of(trial)) for trial in range(fresh)]
        tree_section(source, target, blocks, lane, bands, trials, fresh, shift_of, taken)
        source, target = target, source
        bands, trials = bands // 2, fresh
    return source


def finish(rows, width_ref, out_ref, peaks_ref, prefix, split):
    stride = rows.shape[1]
    blocks = stride - PAD
    length = blocks * LANES
    lane = lax.broadcasted_iota(jnp.int32, (ROWS, LANES), 1)
    flat = rows.reshape(ROWS * stride, LANES)

    total = jnp.zeros((ROWS, LANES), jnp.float32)
    for block in range(blocks):
        value = jnp.concatenate(
            [flat[pl.ds(block + 8 * half * stride, 8, stride=stride), :] for half in range(2)], axis=0
        )
        prefix[2 + block] = value
        total = total + value
    centre = jnp.sum(total, axis=1, keepdims=True) / length
    centre = jnp.broadcast_to(centre, (ROWS, LANES))
    total = jnp.zeros((ROWS, LANES), jnp.float32)
    for block in range(blocks):
        total = total + jnp.square(prefix[2 + block] - centre)
    spread = jnp.sum(total, axis=1, keepdims=True) / length
    gain = jnp.broadcast_to(lax.rsqrt(spread + epsilon), (ROWS, LANES))
    for block in range(blocks):
        value = (prefix[2 + block] - centre) * gain
        rounded = value.astype(jnp.bfloat16)
        out_ref[:, pl.ds(block * LANES, LANES)] = rounded
        split[pl.ds(block * ROWS, ROWS), pl.ds(0, LANES)] = rounded
        rest = value - rounded.astype(jnp.float32)
        split[pl.ds(block * ROWS, ROWS), pl.ds(LANES, LANES)] = rest.astype(jnp.bfloat16)

    above = lax.broadcasted_iota(jnp.int32, (2 * LANES, 2 * LANES), 0) & 127
    across = lax.broadcasted_iota(jnp.int32, (2 * LANES, 2 * LANES), 1)
    weights = jnp.where(above <= across, 1.0, 0.0).astype(jnp.bfloat16)
    sums = jnp.dot(split[...], weights, preferred_element_type=jnp.float32)
    carry = jnp.zeros((ROWS, LANES), jnp.float32)
    prefix[0] = carry
    prefix[1] = carry
    for block in range(blocks):
        part = sums[block * ROWS : (block + 1) * ROWS]
        prefix[2 + block] = part[:, :LANES] + carry
        carry = carry + part[:, LANES:]

    widths = peaks_ref.shape[0]
    peaks = jnp.zeros((ROWS, LANES), jnp.float32)
    for index in range(widths):
        width = width_ref[index]
        back = 2 * LANES - width
        whole, part = back >> 7, back & 127
        turn = (LANES - part) & 127
        keep = lane < LANES - part
        best = None
        here = pltpu.roll(prefix[whole], turn, axis=1)
        for block in range(blocks):
            beyond = pltpu.roll(prefix[whole + block + 1], turn, axis=1)
            gap = prefix[2 + block] - jnp.where(keep, here, beyond)
            best = gap if best is None else jnp.maximum(best, gap)
            here = beyond
        best = jnp.max(best, axis=1, keepdims=True)
        scale = lax.rsqrt(jnp.full((ROWS, LANES), width, jnp.int32).astype(jnp.float32))
        peaks = jnp.where(lane == index, best * scale, peaks)
    peaks_ref[...] = jnp.transpose(peaks)[:widths]


def cross_kernel(
    channels, count, finishing, table_ref, width_ref,
    own_ref, core_ref, x_ref, z1_ref, z2_ref, z3_ref, mean_ref,
    *rest,
):
    blocks = own_ref.shape[1]
    lane = lane_index(blocks)
    if finishing:
        out_ref, peaks_ref, first, second, spare, prefix, split = rest
    else:
        series_ref, first, second, spare = rest
    me = lax.axis_index("chan")
    here = me & 15

    def place(offset, value):
        first[here ^ offset, pl.ds(0, blocks), :] = value

    place(0, own_ref[0])
    place(1, core_ref[0])
    place(2, x_ref[0])
    place(3, x_ref[4])
    for step, ref in ((1, z1_ref), (2, z2_ref), (3, z3_ref)):
        for inner in range(4):
            place(4 * step + inner, ref[inner])
    mean = mean_ref[0]
    if finishing:
        mean = mean + z1_ref[4] + z2_ref[4] + z3_ref[4]
    mean = mean / (channels * count)
    rows = cross_tree(me, mean, table_ref, first, second, spare, blocks, lane, channels)
    if finishing:
        finish(rows, width_ref, out_ref, peaks_ref, prefix, split)
    else:
        for trial in range(ROWS):
            series_ref[trial] = rows[trial, pl.ds(0, blocks), :]


def finish_kernel(width_ref, series_ref, out_ref, peaks_ref, rows, prefix, split):
    blocks = series_ref.shape[1]
    for trial in range(ROWS):
        rows[trial, pl.ds(0, blocks), :] = series_ref[trial]
    finish(rows, width_ref, out_ref, peaks_ref, prefix, split)


def row_scratch(blocks):
    return pltpu.VMEM((ROWS, blocks + PAD, LANES), jnp.float32)


def finish_scratch(blocks):
    return [
        pltpu.VMEM((blocks + 2, ROWS, LANES), jnp.float32),
        pltpu.VMEM((blocks * ROWS, 2 * LANES), jnp.bfloat16),
    ]


def final_shapes(blocks, widths):
    return (
        jax.ShapeDtypeStruct((ROWS, blocks * LANES), jnp.bfloat16),
        jax.ShapeDtypeStruct((widths, ROWS), jnp.float32),
    )


def swapped(block, distance):
    count = lax.axis_size("chan")
    return lax.ppermute(block, "chan", [(device, device ^ distance) for device in range(count)])


def advance(rows_in, shifts, start):
    count, length = rows_in.shape
    padded = jnp.concatenate([rows_in, jnp.zeros_like(rows_in)], axis=1)
    moved = lax.dynamic_slice_in_dim(padded, jnp.minimum(2 * start, length), length, 1)
    moved = jnp.concatenate([moved, jnp.zeros((count, 2 * count), moved.dtype)], axis=1)
    width = length + 2 * count
    flat = jnp.concatenate([moved.reshape(-1), jnp.zeros((2 * count,), moved.dtype)])
    skewed = flat.reshape(count, width + 2)[:, :length]
    odd = jnp.concatenate([skewed[:, 1:], jnp.zeros((count, 1), moved.dtype)], axis=1)
    parity = shifts - 2 * (start + jnp.arange(count, dtype=jnp.int32))
    return jnp.where((parity == 1)[:, None], odd, skewed)


def wider_sections(current, shift_table, me, section_count):
    half = ROWS // 2
    position = reverse4(me % 16)
    for bit in range(4, section_count):
        side = me >> bit & 1
        trials_now = 2 * ROWS << bit
        theirs = lax.dynamic_slice_in_dim(current, (1 - side) * half, half, 0)
        ours = lax.dynamic_slice_in_dim(current, side * half, half, 0)
        arrived = swapped(theirs, 1 << bit)
        lower = jnp.where(side == 0, ours, arrived)
        upper = jnp.where(side == 0, arrived, ours)
        first_trial = 2 * (position * ROWS + side * half)
        shifts = lax.dynamic_slice_in_dim(shift_table, trials_now - 1 + first_trial, ROWS)
        current = jnp.repeat(lower, 2, axis=0) + advance(jnp.repeat(upper, 2, axis=0), shifts, first_trial)
        position = 2 * position + side
    return current


def shards(filterbank, shift_table, box_widths):
    channels, length = filterbank.shape
    blocks = length // LANES
    widths = box_widths.shape[0]
    count = lax.axis_size("chan")
    section_count = count.bit_length() - 1
    rows = local_rows(filterbank, shift_table)
    small = section_count == 4

    core = swapped(rows[8:], 1)
    mean = rows[ROWS:] + core[8:]
    across = swapped(jnp.concatenate([rows[4:8], core[4:8], mean], axis=0), 2)
    mean = mean + across[8:]
    arrived = []
    for step in (1, 2, 3):
        low = (0, 2, 1, 3)[step]
        parts = [part[low : low + 1] for part in (rows, core, across, across[4:8])]
        if small:
            parts.append(mean)
        arrived.append(swapped(jnp.concatenate(parts, axis=0), 4 * step))
    if not small:
        mean = lax.psum(rows[ROWS:], "chan")

    smem = pl.BlockSpec(memory_space=pltpu.SMEM)
    vmem = pl.BlockSpec(memory_space=pltpu.VMEM)
    params = pltpu.CompilerParams(vmem_limit_bytes=32 << 20)
    call = pl.pallas_call(
        functools.partial(cross_kernel, channels, count, small),
        out_shape=final_shapes(blocks, widths)
        if small
        else jax.ShapeDtypeStruct((ROWS, blocks, LANES), jnp.float32),
        in_specs=[smem] * 2 + [vmem] * 7,
        out_specs=(vmem, vmem) if small else vmem,
        scratch_shapes=[row_scratch(blocks)] * 3 + (finish_scratch(blocks) if small else []),
        compiler_params=params,
        name="cross_tree",
    )
    result = call(shift_table, box_widths, rows, core, across, *arrived, mean)
    if small:
        return tuple(result)
    me = lax.axis_index("chan")
    current = wider_sections(result.reshape(ROWS, length), shift_table, me, section_count)
    return tuple(
        pl.pallas_call(
            finish_kernel,
            out_shape=final_shapes(blocks, widths),
            in_specs=[smem, vmem],
            out_specs=(vmem, vmem),
            scratch_shapes=[row_scratch(blocks)] + finish_scratch(blocks),
            compiler_params=params,
            name="finish",
        )(box_widths, current.reshape(ROWS, blocks, LANES))
    )


def solution(mesh):
    placed = (P(("beam", "chan"), None), P(), P())
    return jax.shard_map(
        shards,
        mesh=mesh,
        in_specs=placed,
        out_specs=(P(("beam", "chan"), None), P("beam", "chan")),
        check_vma=False,
    )
```

time: 30.7 us -> 28.1 us (0.915)
  Pallas kernels: 8.66 us -> 6.13 us
    pallas_call x2, Pallas kernels: 8.66 us -> 6.13 us  [the longest x1 3.43 us: shards(): result = call(shift_table, box_widths, rows, core, across, *arrived, mean)]
  transfers between devices with their start and end apart: 5 -> 5, of which waited for: 4 -> 5; matrix products, arithmetic and copies ran while one was open for 0% -> 0% of each run, Pallas kernels for 0% -> 0%
where the time goes in v2:
time: 28.1 us; the launch traced here: 27.9 us
  waiting for transfers between devices  11.4 us (41%)
  starting transfers between devices  7.92 us (28%)
  Pallas kernels  6.13 us (22%)
  local copies, waits for them, and re-layouts  1.76 us (6%)
  between operations  0.69 us (2%)
    ppermute x5, waiting for transfers between devices, swapped(): lax.ppermute(block, 'chan', [(device, device ^ distance) for device in ra...  11.4 us
    ppermute x5, starting transfers between devices, swapped(): lax.ppermute(block, 'chan', [(device, device ^ distance) for device in ra...  7.92 us
    pallas_call x1, Pallas kernels, shards(): result = call(shift_table, box_widths, rows, core, across, *arrived, mean)  3.43 us
    pallas_call x1, Pallas kernels, local_rows(): pl.pallas_call(local_kernel, out_shape=jax.ShapeDtypeStruct((ROWS + 1, bl...  2.7 us
    unnamed x9, local copies, waits for them, and re-layouts  1.73 us
  transfers between devices with their start and end apart: 5, of which 5 were waited for; matrix products, arithmetic and copies ran while one was open for 0% of the time, Pallas kernels for 0%

profile of v2, /device:TPU:0, one launch (start us, length us, event | category | flops | bytes accessed | tf_op | source)
XLA Modules:
  0.0 27.9 jit_solution(15061066386706819760)
XLA Ops:
  0.6 0.0 copy-start
  0.6 1.0 %copy-done = bf16[64,4096]{1,0:T(8,128)(2,1)S(1)} copy-done((bf16[64,4096]{1,0:T(8,128)(2,1)S(1)}, bf16[64,4096]{1,0:T(8,128)(2,1)}, u32[]{:S(2)}) %copy-start) | copy-done | bytes 524312
  1.7 0.0 copy-start.1
  1.7 0.7 %copy-done.1 = s32[511]{0:T(512)S(1)} copy-done((s32[511]{0:T(512)S(1)}, s32[511]{0:T(512)}, u32[]{:S(2)}) %copy-start.1) | copy-done | bytes 2068
  2.4 2.7 %local_tree.1.own_ref = f32[17,32,128]{2,1,0:T(8,128)S(1)} custom-call(s32[511]{0:T(512)S(1)} %copy-done.1, bf16[64,4096]{1,0:T(8,128)(2,1)S(1)} %copy-done), custom_call_target="tpu_custom_call" | custom-call | tf_op jit(solution)/shard_map/local_tree/pallas_call | solution.py:123
  5.1 0.5 %collective-permute-start = (f32[9,32,128]{2,1,0:T(8,128)S(1)}, f32[9,32,128]{2,1,0:T(8,128)S(1)}, u32[]{:S(2)}, u32[]{:S(2)}) collective-permute-start(f32[9,32,128]{2,1,0:T(8,128)S(1)} %slice.78), channel_id=1, source_target_pairs={{0,1},{1,0},{2,3},{3,2},{4,5},{5,4},{6,7},{7,6},{8,9},{9,8},{10,11... | collective-permute-start | bytes 442376 | tf_op jit(solution)/shard_map/ppermute | solution.py:306
  5.6 1.0 %collective-permute-done.core_ref = f32[9,32,128]{2,1,0:T(8,128)S(1)} collective-permute-done((f32[9,32,128]{2,1,0:T(8,128)S(1)}, f32[9,32,128]{2,1,0:T(8,128)S(1)}, u32[]{:S(2)}, u32[]{:S(2)}) %collective-permute-start) | collective-permute-done | bytes 147488 | tf_op jit(solution)/shard_map/ppermute | solution.py:306
  6.6 2.9 %collective-permute-start.1 = (f32[9,32,128]{2,1,0:T(8,128)S(1)}, f32[9,32,128]{2,1,0:T(8,128)S(1)}, u32[]{:S(2)}, u32[]{:S(2)}) collective-permute-start(f32[9,32,128]{2,1,0:T(8,128)S(1)} %pad_maximum_fusion), channel_id=1, source_target_pairs={{0,2},{1,3},{2,0},{3,1},{4,6},{5,7},{6,4},{7,5},{8,10},{9,11},{10,... | collective-permute-start | bytes 442376 | tf_op jit(solution)/shard_map/ppermute | solution.py:306
  9.6 4.2 %collective-permute-done.1.x_ref = f32[9,32,128]{2,1,0:T(8,128)S(1)} collective-permute-done((f32[9,32,128]{2,1,0:T(8,128)S(1)}, f32[9,32,128]{2,1,0:T(8,128)S(1)}, u32[]{:S(2)}, u32[]{:S(2)}) %collective-permute-start.1) | collective-permute-done | bytes 147488 | tf_op jit(solution)/shard_map/ppermute | solution.py:306
  13.8 2.9 %collective-permute-start.3 = (f32[5,32,128]{2,1,0:T(8,128)S(1)}, f32[5,32,128]{2,1,0:T(8,128)S(1)}, u32[]{:S(2)}, u32[]{:S(2)}) collective-permute-start(f32[5,32,128]{2,1,0:T(8,128)S(1)} %get-tuple-element.17), channel_id=1, source_target_pairs={{0,8},{1,9},{2,10},{3,11},{4,12},{5,13},{6,14},{7,15},{8,0},{9,1},... | collective-permute-start | bytes 245768 | tf_op jit(solution)/shard_map/ppermute | solution.py:306
  16.7 0.0 copy-start.2
  16.7 1.6 %collective-permute-start.2 = (f32[5,32,128]{2,1,0:T(8,128)S(1)}, f32[5,32,128]{2,1,0:T(8,128)S(1)}, u32[]{:S(2)}, u32[]{:S(2)}) collective-permute-start(f32[5,32,128]{2,1,0:T(8,128)S(1)} %get-tuple-element.18), channel_id=1, source_target_pairs={{0,4},{1,5},{2,6},{3,7},{4,0},{5,1},{6,2},{7,3},{8,12},{9,13},{10,... | collective-permute-start | bytes 245768 | tf_op jit(solution)/shard_map/ppermute | solution.py:306
  18.2 0.0 collective-permute-start.4
  18.2 2.4 %collective-permute-done.3.z2_ref = f32[5,32,128]{2,1,0:T(8,128)S(1)} collective-permute-done((f32[5,32,128]{2,1,0:T(8,128)S(1)}, f32[5,32,128]{2,1,0:T(8,128)S(1)}, u32[]{:S(2)}, u32[]{:S(2)}) %collective-permute-start.3) | collective-permute-done | bytes 81952 | tf_op jit(solution)/shard_map/ppermute | solution.py:306
  20.7 0.5 %collective-permute-done.2.z1_ref = f32[5,32,128]{2,1,0:T(8,128)S(1)} collective-permute-done((f32[5,32,128]{2,1,0:T(8,128)S(1)}, f32[5,32,128]{2,1,0:T(8,128)S(1)}, u32[]{:S(2)}, u32[]{:S(2)}) %collective-permute-start.2) | collective-permute-done | bytes 81952 | tf_op jit(solution)/shard_map/ppermute | solution.py:306
  21.1 3.3 %collective-permute-done.4.z3_ref = f32[5,32,128]{2,1,0:T(8,128)S(1)} collective-permute-done((f32[5,32,128]{2,1,0:T(8,128)S(1)}, f32[5,32,128]{2,1,0:T(8,128)S(1)}, u32[]{:S(2)}, u32[]{:S(2)}) %collective-permute-start.4) | collective-permute-done | bytes 81952 | tf_op jit(solution)/shard_map/ppermute | solution.py:306
  24.5 0.0 copy-done.2
  24.5 3.4 %cross_tree.1 = (bf16[16,4096]{1,0:T(8,128)(2,1)}, f32[8,16]{1,0:T(8,128)}) custom-call(s32[511]{0:T(512)S(1)} %copy-done.1, s32[8]{0:T(128)S(1)} %copy-done.2, f32[17,32,128]{2,1,0:T(8,128)S(1)} %local_tree.1.own_ref, f32[9,32,128]{2,1,0:T(8,128)S(1)} %collective-permute-done.core_ref, f32[9,32,128]{2,1,0:T(8,128)S(1)} %collective-permute-done.1.x_ref, ...), custom_call_target="tpu_custom_call" | custom-call | tf_op jit(solution)/shard_map/cross_tree/pallas_call | solution.py:377
  (10 shorter events, 0.1 us)
Async XLA Ops:
  0.6 1.0 %copy-start = (bf16[64,4096]{1,0:T(8,128)(2,1)S(1)}, bf16[64,4096]{1,0:T(8,128)(2,1)}, u32[]{:S(2)}) copy-start(bf16[64,4096]{1,0:T(8,128)(2,1)} %x_hbm.1) | copy-start | bytes 1572868
  1.7 0.7 %copy-start.1 = (s32[511]{0:T(512)S(1)}, s32[511]{0:T(512)}, u32[]{:S(2)}) copy-start(s32[511]{0:T(512)} %table_ref.1) | copy-start | bytes 6136
  5.1 1.5 %collective-permute-start = (f32[9,32,128]{2,1,0:T(8,128)S(1)}, f32[9,32,128]{2,1,0:T(8,128)S(1)}, u32[]{:S(2)}, u32[]{:S(2)}) collective-permute-start(f32[9,32,128]{2,1,0:T(8,128)S(1)} %slice.78), channel_id=1, source_target_pairs={{0,1},{1,0},{2,3},{3,2},{4,5},{5,4},{6,7},{7,6},{8,9},{9,8},{10,11... | collective-permute-start | bytes 442376 | tf_op jit(solution)/shard_map/ppermute | solution.py:306
  6.6 7.1 %collective-permute-start.1 = (f32[9,32,128]{2,1,0:T(8,128)S(1)}, f32[9,32,128]{2,1,0:T(8,128)S(1)}, u32[]{:S(2)}, u32[]{:S(2)}) collective-permute-start(f32[9,32,128]{2,1,0:T(8,128)S(1)} %pad_maximum_fusion), channel_id=1, source_target_pairs={{0,2},{1,3},{2,0},{3,1},{4,6},{5,7},{6,4},{7,5},{8,10},{9,11},{10,... | collective-permute-start | bytes 442376 | tf_op jit(solution)/shard_map/ppermute | solution.py:306
  13.8 6.9 %collective-permute-start.3 = (f32[5,32,128]{2,1,0:T(8,128)S(1)}, f32[5,32,128]{2,1,0:T(8,128)S(1)}, u32[]{:S(2)}, u32[]{:S(2)}) collective-permute-start(f32[5,32,128]{2,1,0:T(8,128)S(1)} %get-tuple-element.17), channel_id=1, source_target_pairs={{0,8},{1,9},{2,10},{3,11},{4,12},{5,13},{6,14},{7,15},{8,0},{9,1},... | collective-permute-start | bytes 245768 | tf_op jit(solution)/shard_map/ppermute | solution.py:306
  16.7 7.8 %copy-start.2 = (s32[8]{0:T(128)S(1)}, s32[8]{0:T(128)}, u32[]{:S(2)}) copy-start(s32[8]{0:T(128)} %width_ref.1) | copy-start | bytes 100
  16.7 4.5 %collective-permute-start.2 = (f32[5,32,128]{2,1,0:T(8,128)S(1)}, f32[5,32,128]{2,1,0:T(8,128)S(1)}, u32[]{:S(2)}, u32[]{:S(2)}) collective-permute-start(f32[5,32,128]{2,1,0:T(8,128)S(1)} %get-tuple-element.18), channel_id=1, source_target_pairs={{0,4},{1,5},{2,6},{3,7},{4,0},{5,1},{6,2},{7,3},{8,12},{9,13},{10,... | collective-permute-start | bytes 245768 | tf_op jit(solution)/shard_map/ppermute | solution.py:306
  18.2 6.2 %collective-permute-start.4 = (f32[5,32,128]{2,1,0:T(8,128)S(1)}, f32[5,32,128]{2,1,0:T(8,128)S(1)}, u32[]{:S(2)}, u32[]{:S(2)}) collective-permute-start(f32[5,32,128]{2,1,0:T(8,128)S(1)} %get-tuple-element.2), channel_id=1, source_target_pairs={{0,12},{1,13},{2,14},{3,15},{4,8},{5,9},{6,10},{7,11},{8,4},{9,5},... | collective-permute-start | bytes 245768 | tf_op jit(solution)/shard_map/ppermute | solution.py:306

commit v3 on v2

--- a/solution.py
+++ b/solution.py
@@ -91,7 +91,8 @@
     partial = normal[0, pl.ds(0, blocks), :]
     for channel in range(1, channels):
         partial = partial + normal[channel, pl.ds(0, blocks), :]
-    rows_ref[ROWS] = partial
+    for row in (3, 7, 11, 15, 20):
+        rows_ref[row] = partial
     table_copy.wait()
 
     bands, trials = channels, 1
@@ -112,7 +113,9 @@
         shift = table_ref[ROWS - 1 + trial]
         old = trial * trials // ROWS
         high = later(source, trials + old, blocks, lane, shift)
-        rows_ref[mine ^ trial] = source[old, pl.ds(0, blocks), :] + high
+        place = mine ^ trial
+        group, low = place >> 2, place & 3
+        rows_ref[jnp.where(low == 1, ROWS + group, place - (low > 0))] = source[old, pl.ds(0, blocks), :] + high
 
 
 def local_rows(filterbank, shift_table):
@@ -122,7 +125,7 @@
     hbm = pl.BlockSpec(memory_space=pltpu.HBM)
     return pl.pallas_call(
         local_kernel,
-        out_shape=jax.ShapeDtypeStruct((ROWS + 1, blocks, LANES), jnp.float32),
+        out_shape=jax.ShapeDtypeStruct((ROWS + 5, blocks, LANES), jnp.float32),
         in_specs=[hbm, hbm],
         out_specs=pl.BlockSpec(memory_space=pltpu.VMEM),
         scratch_shapes=[
@@ -136,7 +139,7 @@
         ],
         compiler_params=pltpu.CompilerParams(vmem_limit_bytes=32 << 20),
         name="local_tree",
-    )(shift_table, filterbank)
+    )(pltpu.with_memory_space_constraint(shift_table, pltpu.HBM), pltpu.with_memory_space_constraint(filterbank, pltpu.HBM))
 
 
 def mean_path(mean, table_ref, scratch, blocks, lane, channels, row):
@@ -242,7 +245,7 @@
 
 def cross_kernel(
     channels, count, finishing, table_ref, width_ref,
-    own_ref, core_ref, x_ref, z1_ref, z2_ref, z3_ref, mean_ref,
+    own_ref, core_ref, x_ref, both_ref, z1_ref, z3_ref, z2_ref, pc_ref, px_ref, pb_ref, mean_ref,
     *rest,
 ):
     blocks = own_ref.shape[1]
@@ -260,13 +263,15 @@
     place(0, own_ref[0])
     place(1, core_ref[0])
     place(2, x_ref[0])
-    place(3, x_ref[4])
-    for step, ref in ((1, z1_ref), (2, z2_ref), (3, z3_ref)):
+    place(3, both_ref[0])
+    for step, ref in ((1, z1_ref), (3, z3_ref)):
         for inner in range(4):
             place(4 * step + inner, ref[inner])
+    for inner, ref in enumerate((z2_ref, pc_ref, px_ref, pb_ref)):
+        place(8 + inner, ref[0])
     mean = mean_ref[0]
     if finishing:
-        mean = mean + z1_ref[4] + z2_ref[4] + z3_ref[4]
+        mean = mean + z1_ref[4] + z3_ref[4] + pc_ref[1] + px_ref[1] + pb_ref[1]
     mean = mean / (channels * count)
     rows = cross_tree(me, mean, table_ref, first, second, spare, blocks, lane, channels)
     if finishing:
@@ -346,19 +351,22 @@
     rows = local_rows(filterbank, shift_table)
     small = section_count == 4
 
-    core = swapped(rows[8:], 1)
-    mean = rows[ROWS:] + core[8:]
-    across = swapped(jnp.concatenate([rows[4:8], core[4:8], mean], axis=0), 2)
-    mean = mean + across[8:]
-    arrived = []
-    for step in (1, 2, 3):
-        low = (0, 2, 1, 3)[step]
-        parts = [part[low : low + 1] for part in (rows, core, across, across[4:8])]
-        if small:
-            parts.append(mean)
-        arrived.append(swapped(jnp.concatenate(parts, axis=0), 4 * step))
+    across = swapped(rows[4:8], 2)
+    both = swapped(rows[12:16], 3)
+    core = swapped(rows[8:12], 1)
+    z2 = swapped(rows[16:], 8)
+    plane = (rows, core, across, both)
+    mean = sum(part[3:4] for part in plane)
+    z1 = swapped(jnp.concatenate([part[1:2] for part in plane] + [mean], axis=0), 4)
+    z3 = swapped(jnp.concatenate([part[2:3] for part in plane] + [mean], axis=0), 12)
+    passed = [
+        swapped(jnp.concatenate([z2[place : place + 1], z2[4:]], axis=0), offset)
+        for offset, place in ((1, 2), (2, 1), (3, 3))
+    ]
+    mean = mean + z2[4:]
+    arrived = [z1, z3, z2, *passed]
     if not small:
-        mean = lax.psum(rows[ROWS:], "chan")
+        mean = lax.psum(rows[3:4], "chan")
 
     smem = pl.BlockSpec(memory_space=pltpu.SMEM)
     vmem = pl.BlockSpec(memory_space=pltpu.VMEM)
@@ -368,13 +376,13 @@
         out_shape=final_shapes(blocks, widths)
         if small
         else jax.ShapeDtypeStruct((ROWS, blocks, LANES), jnp.float32),
-        in_specs=[smem] * 2 + [vmem] * 7,
+        in_specs=[smem] * 2 + [vmem] * 11,
         out_specs=(vmem, vmem) if small else vmem,
         scratch_shapes=[row_scratch(blocks)] * 3 + (finish_scratch(blocks) if small else []),
         compiler_params=params,
         name="cross_tree",
     )
-    result = call(shift_table, box_widths, rows, core, across, *arrived, mean)
+    result = call(shift_table, box_widths, *plane, *arrived, mean)
     if small:
         return tuple(result)
     me = lax.axis_index("chan")

time: 28.1 us -> 24.9 us (0.89)
  waiting for transfers between devices: 11.4 us -> 7.51 us
  starting transfers between devices: 7.92 us -> 10.1 us
  local copies, waits for them, and re-layouts: 1.76 us -> 0.05 us
    ppermute x5 -> x9, waiting for transfers between devices: 11.4 us -> 7.51 us  [swapped(): lax.ppermute(block, 'chan', [(device, device ^ distance) for device in ra...]
    ppermute x5 -> x9, starting transfers between devices: 7.92 us -> 10.1 us  [swapped(): lax.ppermute(block, 'chan', [(device, device ^ distance) for device in ra...]
    unnamed x9 -> x7, local copies, waits for them, and re-layouts: 1.73 us -> 0.02 us
  transfers between devices with their start and end apart: 5 -> 9, of which waited for: 5 -> 5; matrix products, arithmetic and copies ran while one was open for 0% -> 0% of each run, Pallas kernels for 0% -> 0%
where the time goes in v3:
time: 24.9 us; the launch traced here: 24.8 us
  starting transfers between devices  10.1 us (41%)
  waiting for transfers between devices  7.51 us (30%)
  Pallas kernels  6.36 us (26%)
  between operations  0.71 us (3%)
    ppermute x9, starting transfers between devices, swapped(): lax.ppermute(block, 'chan', [(device, device ^ distance) for device in ra...  10.1 us
    ppermute x9, waiting for transfers between devices, swapped(): lax.ppermute(block, 'chan', [(device, device ^ distance) for device in ra...  7.51 us
    pallas_call x1, Pallas kernels, shards(): result = call(shift_table, box_widths, *plane, *arrived, mean)  3.43 us
    pallas_call x1, Pallas kernels, local_rows(): pl.pallas_call(local_kernel, out_shape=jax.ShapeDtypeStruct((ROWS + 5, bl...  2.93 us
  transfers between devices with their start and end apart: 9, of which 5 were waited for; matrix products, arithmetic and copies ran while one was open for 0% of the time, Pallas kernels for 0%

profile of v3, /device:TPU:0, one launch (start us, length us, event | category | flops | bytes accessed | tf_op | source)
XLA Modules:
  0.0 24.8 jit_solution(7124261637373658808)
XLA Ops:
  0.6 2.9 %local_tree.1.own_ref = f32[21,32,128]{2,1,0:T(8,128)S(1)} custom-call(s32[511]{0:T(512)} %table_ref.1, bf16[64,4096]{1,0:T(8,128)(2,1)} %x_hbm.1), custom_call_target="tpu_custom_call" | custom-call | tf_op jit(solution)/shard_map/local_tree/pallas_call | solution.py:126
  3.6 4.1 %collective-permute-start.5 = (f32[5,32,128]{2,1,0:T(8,128)S(1)}, f32[5,32,128]{2,1,0:T(8,128)S(1)}, u32[]{:S(2)}, u32[]{:S(2)}) collective-permute-start(f32[5,32,128]{2,1,0:T(8,128)S(1)} %slice.96), channel_id=1, source_target_pairs={{0,8},{1,9},{2,10},{3,11},{4,12},{5,13},{6,14},{7,15},{8,0},{9,1},... | collective-permute-start | bytes 245768 | tf_op jit(solution)/shard_map/ppermute | solution.py:311
  7.7 0.1 collective-permute-start
  7.8 1.6 %collective-permute-start.1 = (f32[4,32,128]{2,1,0:T(8,128)S(1)}, f32[4,32,128]{2,1,0:T(8,128)S(1)}, u32[]{:S(2)}, u32[]{:S(2)}) collective-permute-start(f32[4,32,128]{2,1,0:T(8,128)S(1)} %get-tuple-element.7), channel_id=1, source_target_pairs={{0,2},{1,3},{2,0},{3,1},{4,6},{5,7},{6,4},{7,5},{8,10},{9,11},{10,... | collective-permute-start | bytes 196616 | tf_op jit(solution)/shard_map/ppermute | solution.py:311
  9.3 0.3 %collective-permute-start.2 = (f32[4,32,128]{2,1,0:T(8,128)S(1)}, f32[4,32,128]{2,1,0:T(8,128)S(1)}, u32[]{:S(2)}, u32[]{:S(2)}) collective-permute-start(f32[4,32,128]{2,1,0:T(8,128)S(1)} %get-tuple-element.6), channel_id=1, source_target_pairs={{0,3},{1,2},{2,1},{3,0},{4,7},{5,6},{6,5},{7,4},{8,11},{9,10},{10,... | collective-permute-start | bytes 196616 | tf_op jit(solution)/shard_map/ppermute | solution.py:311
  9.6 0.0 collective-permute-done.core_ref
  9.6 2.6 %collective-permute-done.1.x_ref = f32[4,32,128]{2,1,0:T(8,128)S(1)} collective-permute-done((f32[4,32,128]{2,1,0:T(8,128)S(1)}, f32[4,32,128]{2,1,0:T(8,128)S(1)}, u32[]{:S(2)}, u32[]{:S(2)}) %collective-permute-start.1) | collective-permute-done | bytes 65568 | tf_op jit(solution)/shard_map/ppermute | solution.py:311
  12.3 1.1 %collective-permute-done.2.both_ref = f32[4,32,128]{2,1,0:T(8,128)S(1)} collective-permute-done((f32[4,32,128]{2,1,0:T(8,128)S(1)}, f32[4,32,128]{2,1,0:T(8,128)S(1)}, u32[]{:S(2)}, u32[]{:S(2)}) %collective-permute-start.2) | collective-permute-done | bytes 65568 | tf_op jit(solution)/shard_map/ppermute | solution.py:311
  13.4 0.0 collective-permute-done.5.z2_ref
  13.5 1.6 %collective-permute-start.3 = (f32[5,32,128]{2,1,0:T(8,128)S(1)}, f32[5,32,128]{2,1,0:T(8,128)S(1)}, u32[]{:S(2)}, u32[]{:S(2)}) collective-permute-start(f32[5,32,128]{2,1,0:T(8,128)S(1)} %get-tuple-element.21), channel_id=1, source_target_pairs={{0,4},{1,5},{2,6},{3,7},{4,0},{5,1},{6,2},{7,3},{8,12},{9,13},{10,... | collective-permute-start | bytes 245768 | tf_op jit(solution)/shard_map/ppermute | solution.py:311
  15.1 0.5 %collective-permute-start.4 = (f32[5,32,128]{2,1,0:T(8,128)S(1)}, f32[5,32,128]{2,1,0:T(8,128)S(1)}, u32[]{:S(2)}, u32[]{:S(2)}) collective-permute-start(f32[5,32,128]{2,1,0:T(8,128)S(1)} %get-tuple-element.20), channel_id=1, source_target_pairs={{0,12},{1,13},{2,14},{3,15},{4,8},{5,9},{6,10},{7,11},{8,4},{9,5},... | collective-permute-start | bytes 245768 | tf_op jit(solution)/shard_map/ppermute | solution.py:311
  15.6 0.0 collective-permute-start.6
  15.6 1.6 %collective-permute-start.7 = (f32[2,32,128]{2,1,0:T(8,128)S(1)}, f32[2,32,128]{2,1,0:T(8,128)S(1)}, u32[]{:S(2)}, u32[]{:S(2)}) collective-permute-start(f32[2,32,128]{2,1,0:T(8,128)S(1)} %get-tuple-element.18), channel_id=1, source_target_pairs={{0,2},{1,3},{2,0},{3,1},{4,6},{5,7},{6,4},{7,5},{8,10},{9,11},{10,... | collective-permute-start | bytes 98312 | tf_op jit(solution)/shard_map/ppermute | solution.py:311
  17.2 0.0 copy-start
  17.2 0.0 copy-start.1
  17.2 0.4 %collective-permute-start.8 = (f32[2,32,128]{2,1,0:T(8,128)S(1)}, f32[2,32,128]{2,1,0:T(8,128)S(1)}, u32[]{:S(2)}, u32[]{:S(2)}) collective-permute-start(f32[2,32,128]{2,1,0:T(8,128)S(1)} %concatenate.20), channel_id=1, source_target_pairs={{0,3},{1,2},{2,1},{3,0},{4,7},{5,6},{6,5},{7,4},{8,11},{9,10},{10,... | collective-permute-start | bytes 98312 | tf_op jit(solution)/shard_map/ppermute | solution.py:311
  17.6 0.0 collective-permute-done.6.pc_ref
  17.6 2.1 %collective-permute-done.7.px_ref = f32[2,32,128]{2,1,0:T(8,128)S(1)} collective-permute-done((f32[2,32,128]{2,1,0:T(8,128)S(1)}, f32[2,32,128]{2,1,0:T(8,128)S(1)}, u32[]{:S(2)}, u32[]{:S(2)}) %collective-permute-start.7) | collective-permute-done | bytes 32800 | tf_op jit(solution)/shard_map/ppermute | solution.py:311
  19.6 1.0 %collective-permute-done.8.pb_ref = f32[2,32,128]{2,1,0:T(8,128)S(1)} collective-permute-done((f32[2,32,128]{2,1,0:T(8,128)S(1)}, f32[2,32,128]{2,1,0:T(8,128)S(1)}, u32[]{:S(2)}, u32[]{:S(2)}) %collective-permute-start.8) | collective-permute-done | bytes 32800 | tf_op jit(solution)/shard_map/ppermute | solution.py:311
  20.6 0.0 collective-permute-done.3.z1_ref
  20.6 0.7 %collective-permute-done.4.z3_ref = f32[5,32,128]{2,1,0:T(8,128)S(1)} collective-permute-done((f32[5,32,128]{2,1,0:T(8,128)S(1)}, f32[5,32,128]{2,1,0:T(8,128)S(1)}, u32[]{:S(2)}, u32[]{:S(2)}) %collective-permute-start.4) | collective-permute-done | bytes 81952 | tf_op jit(solution)/shard_map/ppermute | solution.py:311
  21.3 0.0 copy-done
  21.3 0.0 copy-done.1
  21.3 3.4 %cross_tree.1 = (bf16[16,4096]{1,0:T(8,128)(2,1)}, f32[8,16]{1,0:T(8,128)}) custom-call(s32[511]{0:T(512)S(1)} %copy-done, s32[8]{0:T(128)S(1)} %copy-done.1, f32[21,32,128]{2,1,0:T(8,128)S(1)} %local_tree.1.own_ref, f32[4,32,128]{2,1,0:T(8,128)S(1)} %collective-permute-done.core_ref, f32[4,32,128]{2,1,0:T(8,128)S(1)} %collective-permute-done.1.x_ref, ...), custom_call_target="tpu_custom_call" | custom-call | tf_op jit(solution)/shard_map/cross_tree/pallas_call | solution.py:385
  (9 shorter events, 0.1 us)
Async XLA Ops:
  3.6 9.8 %collective-permute-start.5 = (f32[5,32,128]{2,1,0:T(8,128)S(1)}, f32[5,32,128]{2,1,0:T(8,128)S(1)}, u32[]{:S(2)}, u32[]{:S(2)}) collective-permute-start(f32[5,32,128]{2,1,0:T(8,128)S(1)} %slice.96), channel_id=1, source_target_pairs={{0,8},{1,9},{2,10},{3,11},{4,12},{5,13},{6,14},{7,15},{8,0},{9,1},... | collective-permute-start | bytes 245768 | tf_op jit(solution)/shard_map/ppermute | solution.py:311
  7.7 1.9 %collective-permute-start = (f32[4,32,128]{2,1,0:T(8,128)S(1)}, f32[4,32,128]{2,1,0:T(8,128)S(1)}, u32[]{:S(2)}, u32[]{:S(2)}) collective-permute-start(f32[4,32,128]{2,1,0:T(8,128)S(1)} %get-tuple-element.8), channel_id=1, source_target_pairs={{0,1},{1,0},{2,3},{3,2},{4,5},{5,4},{6,7},{7,6},{8,9},{9,8},{10,11... | collective-permute-start | bytes 196616 | tf_op jit(solution)/shard_map/ppermute | solution.py:311
  7.8 4.5 %collective-permute-start.1 = (f32[4,32,128]{2,1,0:T(8,128)S(1)}, f32[4,32,128]{2,1,0:T(8,128)S(1)}, u32[]{:S(2)}, u32[]{:S(2)}) collective-permute-start(f32[4,32,128]{2,1,0:T(8,128)S(1)} %get-tuple-element.7), channel_id=1, source_target_pairs={{0,2},{1,3},{2,0},{3,1},{4,6},{5,7},{6,4},{7,5},{8,10},{9,11},{10,... | collective-permute-start | bytes 196616 | tf_op jit(solution)/shard_map/ppermute | solution.py:311
  9.3 4.0 %collective-permute-start.2 = (f32[4,32,128]{2,1,0:T(8,128)S(1)}, f32[4,32,128]{2,1,0:T(8,128)S(1)}, u32[]{:S(2)}, u32[]{:S(2)}) collective-permute-start(f32[4,32,128]{2,1,0:T(8,128)S(1)} %get-tuple-element.6), channel_id=1, source_target_pairs={{0,3},{1,2},{2,1},{3,0},{4,7},{5,6},{6,5},{7,4},{8,11},{9,10},{10,... | collective-permute-start | bytes 196616 | tf_op jit(solution)/shard_map/ppermute | solution.py:311
  13.5 7.2 %collective-permute-start.3 = (f32[5,32,128]{2,1,0:T(8,128)S(1)}, f32[5,32,128]{2,1,0:T(8,128)S(1)}, u32[]{:S(2)}, u32[]{:S(2)}) collective-permute-start(f32[5,32,128]{2,1,0:T(8,128)S(1)} %get-tuple-element.21), channel_id=1, source_target_pairs={{0,4},{1,5},{2,6},{3,7},{4,0},{5,1},{6,2},{7,3},{8,12},{9,13},{10,... | collective-permute-start | bytes 245768 | tf_op jit(solution)/shard_map/ppermute | solution.py:311
  15.1 6.2 %collective-permute-start.4 = (f32[5,32,128]{2,1,0:T(8,128)S(1)}, f32[5,32,128]{2,1,0:T(8,128)S(1)}, u32[]{:S(2)}, u32[]{:S(2)}) collective-permute-start(f32[5,32,128]{2,1,0:T(8,128)S(1)} %get-tuple-element.20), channel_id=1, source_target_pairs={{0,12},{1,13},{2,14},{3,15},{4,8},{5,9},{6,10},{7,11},{8,4},{9,5},... | collective-permute-start | bytes 245768 | tf_op jit(solution)/shard_map/ppermute | solution.py:311
  15.6 1.9 %collective-permute-start.6 = (f32[2,32,128]{2,1,0:T(8,128)S(1)}, f32[2,32,128]{2,1,0:T(8,128)S(1)}, u32[]{:S(2)}, u32[]{:S(2)}) collective-permute-start(f32[2,32,128]{2,1,0:T(8,128)S(1)} %get-tuple-element.19), channel_id=1, source_target_pairs={{0,1},{1,0},{2,3},{3,2},{4,5},{5,4},{6,7},{7,6},{8,9},{9,8},{10,11... | collective-permute-start | bytes 98312 | tf_op jit(solution)/shard_map/ppermute | solution.py:311
  15.6 4.0 %collective-permute-start.7 = (f32[2,32,128]{2,1,0:T(8,128)S(1)}, f32[2,32,128]{2,1,0:T(8,128)S(1)}, u32[]{:S(2)}, u32[]{:S(2)}) collective-permute-start(f32[2,32,128]{2,1,0:T(8,128)S(1)} %get-tuple-element.18), channel_id=1, source_target_pairs={{0,2},{1,3},{2,0},{3,1},{4,6},{5,7},{6,4},{7,5},{8,10},{9,11},{10,... | collective-permute-start | bytes 98312 | tf_op jit(solution)/shard_map/ppermute | solution.py:311
  17.2 4.1 %copy-start = (s32[511]{0:T(512)S(1)}, s32[511]{0:T(512)}, u32[]{:S(2)}) copy-start(s32[511]{0:T(512)} %table_ref.1) | copy-start | bytes 6136
  17.2 4.1 %copy-start.1 = (s32[8]{0:T(128)S(1)}, s32[8]{0:T(128)}, u32[]{:S(2)}) copy-start(s32[8]{0:T(128)} %width_ref.1) | copy-start | bytes 100
  17.2 3.4 %collective-permute-start.8 = (f32[2,32,128]{2,1,0:T(8,128)S(1)}, f32[2,32,128]{2,1,0:T(8,128)S(1)}, u32[]{:S(2)}, u32[]{:S(2)}) collective-permute-start(f32[2,32,128]{2,1,0:T(8,128)S(1)} %concatenate.20), channel_id=1, source_target_pairs={{0,3},{1,2},{2,1},{3,0},{4,7},{5,6},{6,5},{7,4},{8,11},{9,10},{10,... | collective-permute-start | bytes 98312 | tf_op jit(solution)/shard_map/ppermute | solution.py:311

commit v4 on v3

v4 whole, which is shorter than its diff:
```python
import functools

import jax
import jax.numpy as jnp
from jax import lax
from jax.experimental import pallas as pl
from jax.experimental.pallas import tpu as pltpu
from jax.sharding import PartitionSpec as P

ROWS = 16
LANES = 128
PAD = 8
WIDTHS = 8
PATH = ((1, 0), (1, 1), (2, 2), (4, 3), (8, 4), (16, 5))

epsilon = 1e-05


def reverse4(value):
    return (value & 1) << 3 | (value & 2) << 1 | (value & 4) >> 1 | (value & 8) >> 3


def lane_index(blocks):
    return lax.broadcasted_iota(jnp.int32, (blocks, LANES), 1)


def moved(here, beyond, lane, part):
    return pltpu.roll(jnp.where(lane >= part, here, beyond), (LANES - part) & 127, axis=1)


def later(ref, row, blocks, lane, shift):
    whole = shift >> 7
    here = ref[row, pl.ds(whole, blocks), :]
    beyond = ref[row, pl.ds(whole + 1, blocks), :]
    return moved(here, beyond, lane, shift & 127)


def clear_tail(ref, rows, blocks):
    for row in rows:
        ref[row, blocks : blocks + PAD, :] = jnp.zeros((PAD, LANES), jnp.float32)


def spread_sum(terms):
    strands = [None] * 4
    for index, term in enumerate(terms):
        strand = strands[index % 4]
        strands[index % 4] = term if strand is None else strand + term
    return (strands[0] + strands[1]) + (strands[2] + strands[3])


def packed_words(table_ref, width_ref, row):
    path, cross = jnp.int32(0), jnp.int32(0)
    spot = 0
    for trials, _ in PATH:
        index = row >> (ROWS // trials).bit_length() - 1
        path = path | (table_ref[trials - 1 + index] - 2 * index) << spot
        spot += 1
    spot = 0
    for fresh in (2, 4, 8, 16):
        for trial in range(fresh):
            index = row * fresh + trial
            cross = cross | (table_ref[ROWS * fresh - 1 + index] - 2 * index) << spot
            spot += 1
    words = [path, cross]
    for start in range(0, WIDTHS, 4):
        word = jnp.int32(0)
        for place in range(4):
            word = word | width_ref[start + place] << 8 * place
        words.append(word)
    return words


def local_kernel(
    table_hbm, width_hbm, x_hbm, rows_ref, words_ref,
    table_ref, width_ref, x_ref, normal, inner, quads, eights, sixteens, halves, small_sem, x_sem,
):
    channels, length = x_ref.shape
    blocks = length // LANES
    stride = blocks + PAD
    groups = channels // 16
    copies = [
        pltpu.make_async_copy(x_hbm.at[pl.ds(16 * group, 16)], x_ref.at[pl.ds(16 * group, 16)], x_sem.at[group])
        for group in range(groups)
    ]
    for copy in copies:
        copy.start()
    table_copy = pltpu.make_async_copy(table_hbm, table_ref, small_sem.at[0])
    width_copy = pltpu.make_async_copy(width_hbm, width_ref, small_sem.at[1])
    table_copy.start()
    width_copy.start()
    lane = lane_index(blocks)
    flat = normal.reshape(channels * stride, LANES)
    clear_tail(normal, range(3, channels, 4), blocks)
    clear_tail(inner, range(ROWS), blocks)
    for ref in (quads, eights, sixteens, halves):
        clear_tail(ref, range(ROWS), blocks)

    def row_of(ref, row):
        return ref[row, 0:blocks, :]

    for group in range(groups):
        rows = slice(16 * group, 16 * group + 16)

        def piece(block):
            return x_ref[rows, block * LANES : (block + 1) * LANES].astype(jnp.float32)

        copies[group].wait()
        total = spread_sum(piece(block) for block in range(blocks))
        centre = jnp.sum(total, axis=1, keepdims=True) / length
        centre = jnp.broadcast_to(centre, (16, LANES))
        total = spread_sum(jnp.square(piece(block) - centre) for block in range(blocks))
        spread = jnp.sum(total, axis=1, keepdims=True) / length
        gain = jnp.broadcast_to(lax.rsqrt(spread + epsilon), (16, LANES))
        for block in range(blocks):
            value = (piece(block) - centre) * gain
            for half in range(2):
                start = (16 * group + 8 * half) * stride + block
                flat[pl.ds(start, 8, stride=stride), :] = value[8 * half : 8 * half + 8]
    table_copy.wait()
    width_copy.wait()

    shift = table_ref[0]
    partial = []
    for quad in range(ROWS):
        pair = row_of(normal, 4 * quad + 1) + row_of(normal, 4 * quad + 2)
        inner[quad, 0:blocks, :] = pair + later(normal, 4 * quad + 3, blocks, lane, shift)
        partial.append(pair + (row_of(normal, 4 * quad) + row_of(normal, 4 * quad + 3)))
    partial = spread_sum(partial)
    for row in (3, 7, 11, 15, 20):
        rows_ref[row] = partial
    for quad in range(ROWS):
        quads[quad, 0:blocks, :] = row_of(normal, 4 * quad) + later(inner, quad, blocks, lane, shift)
    bands, trials = ROWS, 1
    for source, target in ((quads, eights), (eights, sixteens), (sixteens, halves)):
        fresh = 2 * trials
        for trial in range(fresh):
            shift = table_ref[fresh - 1 + trial]
            for band in range(bands // 2):
                high = later(source, (2 * band + 1) * trials + trial // 2, blocks, lane, shift)
                value = row_of(source, 2 * band * trials + trial // 2) + high
                target[band * fresh + trial, 0:blocks, :] = value
        bands, trials = bands // 2, fresh
    mine = reverse4(lax.axis_index("chan") & 15)
    for trial in range(ROWS):
        high = later(halves, 8 + trial // 2, blocks, lane, table_ref[ROWS - 1 + trial])
        place = mine ^ trial
        group, low = place >> 2, place & 3
        spot = jnp.where(low == 1, ROWS + group, place - (low > 0))
        rows_ref[spot] = row_of(halves, trial // 2) + high
    small_lane = lax.broadcasted_iota(jnp.int32, words_ref.shape, 1)
    words = jnp.zeros(words_ref.shape, jnp.int32)
    for index, word in enumerate(packed_words(table_ref, width_ref, mine)):
        words = jnp.where(small_lane == index, word, words)
    words_ref[...] = words


def local_rows(filterbank, shift_table, box_widths):
    channels, length = filterbank.shape
    blocks = length // LANES
    hbm = pl.BlockSpec(memory_space=pltpu.HBM)
    vmem = pl.BlockSpec(memory_space=pltpu.VMEM)
    inputs = [pltpu.with_memory_space_constraint(value, pltpu.HBM) for value in (shift_table, box_widths, filterbank)]
    return pl.pallas_call(
        local_kernel,
        out_shape=(
            jax.ShapeDtypeStruct((ROWS + 5, blocks, LANES), jnp.float32),
            jax.ShapeDtypeStruct((8, LANES), jnp.int32),
        ),
        in_specs=[hbm] * 3,
        out_specs=(vmem, vmem),
        scratch_shapes=[
            pltpu.SMEM(shift_table.shape, jnp.int32),
            pltpu.SMEM(box_widths.shape, jnp.int32),
            pltpu.VMEM(filterbank.shape, filterbank.dtype),
            pltpu.VMEM((channels, blocks + PAD, LANES), jnp.float32),
            *[row_scratch(blocks)] * 5,
            pltpu.SemaphoreType.DMA((2,)),
            pltpu.SemaphoreType.DMA((channels // 16,)),
        ],
        compiler_params=pltpu.CompilerParams(vmem_limit_bytes=32 << 20),
        name="local_tree",
    )(*inputs)


def mean_path(mean, word, scratch, blocks, lane, row):
    value = mean
    for step in range(0, len(PATH), 2):
        shifts = []
        for trials, spot in PATH[step : step + 2]:
            index = row >> (ROWS // trials).bit_length() - 1
            shifts.append(2 * index + (word >> spot & 1))
        scratch[step, 0:blocks, :] = value
        near, far = shifts
        value = (value + later(scratch, step, blocks, lane, near)) + (
            later(scratch, step, blocks, lane, far) + later(scratch, step, blocks, lane, near + far)
        )
    return value


def cross_tree(me, mean, words, buffers, spare, blocks, lane):
    row = reverse4(me & 15)
    path, cross = words[0], words[1]
    mean = mean_path(mean, path, spare, blocks, lane, row)
    spare[ROWS - 1, 0:blocks, :] = mean
    bands, trials = ROWS, 1
    spot = 0
    for source, target in zip(buffers[:-1], buffers[1:]):
        fresh = 2 * trials
        for trial in range(fresh):
            shift = 2 * (row * fresh + trial) + (cross >> spot & 1)
            spot += 1
            old = trial // 2
            if bands == ROWS:
                taken = mean + later(spare, ROWS - 1, blocks, lane, shift)
            for band in range(bands // 2):
                high = later(source, (2 * band + 1) * trials + old, blocks, lane, shift)
                value = source[2 * band * trials + old, 0:blocks, :] + high
                if bands == ROWS:
                    value = value - taken
                target[band * fresh + trial, 0:blocks, :] = value
        bands, trials = bands // 2, fresh
    return buffers[-1]


def finish(rows, widths, out_ref, peaks_ref, prefix, split):
    stride = rows.shape[1]
    blocks = stride - PAD
    length = blocks * LANES
    lane = lax.broadcasted_iota(jnp.int32, (ROWS, LANES), 1)
    flat = rows.reshape(ROWS * stride, LANES)

    total = jnp.zeros((ROWS, LANES), jnp.float32)
    for block in range(blocks):
        value = jnp.concatenate(
            [flat[pl.ds(block + 8 * half * stride, 8, stride=stride), :] for half in range(2)], axis=0
        )
        prefix[2 + block] = value
        total = total + value
    centre = jnp.sum(total, axis=1, keepdims=True) / length
    centre = jnp.broadcast_to(centre, (ROWS, LANES))
    total = jnp.zeros((ROWS, LANES), jnp.float32)
    for block in range(blocks):
        total = total + jnp.square(prefix[2 + block] - centre)
    spread = jnp.sum(total, axis=1, keepdims=True) / length
    gain = jnp.broadcast_to(lax.rsqrt(spread + epsilon), (ROWS, LANES))
    for block in range(blocks):
        value = (prefix[2 + block] - centre) * gain
        rounded = value.astype(jnp.bfloat16)
        out_ref[:, pl.ds(block * LANES, LANES)] = rounded
        split[pl.ds(block * ROWS, ROWS), pl.ds(0, LANES)] = rounded
        rest = value - rounded.astype(jnp.float32)
        split[pl.ds(block * ROWS, ROWS), pl.ds(LANES, LANES)] = rest.astype(jnp.bfloat16)

    above = lax.broadcasted_iota(jnp.int32, (2 * LANES, 2 * LANES), 0) & 127
    across = lax.broadcasted_iota(jnp.int32, (2 * LANES, 2 * LANES), 1)
    weights = jnp.where(above <= across, 1.0, 0.0).astype(jnp.bfloat16)
    sums = jnp.dot(split[...], weights, preferred_element_type=jnp.float32)
    carry = jnp.zeros((ROWS, LANES), jnp.float32)
    prefix[0] = carry
    prefix[1] = carry
    for block in range(blocks):
        part = sums[block * ROWS : (block + 1) * ROWS]
        prefix[2 + block] = part[:, :LANES] + carry
        carry = carry + part[:, LANES:]

    peaks = jnp.zeros((ROWS, LANES), jnp.float32)
    backs = [2 * LANES - width for width in widths]
    heres = [prefix[back >> 7] for back in backs]
    best = [None] * len(widths)
    for block in range(blocks):
        now = prefix[2 + block]
        for index, back in enumerate(backs):
            beyond = prefix[(back >> 7) + block + 1]
            gap = now - moved(heres[index], beyond, lane, back & 127)
            best[index] = gap if best[index] is None else jnp.maximum(best[index], gap)
            heres[index] = beyond
    for index, width in enumerate(widths):
        peak = jnp.max(best[index], axis=1, keepdims=True)
        scale = lax.rsqrt(jnp.full((ROWS, LANES), width, jnp.int32).astype(jnp.float32))
        peaks = jnp.where(lane == index, peak * scale, peaks)
    peaks_ref[...] = jnp.transpose(peaks)[: len(widths)]


def cross_kernel(
    channels, count, finishing, words_ref,
    own_ref, core_ref, x_ref, both_ref, z1_ref, z3_ref, z2_ref, pc_ref, px_ref, pb_ref, mean_ref,
    *rest,
):
    blocks = own_ref.shape[1]
    lane = lane_index(blocks)
    if finishing:
        out_ref, peaks_ref, spare, *buffers, prefix, split = rest
    else:
        series_ref, spare, *buffers = rest
    words = [words_ref[0, index] for index in range(2 + WIDTHS // 4)]
    for ref in (spare, *buffers):
        clear_tail(ref, range(ROWS), blocks)
    first = buffers[0]
    me = lax.axis_index("chan")
    here = me & 15

    def place(offset, value):
        first[here ^ offset, pl.ds(0, blocks), :] = value

    place(0, own_ref[0])
    place(1, core_ref[0])
    place(2, x_ref[0])
    place(3, both_ref[0])
    for step, ref in ((1, z1_ref), (3, z3_ref)):
        for inner in range(4):
            place(4 * step + inner, ref[inner])
    for inner, ref in enumerate((z2_ref, pc_ref, px_ref, pb_ref)):
        place(8 + inner, ref[0])
    mean = mean_ref[0]
    if finishing:
        mean = mean + z1_ref[4] + z3_ref[4] + pc_ref[1] + px_ref[1] + pb_ref[1]
    mean = mean / (channels * count)
    rows = cross_tree(me, mean, words, buffers, spare, blocks, lane)
    if finishing:
        finish(rows, unpacked_widths(words), out_ref, peaks_ref, prefix, split)
    else:
        for trial in range(ROWS):
            series_ref[trial] = rows[trial, pl.ds(0, blocks), :]


def unpacked_widths(words):
    return [words[2 + index // 4] >> 8 * (index % 4) & 255 for index in range(WIDTHS)]


def finish_kernel(words_ref, series_ref, out_ref, peaks_ref, rows, *scratch):
    blocks = series_ref.shape[1]
    words = [words_ref[0, index] for index in range(2 + WIDTHS // 4)]
    for trial in range(ROWS):
        rows[trial, pl.ds(0, blocks), :] = series_ref[trial]
    finish(rows, unpacked_widths(words), out_ref, peaks_ref, *scratch)


def row_scratch(blocks):
    return pltpu.VMEM((ROWS, blocks + PAD, LANES), jnp.float32)


def finish_scratch(blocks):
    return [
        pltpu.VMEM((blocks + 2, ROWS, LANES), jnp.float32),
        pltpu.VMEM((blocks * ROWS, 2 * LANES), jnp.bfloat16),
    ]


def final_shapes(blocks):
    return (
        jax.ShapeDtypeStruct((ROWS, blocks * LANES), jnp.bfloat16),
        jax.ShapeDtypeStruct((WIDTHS, ROWS), jnp.float32),
    )


def swapped(block, distance):
    count = lax.axis_size("chan")
    return lax.ppermute(block, "chan", [(device, device ^ distance) for device in range(count)])


def advance(rows_in, shifts, start):
    count, length = rows_in.shape
    padded = jnp.concatenate([rows_in, jnp.zeros_like(rows_in)], axis=1)
    moved = lax.dynamic_slice_in_dim(padded, jnp.minimum(2 * start, length), length, 1)
    moved = jnp.concatenate([moved, jnp.zeros((count, 2 * count), moved.dtype)], axis=1)
    width = length + 2 * count
    flat = jnp.concatenate([moved.reshape(-1), jnp.zeros((2 * count,), moved.dtype)])
    skewed = flat.reshape(count, width + 2)[:, :length]
    odd = jnp.concatenate([skewed[:, 1:], jnp.zeros((count, 1), moved.dtype)], axis=1)
    parity = shifts - 2 * (start + jnp.arange(count, dtype=jnp.int32))
    return jnp.where((parity == 1)[:, None], odd, skewed)


def wider_sections(current, shift_table, me, section_count):
    half = ROWS // 2
    position = reverse4(me % 16)
    for bit in range(4, section_count):
        side = me >> bit & 1
        trials_now = 2 * ROWS << bit
        theirs = lax.dynamic_slice_in_dim(current, (1 - side) * half, half, 0)
        ours = lax.dynamic_slice_in_dim(current, side * half, half, 0)
        arrived = swapped(theirs, 1 << bit)
        lower = jnp.where(side == 0, ours, arrived)
        upper = jnp.where(side == 0, arrived, ours)
        first_trial = 2 * (position * ROWS + side * half)
        shifts = lax.dynamic_slice_in_dim(shift_table, trials_now - 1 + first_trial, ROWS)
        current = jnp.repeat(lower, 2, axis=0) + advance(jnp.repeat(upper, 2, axis=0), shifts, first_trial)
        position = 2 * position + side
    return current


def shards(filterbank, shift_table, box_widths):
    channels, length = filterbank.shape
    blocks = length // LANES
    count = lax.axis_size("chan")
    section_count = count.bit_length() - 1
    rows, words = local_rows(filterbank, shift_table, box_widths)
    small = section_count == 4

    across = swapped(rows[4:8], 2)
    both = swapped(rows[12:16], 3)
    core = swapped(rows[8:12], 1)
    z2 = swapped(rows[16:], 8)
    plane = (rows, core, across, both)
    mean = sum(part[3:4] for part in plane)
    z1 = swapped(jnp.concatenate([part[1:2] for part in plane] + [mean], axis=0), 4)
    z3 = swapped(jnp.concatenate([part[2:3] for part in plane] + [mean], axis=0), 12)
    passed = [
        swapped(jnp.concatenate([z2[place : place + 1], z2[4:]], axis=0), offset)
        for offset, place in ((1, 2), (2, 1), (3, 3))
    ]
    mean = mean + z2[4:]
    arrived = [z1, z3, z2, *passed]
    if not small:
        mean = lax.psum(rows[3:4], "chan")

    vmem = pl.BlockSpec(memory_space=pltpu.VMEM)
    params = pltpu.CompilerParams(vmem_limit_bytes=32 << 20)
    call = pl.pallas_call(
        functools.partial(cross_kernel, channels, count, small),
        out_shape=final_shapes(blocks)
        if small
        else jax.ShapeDtypeStruct((ROWS, blocks, LANES), jnp.float32),
        in_specs=[vmem] * 12,
        out_specs=(vmem, vmem) if small else vmem,
        scratch_shapes=[
            *[row_scratch(blocks)] * 6,
            *(finish_scratch(blocks) if small else []),
        ],
        compiler_params=params,
        name="cross_tree",
    )
    result = call(words, *plane, *arrived, mean)
    if small:
        return tuple(result)
    me = lax.axis_index("chan")
    current = wider_sections(result.reshape(ROWS, length), shift_table, me, section_count)
    return tuple(
        pl.pallas_call(
            finish_kernel,
            out_shape=final_shapes(blocks),
            in_specs=[vmem, vmem],
            out_specs=(vmem, vmem),
            scratch_shapes=[row_scratch(blocks)] + finish_scratch(blocks),
            compiler_params=params,
            name="finish",
        )(words, current.reshape(ROWS, blocks, LANES))
    )


def solution(mesh):
    placed = (P(("beam", "chan"), None), P(), P())
    return jax.shard_map(
        shards,
        mesh=mesh,
        in_specs=placed,
        out_specs=(P(("beam", "chan"), None), P("beam", "chan")),
        check_vma=False,
    )
```

time: 24.9 us -> 24 us (0.964)
  Pallas kernels: 6.36 us -> 5.41 us
    pallas_call x2, Pallas kernels: 6.36 us -> 5.41 us  [the longest x1 2.75 us: local_rows(): pl.pallas_call(local_kernel, out_shape=(jax.ShapeDtypeStruct((ROWS + 5, b...]
where the time goes in v4:
time: 24 us; the launch traced here: 23.8 us
  starting transfers between devices  10.1 us (42%)
  waiting for transfers between devices  7.57 us (32%)
  Pallas kernels  5.41 us (23%)
  between operations  0.71 us (3%)
    ppermute x9, starting transfers between devices, swapped(): lax.ppermute(block, 'chan', [(device, device ^ distance) for device in ra...  10.1 us
    ppermute x9, waiting for transfers between devices, swapped(): lax.ppermute(block, 'chan', [(device, device ^ distance) for device in ra...  7.57 us
    pallas_call x1, Pallas kernels, local_rows(): pl.pallas_call(local_kernel, out_shape=(jax.ShapeDtypeStruct((ROWS + 5, b...  2.75 us
    pallas_call x1, Pallas kernels, shards(): result = call(words, *plane, *arrived, mean)  2.67 us
  transfers between devices with their start and end apart: 9, of which 5 were waited for; matrix products, arithmetic and copies ran while one was open for 0% of the time, Pallas kernels for 0%

profile of v4, /device:TPU:0, one launch (start us, length us, event | category | flops | bytes accessed | tf_op | source)
XLA Modules:
  0.0 23.8 jit_solution(8944612932917566246)
XLA Ops:
  0.6 2.7 %local_tree.1 = (f32[21,32,128]{2,1,0:T(8,128)S(1)}, s32[8,128]{1,0:T(8,128)S(1)}) custom-call(s32[511]{0:T(512)} %table_hbm.1, s32[8]{0:T(128)} %width_hbm.1, bf16[64,4096]{1,0:T(8,128)(2,1)} %x_hbm.1), custom_call_target="tpu_custom_call" | custom-call | tf_op jit(solution)/shard_map/local_tree/pallas_call | solution.py:163
  3.4 4.1 %collective-permute-start.5 = (f32[5,32,128]{2,1,0:T(8,128)S(1)}, f32[5,32,128]{2,1,0:T(8,128)S(1)}, u32[]{:S(2)}, u32[]{:S(2)}) collective-permute-start(f32[5,32,128]{2,1,0:T(8,128)S(1)} %slice.77), channel_id=1, source_target_pairs={{0,8},{1,9},{2,10},{3,11},{4,12},{5,13},{6,14},{7,15},{8,0},{9,1},... | collective-permute-start | bytes 245768 | tf_op jit(solution)/shard_map/ppermute | solution.py:358
  7.5 0.1 collective-permute-start
  7.6 1.6 %collective-permute-start.1 = (f32[4,32,128]{2,1,0:T(8,128)S(1)}, f32[4,32,128]{2,1,0:T(8,128)S(1)}, u32[]{:S(2)}, u32[]{:S(2)}) collective-permute-start(f32[4,32,128]{2,1,0:T(8,128)S(1)} %get-tuple-element.11), channel_id=1, source_target_pairs={{0,2},{1,3},{2,0},{3,1},{4,6},{5,7},{6,4},{7,5},{8,10},{9,11},{10,... | collective-permute-start | bytes 196616 | tf_op jit(solution)/shard_map/ppermute | solution.py:358
  9.2 0.3 %collective-permute-start.2 = (f32[4,32,128]{2,1,0:T(8,128)S(1)}, f32[4,32,128]{2,1,0:T(8,128)S(1)}, u32[]{:S(2)}, u32[]{:S(2)}) collective-permute-start(f32[4,32,128]{2,1,0:T(8,128)S(1)} %get-tuple-element.10), channel_id=1, source_target_pairs={{0,3},{1,2},{2,1},{3,0},{4,7},{5,6},{6,5},{7,4},{8,11},{9,10},{10,... | collective-permute-start | bytes 196616 | tf_op jit(solution)/shard_map/ppermute | solution.py:358
  9.5 0.0 collective-permute-done.core_ref
  9.5 2.6 %collective-permute-done.1.x_ref = f32[4,32,128]{2,1,0:T(8,128)S(1)} collective-permute-done((f32[4,32,128]{2,1,0:T(8,128)S(1)}, f32[4,32,128]{2,1,0:T(8,128)S(1)}, u32[]{:S(2)}, u32[]{:S(2)}) %collective-permute-start.1) | collective-permute-done | bytes 65568 | tf_op jit(solution)/shard_map/ppermute | solution.py:358
  12.1 1.1 %collective-permute-done.2.both_ref = f32[4,32,128]{2,1,0:T(8,128)S(1)} collective-permute-done((f32[4,32,128]{2,1,0:T(8,128)S(1)}, f32[4,32,128]{2,1,0:T(8,128)S(1)}, u32[]{:S(2)}, u32[]{:S(2)}) %collective-permute-start.2) | collective-permute-done | bytes 65568 | tf_op jit(solution)/shard_map/ppermute | solution.py:358
  13.2 0.0 collective-permute-done.5.z2_ref
  13.3 1.6 %collective-permute-start.3 = (f32[5,32,128]{2,1,0:T(8,128)S(1)}, f32[5,32,128]{2,1,0:T(8,128)S(1)}, u32[]{:S(2)}, u32[]{:S(2)}) collective-permute-start(f32[5,32,128]{2,1,0:T(8,128)S(1)} %get-tuple-element.25), channel_id=1, source_target_pairs={{0,4},{1,5},{2,6},{3,7},{4,0},{5,1},{6,2},{7,3},{8,12},{9,13},{10,... | collective-permute-start | bytes 245768 | tf_op jit(solution)/shard_map/ppermute | solution.py:358
  14.9 0.5 %collective-permute-start.4 = (f32[5,32,128]{2,1,0:T(8,128)S(1)}, f32[5,32,128]{2,1,0:T(8,128)S(1)}, u32[]{:S(2)}, u32[]{:S(2)}) collective-permute-start(f32[5,32,128]{2,1,0:T(8,128)S(1)} %get-tuple-element.24), channel_id=1, source_target_pairs={{0,12},{1,13},{2,14},{3,15},{4,8},{5,9},{6,10},{7,11},{8,4},{9,5},... | collective-permute-start | bytes 245768 | tf_op jit(solution)/shard_map/ppermute | solution.py:358
  15.5 0.0 collective-permute-start.6
  15.5 1.6 %collective-permute-start.7 = (f32[2,32,128]{2,1,0:T(8,128)S(1)}, f32[2,32,128]{2,1,0:T(8,128)S(1)}, u32[]{:S(2)}, u32[]{:S(2)}) collective-permute-start(f32[2,32,128]{2,1,0:T(8,128)S(1)} %get-tuple-element.22), channel_id=1, source_target_pairs={{0,2},{1,3},{2,0},{3,1},{4,6},{5,7},{6,4},{7,5},{8,10},{9,11},{10,... | collective-permute-start | bytes 98312 | tf_op jit(solution)/shard_map/ppermute | solution.py:358
  17.0 0.3 %collective-permute-start.8 = (f32[2,32,128]{2,1,0:T(8,128)S(1)}, f32[2,32,128]{2,1,0:T(8,128)S(1)}, u32[]{:S(2)}, u32[]{:S(2)}) collective-permute-start(f32[2,32,128]{2,1,0:T(8,128)S(1)} %concatenate.20), channel_id=1, source_target_pairs={{0,3},{1,2},{2,1},{3,0},{4,7},{5,6},{6,5},{7,4},{8,11},{9,10},{10,... | collective-permute-start | bytes 98312 | tf_op jit(solution)/shard_map/ppermute | solution.py:358
  17.3 0.0 collective-permute-done.6.pc_ref
  17.3 2.1 %collective-permute-done.7.px_ref = f32[2,32,128]{2,1,0:T(8,128)S(1)} collective-permute-done((f32[2,32,128]{2,1,0:T(8,128)S(1)}, f32[2,32,128]{2,1,0:T(8,128)S(1)}, u32[]{:S(2)}, u32[]{:S(2)}) %collective-permute-start.7) | collective-permute-done | bytes 32800 | tf_op jit(solution)/shard_map/ppermute | solution.py:358
  19.4 0.9 %collective-permute-done.8.pb_ref = f32[2,32,128]{2,1,0:T(8,128)S(1)} collective-permute-done((f32[2,32,128]{2,1,0:T(8,128)S(1)}, f32[2,32,128]{2,1,0:T(8,128)S(1)}, u32[]{:S(2)}, u32[]{:S(2)}) %collective-permute-start.8) | collective-permute-done | bytes 32800 | tf_op jit(solution)/shard_map/ppermute | solution.py:358
  20.4 0.0 collective-permute-done.3.z1_ref
  20.4 0.8 %collective-permute-done.4.z3_ref = f32[5,32,128]{2,1,0:T(8,128)S(1)} collective-permute-done((f32[5,32,128]{2,1,0:T(8,128)S(1)}, f32[5,32,128]{2,1,0:T(8,128)S(1)}, u32[]{:S(2)}, u32[]{:S(2)}) %collective-permute-start.4) | collective-permute-done | bytes 81952 | tf_op jit(solution)/shard_map/ppermute | solution.py:358
  21.2 2.7 %cross_tree.1 = (bf16[16,4096]{1,0:T(8,128)(2,1)}, f32[8,16]{1,0:T(8,128)}) custom-call(s32[8,128]{1,0:T(8,128)S(1)} %get-tuple-element.4.words_ref, f32[21,32,128]{2,1,0:T(8,128)S(1)} %get-tuple-element.5.own_ref, f32[4,32,128]{2,1,0:T(8,128)S(1)} %collective-permute-done.core_ref, f32[4,32,128]{2,1,0:T(8,128)S(1)} %collective-permute-done.1.x_ref, ...), custom_call_target="tpu_custom_call" | custom-call | tf_op jit(solution)/shard_map/cross_tree/pallas_call | solution.py:433
  (9 shorter events, 0.1 us)
Async XLA Ops:
  3.4 9.8 %collective-permute-start.5 = (f32[5,32,128]{2,1,0:T(8,128)S(1)}, f32[5,32,128]{2,1,0:T(8,128)S(1)}, u32[]{:S(2)}, u32[]{:S(2)}) collective-permute-start(f32[5,32,128]{2,1,0:T(8,128)S(1)} %slice.77), channel_id=1, source_target_pairs={{0,8},{1,9},{2,10},{3,11},{4,12},{5,13},{6,14},{7,15},{8,0},{9,1},... | collective-permute-start | bytes 245768 | tf_op jit(solution)/shard_map/ppermute | solution.py:358
  7.5 1.9 %collective-permute-start = (f32[4,32,128]{2,1,0:T(8,128)S(1)}, f32[4,32,128]{2,1,0:T(8,128)S(1)}, u32[]{:S(2)}, u32[]{:S(2)}) collective-permute-start(f32[4,32,128]{2,1,0:T(8,128)S(1)} %get-tuple-element.12), channel_id=1, source_target_pairs={{0,1},{1,0},{2,3},{3,2},{4,5},{5,4},{6,7},{7,6},{8,9},{9,8},{10,11... | collective-permute-start | bytes 196616 | tf_op jit(solution)/shard_map/ppermute | solution.py:358
  7.6 4.5 %collective-permute-start.1 = (f32[4,32,128]{2,1,0:T(8,128)S(1)}, f32[4,32,128]{2,1,0:T(8,128)S(1)}, u32[]{:S(2)}, u32[]{:S(2)}) collective-permute-start(f32[4,32,128]{2,1,0:T(8,128)S(1)} %get-tuple-element.11), channel_id=1, source_target_pairs={{0,2},{1,3},{2,0},{3,1},{4,6},{5,7},{6,4},{7,5},{8,10},{9,11},{10,... | collective-permute-start | bytes 196616 | tf_op jit(solution)/shard_map/ppermute | solution.py:358
  9.2 4.0 %collective-permute-start.2 = (f32[4,32,128]{2,1,0:T(8,128)S(1)}, f32[4,32,128]{2,1,0:T(8,128)S(1)}, u32[]{:S(2)}, u32[]{:S(2)}) collective-permute-start(f32[4,32,128]{2,1,0:T(8,128)S(1)} %get-tuple-element.10), channel_id=1, source_target_pairs={{0,3},{1,2},{2,1},{3,0},{4,7},{5,6},{6,5},{7,4},{8,11},{9,10},{10,... | collective-permute-start | bytes 196616 | tf_op jit(solution)/shard_map/ppermute | solution.py:358
  13.3 7.1 %collective-permute-start.3 = (f32[5,32,128]{2,1,0:T(8,128)S(1)}, f32[5,32,128]{2,1,0:T(8,128)S(1)}, u32[]{:S(2)}, u32[]{:S(2)}) collective-permute-start(f32[5,32,128]{2,1,0:T(8,128)S(1)} %get-tuple-element.25), channel_id=1, source_target_pairs={{0,4},{1,5},{2,6},{3,7},{4,0},{5,1},{6,2},{7,3},{8,12},{9,13},{10,... | collective-permute-start | bytes 245768 | tf_op jit(solution)/shard_map/ppermute | solution.py:358
  14.9 6.2 %collective-permute-start.4 = (f32[5,32,128]{2,1,0:T(8,128)S(1)}, f32[5,32,128]{2,1,0:T(8,128)S(1)}, u32[]{:S(2)}, u32[]{:S(2)}) collective-permute-start(f32[5,32,128]{2,1,0:T(8,128)S(1)} %get-tuple-element.24), channel_id=1, source_target_pairs={{0,12},{1,13},{2,14},{3,15},{4,8},{5,9},{6,10},{7,11},{8,4},{9,5},... | collective-permute-start | bytes 245768 | tf_op jit(solution)/shard_map/ppermute | solution.py:358
  15.5 1.9 %collective-permute-start.6 = (f32[2,32,128]{2,1,0:T(8,128)S(1)}, f32[2,32,128]{2,1,0:T(8,128)S(1)}, u32[]{:S(2)}, u32[]{:S(2)}) collective-permute-start(f32[2,32,128]{2,1,0:T(8,128)S(1)} %get-tuple-element.23), channel_id=1, source_target_pairs={{0,1},{1,0},{2,3},{3,2},{4,5},{5,4},{6,7},{7,6},{8,9},{9,8},{10,11... | collective-permute-start | bytes 98312 | tf_op jit(solution)/shard_map/ppermute | solution.py:358
  15.5 4.0 %collective-permute-start.7 = (f32[2,32,128]{2,1,0:T(8,128)S(1)}, f32[2,32,128]{2,1,0:T(8,128)S(1)}, u32[]{:S(2)}, u32[]{:S(2)}) collective-permute-start(f32[2,32,128]{2,1,0:T(8,128)S(1)} %get-tuple-element.22), channel_id=1, source_target_pairs={{0,2},{1,3},{2,0},{3,1},{4,6},{5,7},{6,4},{7,5},{8,10},{9,11},{10,... | collective-permute-start | bytes 98312 | tf_op jit(solution)/shard_map/ppermute | solution.py:358
  17.0 3.4 %collective-permute-start.8 = (f32[2,32,128]{2,1,0:T(8,128)S(1)}, f32[2,32,128]{2,1,0:T(8,128)S(1)}, u32[]{:S(2)}, u32[]{:S(2)}) collective-permute-start(f32[2,32,128]{2,1,0:T(8,128)S(1)} %concatenate.20), channel_id=1, source_target_pairs={{0,3},{1,2},{2,1},{3,0},{4,7},{5,6},{6,5},{7,4},{8,11},{9,10},{10,... | collective-permute-start | bytes 98312 | tf_op jit(solution)/shard_map/ppermute | solution.py:358

commit v5 on v4

--- a/solution.py
+++ b/solution.py
@@ -11,6 +11,13 @@
 LANES = 128
 PAD = 8
 WIDTHS = 8
+EARLY = (4, 12)
+LATE = tuple(step for step in (4, 8, 12) if step not in EARLY)
+SPAN = len(LATE) + 2
+LOW = {4: 2, 8: 1, 12: 3}
+SPOTS = {LOW[step]: (1 + index, SPAN) for index, step in enumerate(LATE)}
+SPOTS.update({LOW[step]: (4 * SPAN + 5 * index, 1) for index, step in enumerate(EARLY)})
+MEAN_ROWS = [SPAN * group + SPAN - 1 for group in range(4)] + [4 * SPAN + 5 * index + 4 for index in range(len(EARLY))]
 PATH = ((1, 0), (1, 1), (2, 2), (4, 3), (8, 4), (16, 5))
 
 epsilon = 1e-05
@@ -126,7 +133,7 @@
         inner[quad, 0:blocks, :] = pair + later(normal, 4 * quad + 3, blocks, lane, shift)
         partial.append(pair + (row_of(normal, 4 * quad) + row_of(normal, 4 * quad + 3)))
     partial = spread_sum(partial)
-    for row in (3, 7, 11, 15, 20):
+    for row in MEAN_ROWS:
         rows_ref[row] = partial
     for quad in range(ROWS):
         quads[quad, 0:blocks, :] = row_of(normal, 4 * quad) + later(inner, quad, blocks, lane, shift)
@@ -145,7 +152,9 @@
         high = later(halves, 8 + trial // 2, blocks, lane, table_ref[ROWS - 1 + trial])
         place = mine ^ trial
         group, low = place >> 2, place & 3
-        spot = jnp.where(low == 1, ROWS + group, place - (low > 0))
+        spot = group * SPAN
+        for other, (base, scale) in SPOTS.items():
+            spot = jnp.where(low == other, base + scale * group, spot)
         rows_ref[spot] = row_of(halves, trial // 2) + high
     small_lane = lax.broadcasted_iota(jnp.int32, words_ref.shape, 1)
     words = jnp.zeros(words_ref.shape, jnp.int32)
@@ -163,7 +172,7 @@
     return pl.pallas_call(
         local_kernel,
         out_shape=(
-            jax.ShapeDtypeStruct((ROWS + 5, blocks, LANES), jnp.float32),
+            jax.ShapeDtypeStruct((4 * SPAN + 5 * len(EARLY), blocks, LANES), jnp.float32),
             jax.ShapeDtypeStruct((8, LANES), jnp.int32),
         ),
         in_specs=[hbm] * 3,
@@ -282,11 +291,13 @@
 
 
 def cross_kernel(
-    channels, count, finishing, words_ref,
-    own_ref, core_ref, x_ref, both_ref, z1_ref, z3_ref, z2_ref, pc_ref, px_ref, pb_ref, mean_ref,
-    *rest,
+    channels, count, finishing, words_ref, *rest,
 ):
-    blocks = own_ref.shape[1]
+    plane, rest = rest[:4], rest[4:]
+    early, rest = rest[: len(EARLY)], rest[len(EARLY) :]
+    late, rest = rest[: len(LATE)], rest[len(LATE) :]
+    passed, (mean_ref, *rest) = rest[:3], rest[3:]
+    blocks = mean_ref.shape[1]
     lane = lane_index(blocks)
     if finishing:
         out_ref, peaks_ref, spare, *buffers, prefix, split = rest
@@ -302,18 +313,19 @@
     def place(offset, value):
         first[here ^ offset, pl.ds(0, blocks), :] = value
 
-    place(0, own_ref[0])
-    place(1, core_ref[0])
-    place(2, x_ref[0])
-    place(3, both_ref[0])
-    for step, ref in ((1, z1_ref), (3, z3_ref)):
-        for inner in range(4):
-            place(4 * step + inner, ref[inner])
-    for inner, ref in enumerate((z2_ref, pc_ref, px_ref, pb_ref)):
-        place(8 + inner, ref[0])
+    offsets = (0, 2, 1, 3)
+    for group, offset in enumerate(offsets):
+        place(offset, plane[group][0])
+        for index, step in enumerate(LATE):
+            place(step + offset, late[index][group])
+        for index, step in enumerate(EARLY):
+            place(step + offset, passed[group - 1][index] if group else early[index][0])
     mean = mean_ref[0]
     if finishing:
-        mean = mean + z1_ref[4] + z3_ref[4] + pc_ref[1] + px_ref[1] + pb_ref[1]
+        for ref in late:
+            mean = mean + ref[4]
+        for ref in passed:
+            mean = mean + ref[len(EARLY)]
     mean = mean / (channels * count)
     rows = cross_tree(me, mean, words, buffers, spare, blocks, lane)
     if finishing:
@@ -397,22 +409,24 @@
     rows, words = local_rows(filterbank, shift_table, box_widths)
     small = section_count == 4
 
-    across = swapped(rows[4:8], 2)
-    both = swapped(rows[12:16], 3)
-    core = swapped(rows[8:12], 1)
-    z2 = swapped(rows[16:], 8)
-    plane = (rows, core, across, both)
-    mean = sum(part[3:4] for part in plane)
-    z1 = swapped(jnp.concatenate([part[1:2] for part in plane] + [mean], axis=0), 4)
-    z3 = swapped(jnp.concatenate([part[2:3] for part in plane] + [mean], axis=0), 12)
+    early = [swapped(rows[4 * SPAN + 5 * index : 4 * SPAN + 5 * index + 5], step) for index, step in enumerate(EARLY)]
+    plane = [rows] + [
+        swapped(rows[SPAN * group : SPAN * (group + 1)], offset) for group, offset in ((1, 2), (2, 1), (3, 3))
+    ]
+    mean = sum(part[SPAN - 1 : SPAN] for part in plane)
+    late = [
+        swapped(jnp.concatenate([part[1 + index : 2 + index] for part in plane] + [mean], axis=0), step)
+        for index, step in enumerate(LATE)
+    ]
+    column = sum(part[4:] for part in early)
     passed = [
-        swapped(jnp.concatenate([z2[place : place + 1], z2[4:]], axis=0), offset)
-        for offset, place in ((1, 2), (2, 1), (3, 3))
+        swapped(jnp.concatenate([part[group : group + 1] for part in early] + [column], axis=0), offset)
+        for group, offset in ((1, 2), (2, 1), (3, 3))
     ]
-    mean = mean + z2[4:]
-    arrived = [z1, z3, z2, *passed]
+    mean = mean + column
+    arrived = [*plane, *early, *late, *passed]
     if not small:
-        mean = lax.psum(rows[3:4], "chan")
+        mean = lax.psum(rows[SPAN - 1 : SPAN], "chan")
 
     vmem = pl.BlockSpec(memory_space=pltpu.VMEM)
     params = pltpu.CompilerParams(vmem_limit_bytes=32 << 20)
@@ -421,7 +435,7 @@
         out_shape=final_shapes(blocks)
         if small
         else jax.ShapeDtypeStruct((ROWS, blocks, LANES), jnp.float32),
-        in_specs=[vmem] * 12,
+        in_specs=[vmem] * (len(arrived) + 2),
         out_specs=(vmem, vmem) if small else vmem,
         scratch_shapes=[
             *[row_scratch(blocks)] * 6,
@@ -430,7 +444,7 @@
         compiler_params=params,
         name="cross_tree",
     )
-    result = call(words, *plane, *arrived, mean)
+    result = call(words, *arrived, mean)
     if small:
         return tuple(result)
     me = lax.axis_index("chan")

time: 24 us -> 22.8 us (0.950)
  waiting for transfers between devices: 7.57 us -> 6.11 us
  starting transfers between devices: 10.1 us -> 10.4 us
    ppermute x9, waiting for transfers between devices: 7.57 us -> 6.11 us  [swapped(): lax.ppermute(block, 'chan', [(device, device ^ distance) for device in ra...]
    ppermute x9, starting transfers between devices: 10.1 us -> 10.4 us  [swapped(): lax.ppermute(block, 'chan', [(device, device ^ distance) for device in ra...]
  transfers between devices with their start and end apart: 9 -> 9, of which waited for: 5 -> 4; matrix products, arithmetic and copies ran while one was open for 0% -> 0% of each run, Pallas kernels for 0% -> 0%
where the time goes in v5:
time: 22.8 us; the launch traced here: 22.7 us
  starting transfers between devices  10.4 us (46%)
  waiting for transfers between devices  6.11 us (27%)
  Pallas kernels  5.42 us (24%)
  between operations  0.71 us (3%)
    ppermute x9, starting transfers between devices, swapped(): lax.ppermute(block, 'chan', [(device, device ^ distance) for device in ra...  10.4 us
    ppermute x9, waiting for transfers between devices, swapped(): lax.ppermute(block, 'chan', [(device, device ^ distance) for device in ra...  6.11 us
    pallas_call x1, Pallas kernels, local_rows(): pl.pallas_call(local_kernel, out_shape=(jax.ShapeDtypeStruct((4 * SPAN +...  2.75 us
    pallas_call x1, Pallas kernels, shards(): result = call(words, *arrived, mean)  2.67 us
  transfers between devices with their start and end apart: 9, of which 4 were waited for; matrix products, arithmetic and copies ran while one was open for 0% of the time, Pallas kernels for 0%

profile of v5, /device:TPU:0, one launch (start us, length us, event | category | flops | bytes accessed | tf_op | source)
XLA Modules:
  0.0 22.7 jit_solution(15196560063271272772)
XLA Ops:
  0.6 2.8 %local_tree.1 = (f32[22,32,128]{2,1,0:T(8,128)S(1)}, s32[8,128]{1,0:T(8,128)S(1)}) custom-call(s32[511]{0:T(512)} %table_hbm.1, s32[8]{0:T(128)} %width_hbm.1, bf16[64,4096]{1,0:T(8,128)(2,1)} %x_hbm.1), custom_call_target="tpu_custom_call" | custom-call | tf_op jit(solution)/shard_map/local_tree/pallas_call | solution.py:172
  3.4 5.1 %collective-permute-start.4 = (f32[5,32,128]{2,1,0:T(8,128)S(1)}, f32[5,32,128]{2,1,0:T(8,128)S(1)}, u32[]{:S(2)}, u32[]{:S(2)}) collective-permute-start(f32[5,32,128]{2,1,0:T(8,128)S(1)} %get-tuple-element.10), channel_id=1, source_target_pairs={{0,12},{1,13},{2,14},{3,15},{4,8},{5,9},{6,10},{7,11},{8,4},{9,5},... | collective-permute-start | bytes 245768 | tf_op jit(solution)/shard_map/ppermute | solution.py:370
  8.5 0.0 collective-permute-start.3
  8.5 0.7 %collective-permute-start.2 = (f32[3,32,128]{2,1,0:T(8,128)S(1)}, f32[3,32,128]{2,1,0:T(8,128)S(1)}, u32[]{:S(2)}, u32[]{:S(2)}) collective-permute-start(f32[3,32,128]{2,1,0:T(8,128)S(1)} %get-tuple-element.12), channel_id=1, source_target_pairs={{0,3},{1,2},{2,1},{3,0},{4,7},{5,6},{6,5},{7,4},{8,11},{9,10},{10,... | collective-permute-start | bytes 147464 | tf_op jit(solution)/shard_map/ppermute | solution.py:370
  9.3 1.0 %collective-permute-start.1 = (f32[3,32,128]{2,1,0:T(8,128)S(1)}, f32[3,32,128]{2,1,0:T(8,128)S(1)}, u32[]{:S(2)}, u32[]{:S(2)}) collective-permute-start(f32[3,32,128]{2,1,0:T(8,128)S(1)} %get-tuple-element.13), channel_id=1, source_target_pairs={{0,1},{1,0},{2,3},{3,2},{4,5},{5,4},{6,7},{7,6},{8,9},{9,8},{10,11... | collective-permute-start | bytes 147464 | tf_op jit(solution)/shard_map/ppermute | solution.py:370
  10.2 0.5 %collective-permute-start = (f32[3,32,128]{2,1,0:T(8,128)S(1)}, f32[3,32,128]{2,1,0:T(8,128)S(1)}, u32[]{:S(2)}, u32[]{:S(2)}) collective-permute-start(f32[3,32,128]{2,1,0:T(8,128)S(1)} %get-tuple-element.14), channel_id=1, source_target_pairs={{0,2},{1,3},{2,0},{3,1},{4,6},{5,7},{6,4},{7,5},{8,10},{9,11},{10,... | collective-permute-start | bytes 147464 | tf_op jit(solution)/shard_map/ppermute | solution.py:370
  10.8 1.9 %collective-permute-done.2.rest_3_ = f32[3,32,128]{2,1,0:T(8,128)S(1)} collective-permute-done((f32[3,32,128]{2,1,0:T(8,128)S(1)}, f32[3,32,128]{2,1,0:T(8,128)S(1)}, u32[]{:S(2)}, u32[]{:S(2)}) %collective-permute-start.2) | collective-permute-done | bytes 49184 | tf_op jit(solution)/shard_map/ppermute | solution.py:370
  12.6 0.0 collective-permute-done.1.rest_2_
  12.6 1.7 %collective-permute-done.rest_1_ = f32[3,32,128]{2,1,0:T(8,128)S(1)} collective-permute-done((f32[3,32,128]{2,1,0:T(8,128)S(1)}, f32[3,32,128]{2,1,0:T(8,128)S(1)}, u32[]{:S(2)}, u32[]{:S(2)}) %collective-permute-start) | collective-permute-done | bytes 49184 | tf_op jit(solution)/shard_map/ppermute | solution.py:370
  14.3 0.0 collective-permute-done.4.rest_5_
  14.3 0.0 collective-permute-done.3.rest_4_
  14.4 0.8 %collective-permute-start.5 = (f32[5,32,128]{2,1,0:T(8,128)S(1)}, f32[5,32,128]{2,1,0:T(8,128)S(1)}, u32[]{:S(2)}, u32[]{:S(2)}) collective-permute-start(f32[5,32,128]{2,1,0:T(8,128)S(1)} %constant_dynamic-update-slice_fusion), channel_id=1, source_target_pairs={{0,8},{1,9},{2,10},{3,11},{4,12},{5,13},{6,14},{7,15},{8,0},{9,1},... | collective-permute-start | bytes 245768 | tf_op jit(solution)/shard_map/ppermute | solution.py:370
  15.2 0.1 collective-permute-start.8
  15.3 0.6 %collective-permute-start.7 = (f32[3,32,128]{2,1,0:T(8,128)S(1)}, f32[3,32,128]{2,1,0:T(8,128)S(1)}, u32[]{:S(2)}, u32[]{:S(2)}) collective-permute-start(f32[3,32,128]{2,1,0:T(8,128)S(1)} %get-tuple-element.26), channel_id=1, source_target_pairs={{0,1},{1,0},{2,3},{3,2},{4,5},{5,4},{6,7},{7,6},{8,9},{9,8},{10,11... | collective-permute-start | bytes 147464 | tf_op jit(solution)/shard_map/ppermute | solution.py:370
  15.9 1.5 %collective-permute-start.6 = (f32[3,32,128]{2,1,0:T(8,128)S(1)}, f32[3,32,128]{2,1,0:T(8,128)S(1)}, u32[]{:S(2)}, u32[]{:S(2)}) collective-permute-start(f32[3,32,128]{2,1,0:T(8,128)S(1)} %get-tuple-element.27), channel_id=1, source_target_pairs={{0,2},{1,3},{2,0},{3,1},{4,6},{5,7},{6,4},{7,5},{8,10},{9,11},{10,... | collective-permute-start | bytes 147464 | tf_op jit(solution)/shard_map/ppermute | solution.py:370
  17.4 1.4 %collective-permute-done.8.rest_9_ = f32[3,32,128]{2,1,0:T(8,128)S(1)} collective-permute-done((f32[3,32,128]{2,1,0:T(8,128)S(1)}, f32[3,32,128]{2,1,0:T(8,128)S(1)}, u32[]{:S(2)}, u32[]{:S(2)}) %collective-permute-start.8) | collective-permute-done | bytes 49184 | tf_op jit(solution)/shard_map/ppermute | solution.py:370
  18.8 0.0 collective-permute-done.7.rest_8_
  18.8 1.2 %collective-permute-done.6.rest_7_ = f32[3,32,128]{2,1,0:T(8,128)S(1)} collective-permute-done((f32[3,32,128]{2,1,0:T(8,128)S(1)}, f32[3,32,128]{2,1,0:T(8,128)S(1)}, u32[]{:S(2)}, u32[]{:S(2)}) %collective-permute-start.6) | collective-permute-done | bytes 49184 | tf_op jit(solution)/shard_map/ppermute | solution.py:370
  20.0 0.0 collective-permute-done.5.rest_6_
  20.0 2.7 %cross_tree.1 = (bf16[16,4096]{1,0:T(8,128)(2,1)}, f32[8,16]{1,0:T(8,128)}) custom-call(s32[8,128]{1,0:T(8,128)S(1)} %get-tuple-element.4.words_ref, f32[22,32,128]{2,1,0:T(8,128)S(1)} %get-tuple-element.5.rest_0_, f32[3,32,128]{2,1,0:T(8,128)S(1)} %collective-permute-done.rest_1_, f32[3,32,128]{2,1,0:T(8,128)S(1)} %collective-permute-done.1.rest_2_, ...), custom_call_target="tpu_custom_call" | custom-call | tf_op jit(solution)/shard_map/cross_tree/pallas_call | solution.py:447
  (8 shorter events, 0.1 us)
Async XLA Ops:
  3.4 10.9 %collective-permute-start.4 = (f32[5,32,128]{2,1,0:T(8,128)S(1)}, f32[5,32,128]{2,1,0:T(8,128)S(1)}, u32[]{:S(2)}, u32[]{:S(2)}) collective-permute-start(f32[5,32,128]{2,1,0:T(8,128)S(1)} %get-tuple-element.10), channel_id=1, source_target_pairs={{0,12},{1,13},{2,14},{3,15},{4,8},{5,9},{6,10},{7,11},{8,4},{9,5},... | collective-permute-start | bytes 245768 | tf_op jit(solution)/shard_map/ppermute | solution.py:370
  8.5 5.8 %collective-permute-start.3 = (f32[5,32,128]{2,1,0:T(8,128)S(1)}, f32[5,32,128]{2,1,0:T(8,128)S(1)}, u32[]{:S(2)}, u32[]{:S(2)}) collective-permute-start(f32[5,32,128]{2,1,0:T(8,128)S(1)} %get-tuple-element.11), channel_id=1, source_target_pairs={{0,4},{1,5},{2,6},{3,7},{4,0},{5,1},{6,2},{7,3},{8,12},{9,13},{10,... | collective-permute-start | bytes 245768 | tf_op jit(solution)/shard_map/ppermute | solution.py:370
  8.5 4.1 %collective-permute-start.2 = (f32[3,32,128]{2,1,0:T(8,128)S(1)}, f32[3,32,128]{2,1,0:T(8,128)S(1)}, u32[]{:S(2)}, u32[]{:S(2)}) collective-permute-start(f32[3,32,128]{2,1,0:T(8,128)S(1)} %get-tuple-element.12), channel_id=1, source_target_pairs={{0,3},{1,2},{2,1},{3,0},{4,7},{5,6},{6,5},{7,4},{8,11},{9,10},{10,... | collective-permute-start | bytes 147464 | tf_op jit(solution)/shard_map/ppermute | solution.py:370
  9.3 3.3 %collective-permute-start.1 = (f32[3,32,128]{2,1,0:T(8,128)S(1)}, f32[3,32,128]{2,1,0:T(8,128)S(1)}, u32[]{:S(2)}, u32[]{:S(2)}) collective-permute-start(f32[3,32,128]{2,1,0:T(8,128)S(1)} %get-tuple-element.13), channel_id=1, source_target_pairs={{0,1},{1,0},{2,3},{3,2},{4,5},{5,4},{6,7},{7,6},{8,9},{9,8},{10,11... | collective-permute-start | bytes 147464 | tf_op jit(solution)/shard_map/ppermute | solution.py:370
  10.2 4.1 %collective-permute-start = (f32[3,32,128]{2,1,0:T(8,128)S(1)}, f32[3,32,128]{2,1,0:T(8,128)S(1)}, u32[]{:S(2)}, u32[]{:S(2)}) collective-permute-start(f32[3,32,128]{2,1,0:T(8,128)S(1)} %get-tuple-element.14), channel_id=1, source_target_pairs={{0,2},{1,3},{2,0},{3,1},{4,6},{5,7},{6,4},{7,5},{8,10},{9,11},{10,... | collective-permute-start | bytes 147464 | tf_op jit(solution)/shard_map/ppermute | solution.py:370
  14.4 5.6 %collective-permute-start.5 = (f32[5,32,128]{2,1,0:T(8,128)S(1)}, f32[5,32,128]{2,1,0:T(8,128)S(1)}, u32[]{:S(2)}, u32[]{:S(2)}) collective-permute-start(f32[5,32,128]{2,1,0:T(8,128)S(1)} %constant_dynamic-update-slice_fusion), channel_id=1, source_target_pairs={{0,8},{1,9},{2,10},{3,11},{4,12},{5,13},{6,14},{7,15},{8,0},{9,1},... | collective-permute-start | bytes 245768 | tf_op jit(solution)/shard_map/ppermute | solution.py:370
  15.2 3.6 %collective-permute-start.8 = (f32[3,32,128]{2,1,0:T(8,128)S(1)}, f32[3,32,128]{2,1,0:T(8,128)S(1)}, u32[]{:S(2)}, u32[]{:S(2)}) collective-permute-start(f32[3,32,128]{2,1,0:T(8,128)S(1)} %get-tuple-element.25), channel_id=1, source_target_pairs={{0,3},{1,2},{2,1},{3,0},{4,7},{5,6},{6,5},{7,4},{8,11},{9,10},{10,... | collective-permute-start | bytes 147464 | tf_op jit(solution)/shard_map/ppermute | solution.py:370
  15.3 3.5 %collective-permute-start.7 = (f32[3,32,128]{2,1,0:T(8,128)S(1)}, f32[3,32,128]{2,1,0:T(8,128)S(1)}, u32[]{:S(2)}, u32[]{:S(2)}) collective-permute-start(f32[3,32,128]{2,1,0:T(8,128)S(1)} %get-tuple-element.26), channel_id=1, source_target_pairs={{0,1},{1,0},{2,3},{3,2},{4,5},{5,4},{6,7},{7,6},{8,9},{9,8},{10,11... | collective-permute-start | bytes 147464 | tf_op jit(solution)/shard_map/ppermute | solution.py:370
  15.9 4.1 %collective-permute-start.6 = (f32[3,32,128]{2,1,0:T(8,128)S(1)}, f32[3,32,128]{2,1,0:T(8,128)S(1)}, u32[]{:S(2)}, u32[]{:S(2)}) collective-permute-start(f32[3,32,128]{2,1,0:T(8,128)S(1)} %get-tuple-element.27), channel_id=1, source_target_pairs={{0,2},{1,3},{2,0},{3,1},{4,6},{5,7},{6,4},{7,5},{8,10},{9,11},{10,... | collective-permute-start | bytes 147464 | tf_op jit(solution)/shard_map/ppermute | solution.py:370

commit v6 on v5

--- a/solution.py
+++ b/solution.py
@@ -231,35 +231,26 @@
     return buffers[-1]
 
 
-def finish(rows, widths, out_ref, peaks_ref, prefix, split):
+def finish(rows, widths, out_ref, peaks_ref, values, prefix, split):
     stride = rows.shape[1]
     blocks = stride - PAD
     length = blocks * LANES
     lane = lax.broadcasted_iota(jnp.int32, (ROWS, LANES), 1)
     flat = rows.reshape(ROWS * stride, LANES)
 
-    total = jnp.zeros((ROWS, LANES), jnp.float32)
+    total = []
     for block in range(blocks):
         value = jnp.concatenate(
             [flat[pl.ds(block + 8 * half * stride, 8, stride=stride), :] for half in range(2)], axis=0
         )
-        prefix[2 + block] = value
-        total = total + value
-    centre = jnp.sum(total, axis=1, keepdims=True) / length
+        values[block] = value
+        high = value.astype(jnp.bfloat16)
+        rest = (value - high.astype(jnp.float32)).astype(jnp.bfloat16)
+        split[pl.ds(block * ROWS, ROWS), pl.ds(0, LANES)] = high
+        split[pl.ds(block * ROWS, ROWS), pl.ds(LANES, LANES)] = rest
+        total.append(value)
+    centre = jnp.sum(spread_sum(total), axis=1, keepdims=True) / length
     centre = jnp.broadcast_to(centre, (ROWS, LANES))
-    total = jnp.zeros((ROWS, LANES), jnp.float32)
-    for block in range(blocks):
-        total = total + jnp.square(prefix[2 + block] - centre)
-    spread = jnp.sum(total, axis=1, keepdims=True) / length
-    gain = jnp.broadcast_to(lax.rsqrt(spread + epsilon), (ROWS, LANES))
-    for block in range(blocks):
-        value = (prefix[2 + block] - centre) * gain
-        rounded = value.astype(jnp.bfloat16)
-        out_ref[:, pl.ds(block * LANES, LANES)] = rounded
-        split[pl.ds(block * ROWS, ROWS), pl.ds(0, LANES)] = rounded
-        rest = value - rounded.astype(jnp.float32)
-        split[pl.ds(block * ROWS, ROWS), pl.ds(LANES, LANES)] = rest.astype(jnp.bfloat16)
-
     above = lax.broadcasted_iota(jnp.int32, (2 * LANES, 2 * LANES), 0) & 127
     across = lax.broadcasted_iota(jnp.int32, (2 * LANES, 2 * LANES), 1)
     weights = jnp.where(above <= across, 1.0, 0.0).astype(jnp.bfloat16)
@@ -267,10 +258,18 @@
     carry = jnp.zeros((ROWS, LANES), jnp.float32)
     prefix[0] = carry
     prefix[1] = carry
+    ramp = centre * (lane + 1).astype(jnp.float32)
+    drop = centre * LANES
     for block in range(blocks):
         part = sums[block * ROWS : (block + 1) * ROWS]
-        prefix[2 + block] = part[:, :LANES] + carry
-        carry = carry + part[:, LANES:]
+        prefix[2 + block] = (part[:, :LANES] - ramp) + carry
+        carry = carry + (part[:, LANES:] - drop)
+
+    spread = spread_sum(jnp.square(values[block] - centre) for block in range(blocks))
+    spread = jnp.sum(spread, axis=1, keepdims=True) / length
+    gain = jnp.broadcast_to(lax.rsqrt(spread + epsilon), (ROWS, LANES))
+    for block in range(blocks):
+        out_ref[:, pl.ds(block * LANES, LANES)] = ((values[block] - centre) * gain).astype(jnp.bfloat16)
 
     peaks = jnp.zeros((ROWS, LANES), jnp.float32)
     backs = [2 * LANES - width for width in widths]
@@ -285,7 +284,7 @@
             heres[index] = beyond
     for index, width in enumerate(widths):
         peak = jnp.max(best[index], axis=1, keepdims=True)
-        scale = lax.rsqrt(jnp.full((ROWS, LANES), width, jnp.int32).astype(jnp.float32))
+        scale = gain * lax.rsqrt(jnp.full((ROWS, LANES), width, jnp.int32).astype(jnp.float32))
         peaks = jnp.where(lane == index, peak * scale, peaks)
     peaks_ref[...] = jnp.transpose(peaks)[: len(widths)]
 
@@ -300,7 +299,7 @@
     blocks = mean_ref.shape[1]
     lane = lane_index(blocks)
     if finishing:
-        out_ref, peaks_ref, spare, *buffers, prefix, split = rest
+        out_ref, peaks_ref, spare, *buffers, values, prefix, split = rest
     else:
         series_ref, spare, *buffers = rest
     words = [words_ref[0, index] for index in range(2 + WIDTHS // 4)]
@@ -329,7 +328,7 @@
     mean = mean / (channels * count)
     rows = cross_tree(me, mean, words, buffers, spare, blocks, lane)
     if finishing:
-        finish(rows, unpacked_widths(words), out_ref, peaks_ref, prefix, split)
+        finish(rows, unpacked_widths(words), out_ref, peaks_ref, values, prefix, split)
     else:
         for trial in range(ROWS):
             series_ref[trial] = rows[trial, pl.ds(0, blocks), :]
@@ -353,6 +352,7 @@
 
 def finish_scratch(blocks):
     return [
+        pltpu.VMEM((blocks, ROWS, LANES), jnp.float32),
         pltpu.VMEM((blocks + 2, ROWS, LANES), jnp.float32),
         pltpu.VMEM((blocks * ROWS, 2 * LANES), jnp.bfloat16),
     ]

time: 22.8 us -> 22.6 us (level)
  Pallas kernels: 5.42 us -> 5.19 us
    pallas_call x1, Pallas kernels: 2.67 us -> 2.44 us  [shards(): result = call(words, *arrived, mean)]
where the time goes in v6:
time: 22.6 us; the launch traced here: 22.4 us
  starting transfers between devices  10.4 us (46%)
  waiting for transfers between devices  6.11 us (27%)
  Pallas kernels  5.19 us (23%)
  between operations  0.71 us (3%)
    ppermute x9, starting transfers between devices, swapped(): lax.ppermute(block, 'chan', [(device, device ^ distance) for device in ra...  10.4 us
    ppermute x9, waiting for transfers between devices, swapped(): lax.ppermute(block, 'chan', [(device, device ^ distance) for device in ra...  6.11 us
    pallas_call x1, Pallas kernels, local_rows(): pl.pallas_call(local_kernel, out_shape=(jax.ShapeDtypeStruct((4 * SPAN +...  2.75 us
    pallas_call x1, Pallas kernels, shards(): result = call(words, *arrived, mean)  2.44 us
  transfers between devices with their start and end apart: 9, of which 4 were waited for; matrix products, arithmetic and copies ran while one was open for 0% of the time, Pallas kernels for 0%

profile of v6, /device:TPU:0, one launch (start us, length us, event | category | flops | bytes accessed | tf_op | source)
XLA Modules:
  0.0 22.4 jit_solution(7566503973495362526)
XLA Ops:
  0.6 2.8 %local_tree.1 = (f32[22,32,128]{2,1,0:T(8,128)S(1)}, s32[8,128]{1,0:T(8,128)S(1)}) custom-call(s32[511]{0:T(512)} %table_hbm.1, s32[8]{0:T(128)} %width_hbm.1, bf16[64,4096]{1,0:T(8,128)(2,1)} %x_hbm.1), custom_call_target="tpu_custom_call" | custom-call | tf_op jit(solution)/shard_map/local_tree/pallas_call | solution.py:172
  3.4 5.1 %collective-permute-start.4 = (f32[5,32,128]{2,1,0:T(8,128)S(1)}, f32[5,32,128]{2,1,0:T(8,128)S(1)}, u32[]{:S(2)}, u32[]{:S(2)}) collective-permute-start(f32[5,32,128]{2,1,0:T(8,128)S(1)} %get-tuple-element.10), channel_id=1, source_target_pairs={{0,12},{1,13},{2,14},{3,15},{4,8},{5,9},{6,10},{7,11},{8,4},{9,5},... | collective-permute-start | bytes 245768 | tf_op jit(solution)/shard_map/ppermute | solution.py:370
  8.5 0.0 collective-permute-start.3
  8.5 0.7 %collective-permute-start.2 = (f32[3,32,128]{2,1,0:T(8,128)S(1)}, f32[3,32,128]{2,1,0:T(8,128)S(1)}, u32[]{:S(2)}, u32[]{:S(2)}) collective-permute-start(f32[3,32,128]{2,1,0:T(8,128)S(1)} %get-tuple-element.12), channel_id=1, source_target_pairs={{0,3},{1,2},{2,1},{3,0},{4,7},{5,6},{6,5},{7,4},{8,11},{9,10},{10,... | collective-permute-start | bytes 147464 | tf_op jit(solution)/shard_map/ppermute | solution.py:370
  9.3 1.0 %collective-permute-start.1 = (f32[3,32,128]{2,1,0:T(8,128)S(1)}, f32[3,32,128]{2,1,0:T(8,128)S(1)}, u32[]{:S(2)}, u32[]{:S(2)}) collective-permute-start(f32[3,32,128]{2,1,0:T(8,128)S(1)} %get-tuple-element.13), channel_id=1, source_target_pairs={{0,1},{1,0},{2,3},{3,2},{4,5},{5,4},{6,7},{7,6},{8,9},{9,8},{10,11... | collective-permute-start | bytes 147464 | tf_op jit(solution)/shard_map/ppermute | solution.py:370
  10.2 0.5 %collective-permute-start = (f32[3,32,128]{2,1,0:T(8,128)S(1)}, f32[3,32,128]{2,1,0:T(8,128)S(1)}, u32[]{:S(2)}, u32[]{:S(2)}) collective-permute-start(f32[3,32,128]{2,1,0:T(8,128)S(1)} %get-tuple-element.14), channel_id=1, source_target_pairs={{0,2},{1,3},{2,0},{3,1},{4,6},{5,7},{6,4},{7,5},{8,10},{9,11},{10,... | collective-permute-start | bytes 147464 | tf_op jit(solution)/shard_map/ppermute | solution.py:370
  10.8 1.9 %collective-permute-done.2.rest_3_ = f32[3,32,128]{2,1,0:T(8,128)S(1)} collective-permute-done((f32[3,32,128]{2,1,0:T(8,128)S(1)}, f32[3,32,128]{2,1,0:T(8,128)S(1)}, u32[]{:S(2)}, u32[]{:S(2)}) %collective-permute-start.2) | collective-permute-done | bytes 49184 | tf_op jit(solution)/shard_map/ppermute | solution.py:370
  12.6 0.0 collective-permute-done.1.rest_2_
  12.6 1.7 %collective-permute-done.rest_1_ = f32[3,32,128]{2,1,0:T(8,128)S(1)} collective-permute-done((f32[3,32,128]{2,1,0:T(8,128)S(1)}, f32[3,32,128]{2,1,0:T(8,128)S(1)}, u32[]{:S(2)}, u32[]{:S(2)}) %collective-permute-start) | collective-permute-done | bytes 49184 | tf_op jit(solution)/shard_map/ppermute | solution.py:370
  14.3 0.0 collective-permute-done.4.rest_5_
  14.3 0.0 collective-permute-done.3.rest_4_
  14.4 0.8 %collective-permute-start.5 = (f32[5,32,128]{2,1,0:T(8,128)S(1)}, f32[5,32,128]{2,1,0:T(8,128)S(1)}, u32[]{:S(2)}, u32[]{:S(2)}) collective-permute-start(f32[5,32,128]{2,1,0:T(8,128)S(1)} %constant_dynamic-update-slice_fusion), channel_id=1, source_target_pairs={{0,8},{1,9},{2,10},{3,11},{4,12},{5,13},{6,14},{7,15},{8,0},{9,1},... | collective-permute-start | bytes 245768 | tf_op jit(solution)/shard_map/ppermute | solution.py:370
  15.2 0.1 collective-permute-start.8
  15.3 0.6 %collective-permute-start.7 = (f32[3,32,128]{2,1,0:T(8,128)S(1)}, f32[3,32,128]{2,1,0:T(8,128)S(1)}, u32[]{:S(2)}, u32[]{:S(2)}) collective-permute-start(f32[3,32,128]{2,1,0:T(8,128)S(1)} %get-tuple-element.26), channel_id=1, source_target_pairs={{0,1},{1,0},{2,3},{3,2},{4,5},{5,4},{6,7},{7,6},{8,9},{9,8},{10,11... | collective-permute-start | bytes 147464 | tf_op jit(solution)/shard_map/ppermute | solution.py:370
  15.9 1.5 %collective-permute-start.6 = (f32[3,32,128]{2,1,0:T(8,128)S(1)}, f32[3,32,128]{2,1,0:T(8,128)S(1)}, u32[]{:S(2)}, u32[]{:S(2)}) collective-permute-start(f32[3,32,128]{2,1,0:T(8,128)S(1)} %get-tuple-element.27), channel_id=1, source_target_pairs={{0,2},{1,3},{2,0},{3,1},{4,6},{5,7},{6,4},{7,5},{8,10},{9,11},{10,... | collective-permute-start | bytes 147464 | tf_op jit(solution)/shard_map/ppermute | solution.py:370
  17.4 1.4 %collective-permute-done.8.rest_9_ = f32[3,32,128]{2,1,0:T(8,128)S(1)} collective-permute-done((f32[3,32,128]{2,1,0:T(8,128)S(1)}, f32[3,32,128]{2,1,0:T(8,128)S(1)}, u32[]{:S(2)}, u32[]{:S(2)}) %collective-permute-start.8) | collective-permute-done | bytes 49184 | tf_op jit(solution)/shard_map/ppermute | solution.py:370
  18.8 0.0 collective-permute-done.7.rest_8_
  18.8 1.2 %collective-permute-done.6.rest_7_ = f32[3,32,128]{2,1,0:T(8,128)S(1)} collective-permute-done((f32[3,32,128]{2,1,0:T(8,128)S(1)}, f32[3,32,128]{2,1,0:T(8,128)S(1)}, u32[]{:S(2)}, u32[]{:S(2)}) %collective-permute-start.6) | collective-permute-done | bytes 49184 | tf_op jit(solution)/shard_map/ppermute | solution.py:370
  20.0 0.0 collective-permute-done.5.rest_6_
  20.0 2.4 %cross_tree.1 = (bf16[16,4096]{1,0:T(8,128)(2,1)}, f32[8,16]{1,0:T(8,128)}) custom-call(s32[8,128]{1,0:T(8,128)S(1)} %get-tuple-element.4.words_ref, f32[22,32,128]{2,1,0:T(8,128)S(1)} %get-tuple-element.5.rest_0_, f32[3,32,128]{2,1,0:T(8,128)S(1)} %collective-permute-done.rest_1_, f32[3,32,128]{2,1,0:T(8,128)S(1)} %collective-permute-done.1.rest_2_, ...), custom_call_target="tpu_custom_call" | custom-call | tf_op jit(solution)/shard_map/cross_tree/pallas_call | solution.py:447
  (8 shorter events, 0.1 us)
Async XLA Ops:
  3.4 10.9 %collective-permute-start.4 = (f32[5,32,128]{2,1,0:T(8,128)S(1)}, f32[5,32,128]{2,1,0:T(8,128)S(1)}, u32[]{:S(2)}, u32[]{:S(2)}) collective-permute-start(f32[5,32,128]{2,1,0:T(8,128)S(1)} %get-tuple-element.10), channel_id=1, source_target_pairs={{0,12},{1,13},{2,14},{3,15},{4,8},{5,9},{6,10},{7,11},{8,4},{9,5},... | collective-permute-start | bytes 245768 | tf_op jit(solution)/shard_map/ppermute | solution.py:370
  8.5 5.8 %collective-permute-start.3 = (f32[5,32,128]{2,1,0:T(8,128)S(1)}, f32[5,32,128]{2,1,0:T(8,128)S(1)}, u32[]{:S(2)}, u32[]{:S(2)}) collective-permute-start(f32[5,32,128]{2,1,0:T(8,128)S(1)} %get-tuple-element.11), channel_id=1, source_target_pairs={{0,4},{1,5},{2,6},{3,7},{4,0},{5,1},{6,2},{7,3},{8,12},{9,13},{10,... | collective-permute-start | bytes 245768 | tf_op jit(solution)/shard_map/ppermute | solution.py:370
  8.5 4.1 %collective-permute-start.2 = (f32[3,32,128]{2,1,0:T(8,128)S(1)}, f32[3,32,128]{2,1,0:T(8,128)S(1)}, u32[]{:S(2)}, u32[]{:S(2)}) collective-permute-start(f32[3,32,128]{2,1,0:T(8,128)S(1)} %get-tuple-element.12), channel_id=1, source_target_pairs={{0,3},{1,2},{2,1},{3,0},{4,7},{5,6},{6,5},{7,4},{8,11},{9,10},{10,... | collective-permute-start | bytes 147464 | tf_op jit(solution)/shard_map/ppermute | solution.py:370
  9.3 3.3 %collective-permute-start.1 = (f32[3,32,128]{2,1,0:T(8,128)S(1)}, f32[3,32,128]{2,1,0:T(8,128)S(1)}, u32[]{:S(2)}, u32[]{:S(2)}) collective-permute-start(f32[3,32,128]{2,1,0:T(8,128)S(1)} %get-tuple-element.13), channel_id=1, source_target_pairs={{0,1},{1,0},{2,3},{3,2},{4,5},{5,4},{6,7},{7,6},{8,9},{9,8},{10,11... | collective-permute-start | bytes 147464 | tf_op jit(solution)/shard_map/ppermute | solution.py:370
  10.2 4.1 %collective-permute-start = (f32[3,32,128]{2,1,0:T(8,128)S(1)}, f32[3,32,128]{2,1,0:T(8,128)S(1)}, u32[]{:S(2)}, u32[]{:S(2)}) collective-permute-start(f32[3,32,128]{2,1,0:T(8,128)S(1)} %get-tuple-element.14), channel_id=1, source_target_pairs={{0,2},{1,3},{2,0},{3,1},{4,6},{5,7},{6,4},{7,5},{8,10},{9,11},{10,... | collective-permute-start | bytes 147464 | tf_op jit(solution)/shard_map/ppermute | solution.py:370
  14.4 5.6 %collective-permute-start.5 = (f32[5,32,128]{2,1,0:T(8,128)S(1)}, f32[5,32,128]{2,1,0:T(8,128)S(1)}, u32[]{:S(2)}, u32[]{:S(2)}) collective-permute-start(f32[5,32,128]{2,1,0:T(8,128)S(1)} %constant_dynamic-update-slice_fusion), channel_id=1, source_target_pairs={{0,8},{1,9},{2,10},{3,11},{4,12},{5,13},{6,14},{7,15},{8,0},{9,1},... | collective-permute-start | bytes 245768 | tf_op jit(solution)/shard_map/ppermute | solution.py:370
  15.2 3.6 %collective-permute-start.8 = (f32[3,32,128]{2,1,0:T(8,128)S(1)}, f32[3,32,128]{2,1,0:T(8,128)S(1)}, u32[]{:S(2)}, u32[]{:S(2)}) collective-permute-start(f32[3,32,128]{2,1,0:T(8,128)S(1)} %get-tuple-element.25), channel_id=1, source_target_pairs={{0,3},{1,2},{2,1},{3,0},{4,7},{5,6},{6,5},{7,4},{8,11},{9,10},{10,... | collective-permute-start | bytes 147464 | tf_op jit(solution)/shard_map/ppermute | solution.py:370
  15.3 3.5 %collective-permute-start.7 = (f32[3,32,128]{2,1,0:T(8,128)S(1)}, f32[3,32,128]{2,1,0:T(8,128)S(1)}, u32[]{:S(2)}, u32[]{:S(2)}) collective-permute-start(f32[3,32,128]{2,1,0:T(8,128)S(1)} %get-tuple-element.26), channel_id=1, source_target_pairs={{0,1},{1,0},{2,3},{3,2},{4,5},{5,4},{6,7},{7,6},{8,9},{9,8},{10,11... | collective-permute-start | bytes 147464 | tf_op jit(solution)/shard_map/ppermute | solution.py:370
  15.9 4.1 %collective-permute-start.6 = (f32[3,32,128]{2,1,0:T(8,128)S(1)}, f32[3,32,128]{2,1,0:T(8,128)S(1)}, u32[]{:S(2)}, u32[]{:S(2)}) collective-permute-start(f32[3,32,128]{2,1,0:T(8,128)S(1)} %get-tuple-element.27), channel_id=1, source_target_pairs={{0,2},{1,3},{2,0},{3,1},{4,6},{5,7},{6,4},{7,5},{8,10},{9,11},{10,... | collective-permute-start | bytes 147464 | tf_op jit(solution)/shard_map/ppermute | solution.py:370

commit v7 on v6

--- a/solution.py
+++ b/solution.py
@@ -35,16 +35,18 @@
     return pltpu.roll(jnp.where(lane >= part, here, beyond), (LANES - part) & 127, axis=1)
 
 
-def later(ref, row, blocks, lane, shift):
+def later(ref, blocks, lane, shift):
     whole = shift >> 7
-    here = ref[row, pl.ds(whole, blocks), :]
-    beyond = ref[row, pl.ds(whole + 1, blocks), :]
-    return moved(here, beyond, lane, shift & 127)
-
-
-def clear_tail(ref, rows, blocks):
-    for row in rows:
-        ref[row, blocks : blocks + PAD, :] = jnp.zeros((PAD, LANES), jnp.float32)
+    return moved(ref[pl.ds(whole, blocks), :], ref[pl.ds(whole + 1, blocks), :], lane, shift & 127)
+
+
+def clear_tail(refs, blocks):
+    for ref in refs:
+        ref[blocks : blocks + PAD, :] = jnp.zeros((PAD, LANES), jnp.float32)
+
+
+def rows_of(ref):
+    return [ref.at[row] for row in range(ref.shape[0])]
 
 
 def spread_sum(terms):
@@ -79,7 +81,7 @@
 
 def local_kernel(
     table_hbm, width_hbm, x_hbm, rows_ref, words_ref,
-    table_ref, width_ref, x_ref, normal, inner, quads, eights, sixteens, halves, small_sem, x_sem,
+    table_ref, width_ref, x_ref, normal, small_sem, x_sem, *single,
 ):
     channels, length = x_ref.shape
     blocks = length // LANES
@@ -97,13 +99,12 @@
     width_copy.start()
     lane = lane_index(blocks)
     flat = normal.reshape(channels * stride, LANES)
-    clear_tail(normal, range(3, channels, 4), blocks)
-    clear_tail(inner, range(ROWS), blocks)
-    for ref in (quads, eights, sixteens, halves):
-        clear_tail(ref, range(ROWS), blocks)
-
-    def row_of(ref, row):
-        return ref[row, 0:blocks, :]
+    channel = rows_of(normal)
+    inner, quads, eights, sixteens, halves = [single[ROWS * level : ROWS * (level + 1)] for level in range(5)]
+    clear_tail(channel[3::4] + list(single), blocks)
+
+    def row_of(refs, row):
+        return refs[row][0:blocks, :]
 
     for group in range(groups):
         rows = slice(16 * group, 16 * group + 16)
@@ -129,27 +130,27 @@
     shift = table_ref[0]
     partial = []
     for quad in range(ROWS):
-        pair = row_of(normal, 4 * quad + 1) + row_of(normal, 4 * quad + 2)
-        inner[quad, 0:blocks, :] = pair + later(normal, 4 * quad + 3, blocks, lane, shift)
-        partial.append(pair + (row_of(normal, 4 * quad) + row_of(normal, 4 * quad + 3)))
+        pair = row_of(channel, 4 * quad + 1) + row_of(channel, 4 * quad + 2)
+        inner[quad][0:blocks, :] = pair + later(channel[4 * quad + 3], blocks, lane, shift)
+        partial.append(pair + (row_of(channel, 4 * quad) + row_of(channel, 4 * quad + 3)))
     partial = spread_sum(partial)
     for row in MEAN_ROWS:
         rows_ref[row] = partial
     for quad in range(ROWS):
-        quads[quad, 0:blocks, :] = row_of(normal, 4 * quad) + later(inner, quad, blocks, lane, shift)
+        quads[quad][0:blocks, :] = row_of(channel, 4 * quad) + later(inner[quad], blocks, lane, shift)
     bands, trials = ROWS, 1
     for source, target in ((quads, eights), (eights, sixteens), (sixteens, halves)):
         fresh = 2 * trials
         for trial in range(fresh):
             shift = table_ref[fresh - 1 + trial]
             for band in range(bands // 2):
-                high = later(source, (2 * band + 1) * trials + trial // 2, blocks, lane, shift)
+                high = later(source[(2 * band + 1) * trials + trial // 2], blocks, lane, shift)
                 value = row_of(source, 2 * band * trials + trial // 2) + high
-                target[band * fresh + trial, 0:blocks, :] = value
+                target[band * fresh + trial][0:blocks, :] = value
         bands, trials = bands // 2, fresh
     mine = reverse4(lax.axis_index("chan") & 15)
     for trial in range(ROWS):
-        high = later(halves, 8 + trial // 2, blocks, lane, table_ref[ROWS - 1 + trial])
+        high = later(halves[8 + trial // 2], blocks, lane, table_ref[ROWS - 1 + trial])
         place = mine ^ trial
         group, low = place >> 2, place & 3
         spot = group * SPAN
@@ -182,9 +183,9 @@
             pltpu.SMEM(box_widths.shape, jnp.int32),
             pltpu.VMEM(filterbank.shape, filterbank.dtype),
             pltpu.VMEM((channels, blocks + PAD, LANES), jnp.float32),
-            *[row_scratch(blocks)] * 5,
             pltpu.SemaphoreType.DMA((2,)),
             pltpu.SemaphoreType.DMA((channels // 16,)),
+            *[pltpu.VMEM((blocks + PAD, LANES), jnp.float32)] * 5 * ROWS,
         ],
         compiler_params=pltpu.CompilerParams(vmem_limit_bytes=32 << 20),
         name="local_tree",
@@ -198,10 +199,11 @@
         for trials, spot in PATH[step : step + 2]:
             index = row >> (ROWS // trials).bit_length() - 1
             shifts.append(2 * index + (word >> spot & 1))
-        scratch[step, 0:blocks, :] = value
+        ref = scratch[step // 2]
+        ref[0:blocks, :] = value
         near, far = shifts
-        value = (value + later(scratch, step, blocks, lane, near)) + (
-            later(scratch, step, blocks, lane, far) + later(scratch, step, blocks, lane, near + far)
+        value = (value + later(ref, blocks, lane, near)) + (
+            later(ref, blocks, lane, far) + later(ref, blocks, lane, near + far)
         )
     return value
 
@@ -210,7 +212,7 @@
     row = reverse4(me & 15)
     path, cross = words[0], words[1]
     mean = mean_path(mean, path, spare, blocks, lane, row)
-    spare[ROWS - 1, 0:blocks, :] = mean
+    spare[3][0:blocks, :] = mean
     bands, trials = ROWS, 1
     spot = 0
     for source, target in zip(buffers[:-1], buffers[1:]):
@@ -220,15 +222,14 @@
             spot += 1
             old = trial // 2
             if bands == ROWS:
-                taken = mean + later(spare, ROWS - 1, blocks, lane, shift)
+                taken = mean + later(spare[3], blocks, lane, shift)
             for band in range(bands // 2):
-                high = later(source, (2 * band + 1) * trials + old, blocks, lane, shift)
-                value = source[2 * band * trials + old, 0:blocks, :] + high
+                high = later(source[(2 * band + 1) * trials + old], blocks, lane, shift)
+                value = source[2 * band * trials + old][0:blocks, :] + high
                 if bands == ROWS:
                     value = value - taken
-                target[band * fresh + trial, 0:blocks, :] = value
+                target[band * fresh + trial][0:blocks, :] = value
         bands, trials = bands // 2, fresh
-    return buffers[-1]
 
 
 def finish(rows, widths, out_ref, peaks_ref, values, prefix, split):
@@ -299,13 +300,13 @@
     blocks = mean_ref.shape[1]
     lane = lane_index(blocks)
     if finishing:
-        out_ref, peaks_ref, spare, *buffers, values, prefix, split = rest
+        out_ref, peaks_ref, first, final, *single, values, prefix, split = rest
     else:
-        series_ref, spare, *buffers = rest
+        series_ref, first, final, *single = rest
     words = [words_ref[0, index] for index in range(2 + WIDTHS // 4)]
-    for ref in (spare, *buffers):
-        clear_tail(ref, range(ROWS), blocks)
-    first = buffers[0]
+    spare, single = single[:4], single[4:]
+    buffers = [rows_of(first), single[:ROWS], single[ROWS : 2 * ROWS], single[2 * ROWS :], rows_of(final)]
+    clear_tail([*spare, *buffers[0], *single], blocks)
     me = lax.axis_index("chan")
     here = me & 15
 
@@ -326,12 +327,12 @@
         for ref in passed:
             mean = mean + ref[len(EARLY)]
     mean = mean / (channels * count)
-    rows = cross_tree(me, mean, words, buffers, spare, blocks, lane)
+    cross_tree(me, mean, words, buffers, spare, blocks, lane)
     if finishing:
-        finish(rows, unpacked_widths(words), out_ref, peaks_ref, values, prefix, split)
+        finish(final, unpacked_widths(words), out_ref, peaks_ref, values, prefix, split)
     else:
         for trial in range(ROWS):
-            series_ref[trial] = rows[trial, pl.ds(0, blocks), :]
+            series_ref[trial] = final[trial, pl.ds(0, blocks), :]
 
 
 def unpacked_widths(words):
@@ -438,7 +439,8 @@
         in_specs=[vmem] * (len(arrived) + 2),
         out_specs=(vmem, vmem) if small else vmem,
         scratch_shapes=[
-            *[row_scratch(blocks)] * 6,
+            *[row_scratch(blocks)] * 2,
+            *[pltpu.VMEM((blocks + PAD, LANES), jnp.float32)] * (4 + 3 * ROWS),
             *(finish_scratch(blocks) if small else []),
         ],
         compiler_params=params,

time: 22.6 us -> 22.3 us (0.987)
  Pallas kernels: 5.19 us -> 4.91 us
where the time goes in v7:
time: 22.3 us; the launch traced here: 22.2 us
  starting transfers between devices  10.4 us (47%)
  waiting for transfers between devices  6.11 us (27%)
  Pallas kernels  4.91 us (22%)
  between operations  0.71 us (3%)
    ppermute x9, starting transfers between devices, swapped(): lax.ppermute(block, 'chan', [(device, device ^ distance) for device in ra...  10.4 us
    ppermute x9, waiting for transfers between devices, swapped(): lax.ppermute(block, 'chan', [(device, device ^ distance) for device in ra...  6.11 us
    pallas_call x1, Pallas kernels, local_rows(): pl.pallas_call(local_kernel, out_shape=(jax.ShapeDtypeStruct((4 * SPAN +...  2.57 us
    pallas_call x1, Pallas kernels, shards(): result = call(words, *arrived, mean)  2.34 us
  transfers between devices with their start and end apart: 9, of which 4 were waited for; matrix products, arithmetic and copies ran while one was open for 0% of the time, Pallas kernels for 0%

profile of v7, /device:TPU:0, one launch (start us, length us, event | category | flops | bytes accessed | tf_op | source)
XLA Modules:
  0.0 22.2 jit_solution(14813470834561678322)
XLA Ops:
  0.6 2.6 %local_tree.1 = (f32[22,32,128]{2,1,0:T(8,128)S(1)}, s32[8,128]{1,0:T(8,128)S(1)}) custom-call(s32[511]{0:T(512)} %table_hbm.1, s32[8]{0:T(128)} %width_hbm.1, bf16[64,4096]{1,0:T(8,128)(2,1)} %x_hbm.1), custom_call_target="tpu_custom_call" | custom-call | tf_op jit(solution)/shard_map/local_tree/pallas_call | solution.py:173
  3.2 5.1 %collective-permute-start.4 = (f32[5,32,128]{2,1,0:T(8,128)S(1)}, f32[5,32,128]{2,1,0:T(8,128)S(1)}, u32[]{:S(2)}, u32[]{:S(2)}) collective-permute-start(f32[5,32,128]{2,1,0:T(8,128)S(1)} %get-tuple-element.10), channel_id=1, source_target_pairs={{0,12},{1,13},{2,14},{3,15},{4,8},{5,9},{6,10},{7,11},{8,4},{9,5},... | collective-permute-start | bytes 245768 | tf_op jit(solution)/shard_map/ppermute | solution.py:371
  8.3 0.0 collective-permute-start.3
  8.4 0.7 %collective-permute-start.2 = (f32[3,32,128]{2,1,0:T(8,128)S(1)}, f32[3,32,128]{2,1,0:T(8,128)S(1)}, u32[]{:S(2)}, u32[]{:S(2)}) collective-permute-start(f32[3,32,128]{2,1,0:T(8,128)S(1)} %get-tuple-element.12), channel_id=1, source_target_pairs={{0,3},{1,2},{2,1},{3,0},{4,7},{5,6},{6,5},{7,4},{8,11},{9,10},{10,... | collective-permute-start | bytes 147464 | tf_op jit(solution)/shard_map/ppermute | solution.py:371
  9.1 1.0 %collective-permute-start.1 = (f32[3,32,128]{2,1,0:T(8,128)S(1)}, f32[3,32,128]{2,1,0:T(8,128)S(1)}, u32[]{:S(2)}, u32[]{:S(2)}) collective-permute-start(f32[3,32,128]{2,1,0:T(8,128)S(1)} %get-tuple-element.13), channel_id=1, source_target_pairs={{0,1},{1,0},{2,3},{3,2},{4,5},{5,4},{6,7},{7,6},{8,9},{9,8},{10,11... | collective-permute-start | bytes 147464 | tf_op jit(solution)/shard_map/ppermute | solution.py:371
  10.0 0.5 %collective-permute-start = (f32[3,32,128]{2,1,0:T(8,128)S(1)}, f32[3,32,128]{2,1,0:T(8,128)S(1)}, u32[]{:S(2)}, u32[]{:S(2)}) collective-permute-start(f32[3,32,128]{2,1,0:T(8,128)S(1)} %get-tuple-element.14), channel_id=1, source_target_pairs={{0,2},{1,3},{2,0},{3,1},{4,6},{5,7},{6,4},{7,5},{8,10},{9,11},{10,... | collective-permute-start | bytes 147464 | tf_op jit(solution)/shard_map/ppermute | solution.py:371
  10.6 1.9 %collective-permute-done.2.rest_3_ = f32[3,32,128]{2,1,0:T(8,128)S(1)} collective-permute-done((f32[3,32,128]{2,1,0:T(8,128)S(1)}, f32[3,32,128]{2,1,0:T(8,128)S(1)}, u32[]{:S(2)}, u32[]{:S(2)}) %collective-permute-start.2) | collective-permute-done | bytes 49184 | tf_op jit(solution)/shard_map/ppermute | solution.py:371
  12.4 0.0 collective-permute-done.1.rest_2_
  12.4 1.7 %collective-permute-done.rest_1_ = f32[3,32,128]{2,1,0:T(8,128)S(1)} collective-permute-done((f32[3,32,128]{2,1,0:T(8,128)S(1)}, f32[3,32,128]{2,1,0:T(8,128)S(1)}, u32[]{:S(2)}, u32[]{:S(2)}) %collective-permute-start) | collective-permute-done | bytes 49184 | tf_op jit(solution)/shard_map/ppermute | solution.py:371
  14.1 0.0 collective-permute-done.4.rest_5_
  14.1 0.0 collective-permute-done.3.rest_4_
  14.2 0.8 %collective-permute-start.5 = (f32[5,32,128]{2,1,0:T(8,128)S(1)}, f32[5,32,128]{2,1,0:T(8,128)S(1)}, u32[]{:S(2)}, u32[]{:S(2)}) collective-permute-start(f32[5,32,128]{2,1,0:T(8,128)S(1)} %constant_dynamic-update-slice_fusion), channel_id=1, source_target_pairs={{0,8},{1,9},{2,10},{3,11},{4,12},{5,13},{6,14},{7,15},{8,0},{9,1},... | collective-permute-start | bytes 245768 | tf_op jit(solution)/shard_map/ppermute | solution.py:371
  15.1 0.1 collective-permute-start.8
  15.1 0.6 %collective-permute-start.7 = (f32[3,32,128]{2,1,0:T(8,128)S(1)}, f32[3,32,128]{2,1,0:T(8,128)S(1)}, u32[]{:S(2)}, u32[]{:S(2)}) collective-permute-start(f32[3,32,128]{2,1,0:T(8,128)S(1)} %get-tuple-element.26), channel_id=1, source_target_pairs={{0,1},{1,0},{2,3},{3,2},{4,5},{5,4},{6,7},{7,6},{8,9},{9,8},{10,11... | collective-permute-start | bytes 147464 | tf_op jit(solution)/shard_map/ppermute | solution.py:371
  15.7 1.5 %collective-permute-start.6 = (f32[3,32,128]{2,1,0:T(8,128)S(1)}, f32[3,32,128]{2,1,0:T(8,128)S(1)}, u32[]{:S(2)}, u32[]{:S(2)}) collective-permute-start(f32[3,32,128]{2,1,0:T(8,128)S(1)} %get-tuple-element.27), channel_id=1, source_target_pairs={{0,2},{1,3},{2,0},{3,1},{4,6},{5,7},{6,4},{7,5},{8,10},{9,11},{10,... | collective-permute-start | bytes 147464 | tf_op jit(solution)/shard_map/ppermute | solution.py:371
  17.3 1.4 %collective-permute-done.8.rest_9_ = f32[3,32,128]{2,1,0:T(8,128)S(1)} collective-permute-done((f32[3,32,128]{2,1,0:T(8,128)S(1)}, f32[3,32,128]{2,1,0:T(8,128)S(1)}, u32[]{:S(2)}, u32[]{:S(2)}) %collective-permute-start.8) | collective-permute-done | bytes 49184 | tf_op jit(solution)/shard_map/ppermute | solution.py:371
  18.6 0.0 collective-permute-done.7.rest_8_
  18.6 1.2 %collective-permute-done.6.rest_7_ = f32[3,32,128]{2,1,0:T(8,128)S(1)} collective-permute-done((f32[3,32,128]{2,1,0:T(8,128)S(1)}, f32[3,32,128]{2,1,0:T(8,128)S(1)}, u32[]{:S(2)}, u32[]{:S(2)}) %collective-permute-start.6) | collective-permute-done | bytes 49184 | tf_op jit(solution)/shard_map/ppermute | solution.py:371
  19.8 0.0 collective-permute-done.5.rest_6_
  19.8 2.3 %cross_tree.1 = (bf16[16,4096]{1,0:T(8,128)(2,1)}, f32[8,16]{1,0:T(8,128)}) custom-call(s32[8,128]{1,0:T(8,128)S(1)} %get-tuple-element.4.words_ref, f32[22,32,128]{2,1,0:T(8,128)S(1)} %get-tuple-element.5.rest_0_, f32[3,32,128]{2,1,0:T(8,128)S(1)} %collective-permute-done.rest_1_, f32[3,32,128]{2,1,0:T(8,128)S(1)} %collective-permute-done.1.rest_2_, ...), custom_call_target="tpu_custom_call" | custom-call | tf_op jit(solution)/shard_map/cross_tree/pallas_call | solution.py:449
  (8 shorter events, 0.1 us)
Async XLA Ops:
  3.2 10.9 %collective-permute-start.4 = (f32[5,32,128]{2,1,0:T(8,128)S(1)}, f32[5,32,128]{2,1,0:T(8,128)S(1)}, u32[]{:S(2)}, u32[]{:S(2)}) collective-permute-start(f32[5,32,128]{2,1,0:T(8,128)S(1)} %get-tuple-element.10), channel_id=1, source_target_pairs={{0,12},{1,13},{2,14},{3,15},{4,8},{5,9},{6,10},{7,11},{8,4},{9,5},... | collective-permute-start | bytes 245768 | tf_op jit(solution)/shard_map/ppermute | solution.py:371
  8.3 5.8 %collective-permute-start.3 = (f32[5,32,128]{2,1,0:T(8,128)S(1)}, f32[5,32,128]{2,1,0:T(8,128)S(1)}, u32[]{:S(2)}, u32[]{:S(2)}) collective-permute-start(f32[5,32,128]{2,1,0:T(8,128)S(1)} %get-tuple-element.11), channel_id=1, source_target_pairs={{0,4},{1,5},{2,6},{3,7},{4,0},{5,1},{6,2},{7,3},{8,12},{9,13},{10,... | collective-permute-start | bytes 245768 | tf_op jit(solution)/shard_map/ppermute | solution.py:371
  8.4 4.1 %collective-permute-start.2 = (f32[3,32,128]{2,1,0:T(8,128)S(1)}, f32[3,32,128]{2,1,0:T(8,128)S(1)}, u32[]{:S(2)}, u32[]{:S(2)}) collective-permute-start(f32[3,32,128]{2,1,0:T(8,128)S(1)} %get-tuple-element.12), channel_id=1, source_target_pairs={{0,3},{1,2},{2,1},{3,0},{4,7},{5,6},{6,5},{7,4},{8,11},{9,10},{10,... | collective-permute-start | bytes 147464 | tf_op jit(solution)/shard_map/ppermute | solution.py:371
  9.1 3.3 %collective-permute-start.1 = (f32[3,32,128]{2,1,0:T(8,128)S(1)}, f32[3,32,128]{2,1,0:T(8,128)S(1)}, u32[]{:S(2)}, u32[]{:S(2)}) collective-permute-start(f32[3,32,128]{2,1,0:T(8,128)S(1)} %get-tuple-element.13), channel_id=1, source_target_pairs={{0,1},{1,0},{2,3},{3,2},{4,5},{5,4},{6,7},{7,6},{8,9},{9,8},{10,11... | collective-permute-start | bytes 147464 | tf_op jit(solution)/shard_map/ppermute | solution.py:371
  10.0 4.1 %collective-permute-start = (f32[3,32,128]{2,1,0:T(8,128)S(1)}, f32[3,32,128]{2,1,0:T(8,128)S(1)}, u32[]{:S(2)}, u32[]{:S(2)}) collective-permute-start(f32[3,32,128]{2,1,0:T(8,128)S(1)} %get-tuple-element.14), channel_id=1, source_target_pairs={{0,2},{1,3},{2,0},{3,1},{4,6},{5,7},{6,4},{7,5},{8,10},{9,11},{10,... | collective-permute-start | bytes 147464 | tf_op jit(solution)/shard_map/ppermute | solution.py:371
  14.2 5.6 %collective-permute-start.5 = (f32[5,32,128]{2,1,0:T(8,128)S(1)}, f32[5,32,128]{2,1,0:T(8,128)S(1)}, u32[]{:S(2)}, u32[]{:S(2)}) collective-permute-start(f32[5,32,128]{2,1,0:T(8,128)S(1)} %constant_dynamic-update-slice_fusion), channel_id=1, source_target_pairs={{0,8},{1,9},{2,10},{3,11},{4,12},{5,13},{6,14},{7,15},{8,0},{9,1},... | collective-permute-start | bytes 245768 | tf_op jit(solution)/shard_map/ppermute | solution.py:371
  15.1 3.6 %collective-permute-start.8 = (f32[3,32,128]{2,1,0:T(8,128)S(1)}, f32[3,32,128]{2,1,0:T(8,128)S(1)}, u32[]{:S(2)}, u32[]{:S(2)}) collective-permute-start(f32[3,32,128]{2,1,0:T(8,128)S(1)} %get-tuple-element.25), channel_id=1, source_target_pairs={{0,3},{1,2},{2,1},{3,0},{4,7},{5,6},{6,5},{7,4},{8,11},{9,10},{10,... | collective-permute-start | bytes 147464 | tf_op jit(solution)/shard_map/ppermute | solution.py:371
  15.1 3.5 %collective-permute-start.7 = (f32[3,32,128]{2,1,0:T(8,128)S(1)}, f32[3,32,128]{2,1,0:T(8,128)S(1)}, u32[]{:S(2)}, u32[]{:S(2)}) collective-permute-start(f32[3,32,128]{2,1,0:T(8,128)S(1)} %get-tuple-element.26), channel_id=1, source_target_pairs={{0,1},{1,0},{2,3},{3,2},{4,5},{5,4},{6,7},{7,6},{8,9},{9,8},{10,11... | collective-permute-start | bytes 147464 | tf_op jit(solution)/shard_map/ppermute | solution.py:371
  15.7 4.1 %collective-permute-start.6 = (f32[3,32,128]{2,1,0:T(8,128)S(1)}, f32[3,32,128]{2,1,0:T(8,128)S(1)}, u32[]{:S(2)}, u32[]{:S(2)}) collective-permute-start(f32[3,32,128]{2,1,0:T(8,128)S(1)} %get-tuple-element.27), channel_id=1, source_target_pairs={{0,2},{1,3},{2,0},{3,1},{4,6},{5,7},{6,4},{7,5},{8,10},{9,11},{10,... | collective-permute-start | bytes 147464 | tf_op jit(solution)/shard_map/ppermute | solution.py:371

commit v8 on v7

--- a/solution.py
+++ b/solution.py
@@ -88,15 +88,12 @@
     stride = blocks + PAD
     groups = channels // 16
     copies = [
-        pltpu.make_async_copy(x_hbm.at[pl.ds(16 * group, 16)], x_ref.at[pl.ds(16 * group, 16)], x_sem.at[group])
-        for group in range(groups)
+        pltpu.make_async_copy(x_hbm, x_ref, x_sem),
+        pltpu.make_async_copy(table_hbm, table_ref, small_sem.at[0]),
+        pltpu.make_async_copy(width_hbm, width_ref, small_sem.at[1]),
     ]
     for copy in copies:
         copy.start()
-    table_copy = pltpu.make_async_copy(table_hbm, table_ref, small_sem.at[0])
-    width_copy = pltpu.make_async_copy(width_hbm, width_ref, small_sem.at[1])
-    table_copy.start()
-    width_copy.start()
     lane = lane_index(blocks)
     flat = normal.reshape(channels * stride, LANES)
     channel = rows_of(normal)
@@ -106,13 +103,14 @@
     def row_of(refs, row):
         return refs[row][0:blocks, :]
 
+    for copy in copies:
+        copy.wait()
     for group in range(groups):
         rows = slice(16 * group, 16 * group + 16)
 
         def piece(block):
             return x_ref[rows, block * LANES : (block + 1) * LANES].astype(jnp.float32)
 
-        copies[group].wait()
         total = spread_sum(piece(block) for block in range(blocks))
         centre = jnp.sum(total, axis=1, keepdims=True) / length
         centre = jnp.broadcast_to(centre, (16, LANES))
@@ -124,9 +122,6 @@
             for half in range(2):
                 start = (16 * group + 8 * half) * stride + block
                 flat[pl.ds(start, 8, stride=stride), :] = value[8 * half : 8 * half + 8]
-    table_copy.wait()
-    width_copy.wait()
-
     shift = table_ref[0]
     partial = []
     for quad in range(ROWS):
@@ -184,7 +179,7 @@
             pltpu.VMEM(filterbank.shape, filterbank.dtype),
             pltpu.VMEM((channels, blocks + PAD, LANES), jnp.float32),
             pltpu.SemaphoreType.DMA((2,)),
-            pltpu.SemaphoreType.DMA((channels // 16,)),
+            pltpu.SemaphoreType.DMA,
             *[pltpu.VMEM((blocks + PAD, LANES), jnp.float32)] * 5 * ROWS,
         ],
         compiler_params=pltpu.CompilerParams(vmem_limit_bytes=32 << 20),

time: 22.3 us -> 21.9 us (0.982)
  Pallas kernels: 4.91 us -> 4.47 us
    pallas_call x1, Pallas kernels: 2.57 us -> 2.12 us  [local_rows(): pl.pallas_call(local_kernel, out_shape=(jax.ShapeDtypeStruct((4 * SPAN +...]
where the time goes in v8:
time: 21.9 us; the launch traced here: 21.7 us
  starting transfers between devices  10.4 us (47%)
  waiting for transfers between devices  6.11 us (28%)
  Pallas kernels  4.47 us (20%)
  between operations  0.71 us (3%)
    ppermute x9, starting transfers between devices, swapped(): lax.ppermute(block, 'chan', [(device, device ^ distance) for device in ra...  10.4 us
    ppermute x9, waiting for transfers between devices, swapped(): lax.ppermute(block, 'chan', [(device, device ^ distance) for device in ra...  6.11 us
    pallas_call x1, Pallas kernels, shards(): result = call(words, *arrived, mean)  2.34 us
    pallas_call x1, Pallas kernels, local_rows(): pl.pallas_call(local_kernel, out_shape=(jax.ShapeDtypeStruct((4 * SPAN +...  2.12 us
  transfers between devices with their start and end apart: 9, of which 4 were waited for; matrix products, arithmetic and copies ran while one was open for 0% of the time, Pallas kernels for 0%

profile of v8, /device:TPU:0, one launch (start us, length us, event | category | flops | bytes accessed | tf_op | source)
XLA Modules:
  0.0 21.7 jit_solution(18215194329564157333)
XLA Ops:
  0.6 2.1 %local_tree.1 = (f32[22,32,128]{2,1,0:T(8,128)S(1)}, s32[8,128]{1,0:T(8,128)S(1)}) custom-call(s32[511]{0:T(512)} %table_hbm.1, s32[8]{0:T(128)} %width_hbm.1, bf16[64,4096]{1,0:T(8,128)(2,1)} %x_hbm.1), custom_call_target="tpu_custom_call" | custom-call | tf_op jit(solution)/shard_map/local_tree/pallas_call | solution.py:168
  2.8 5.1 %collective-permute-start.4 = (f32[5,32,128]{2,1,0:T(8,128)S(1)}, f32[5,32,128]{2,1,0:T(8,128)S(1)}, u32[]{:S(2)}, u32[]{:S(2)}) collective-permute-start(f32[5,32,128]{2,1,0:T(8,128)S(1)} %get-tuple-element.10), channel_id=1, source_target_pairs={{0,12},{1,13},{2,14},{3,15},{4,8},{5,9},{6,10},{7,11},{8,4},{9,5},... | collective-permute-start | bytes 245768 | tf_op jit(solution)/shard_map/ppermute | solution.py:366
  7.9 0.0 collective-permute-start.3
  7.9 0.7 %collective-permute-start.2 = (f32[3,32,128]{2,1,0:T(8,128)S(1)}, f32[3,32,128]{2,1,0:T(8,128)S(1)}, u32[]{:S(2)}, u32[]{:S(2)}) collective-permute-start(f32[3,32,128]{2,1,0:T(8,128)S(1)} %get-tuple-element.12), channel_id=1, source_target_pairs={{0,3},{1,2},{2,1},{3,0},{4,7},{5,6},{6,5},{7,4},{8,11},{9,10},{10,... | collective-permute-start | bytes 147464 | tf_op jit(solution)/shard_map/ppermute | solution.py:366
  8.6 1.0 %collective-permute-start.1 = (f32[3,32,128]{2,1,0:T(8,128)S(1)}, f32[3,32,128]{2,1,0:T(8,128)S(1)}, u32[]{:S(2)}, u32[]{:S(2)}) collective-permute-start(f32[3,32,128]{2,1,0:T(8,128)S(1)} %get-tuple-element.13), channel_id=1, source_target_pairs={{0,1},{1,0},{2,3},{3,2},{4,5},{5,4},{6,7},{7,6},{8,9},{9,8},{10,11... | collective-permute-start | bytes 147464 | tf_op jit(solution)/shard_map/ppermute | solution.py:366
  9.6 0.5 %collective-permute-start = (f32[3,32,128]{2,1,0:T(8,128)S(1)}, f32[3,32,128]{2,1,0:T(8,128)S(1)}, u32[]{:S(2)}, u32[]{:S(2)}) collective-permute-start(f32[3,32,128]{2,1,0:T(8,128)S(1)} %get-tuple-element.14), channel_id=1, source_target_pairs={{0,2},{1,3},{2,0},{3,1},{4,6},{5,7},{6,4},{7,5},{8,10},{9,11},{10,... | collective-permute-start | bytes 147464 | tf_op jit(solution)/shard_map/ppermute | solution.py:366
  10.1 1.9 %collective-permute-done.2.rest_3_ = f32[3,32,128]{2,1,0:T(8,128)S(1)} collective-permute-done((f32[3,32,128]{2,1,0:T(8,128)S(1)}, f32[3,32,128]{2,1,0:T(8,128)S(1)}, u32[]{:S(2)}, u32[]{:S(2)}) %collective-permute-start.2) | collective-permute-done | bytes 49184 | tf_op jit(solution)/shard_map/ppermute | solution.py:366
  12.0 0.0 collective-permute-done.1.rest_2_
  12.0 1.7 %collective-permute-done.rest_1_ = f32[3,32,128]{2,1,0:T(8,128)S(1)} collective-permute-done((f32[3,32,128]{2,1,0:T(8,128)S(1)}, f32[3,32,128]{2,1,0:T(8,128)S(1)}, u32[]{:S(2)}, u32[]{:S(2)}) %collective-permute-start) | collective-permute-done | bytes 49184 | tf_op jit(solution)/shard_map/ppermute | solution.py:366
  13.7 0.0 collective-permute-done.4.rest_5_
  13.7 0.0 collective-permute-done.3.rest_4_
  13.8 0.8 %collective-permute-start.5 = (f32[5,32,128]{2,1,0:T(8,128)S(1)}, f32[5,32,128]{2,1,0:T(8,128)S(1)}, u32[]{:S(2)}, u32[]{:S(2)}) collective-permute-start(f32[5,32,128]{2,1,0:T(8,128)S(1)} %constant_dynamic-update-slice_fusion), channel_id=1, source_target_pairs={{0,8},{1,9},{2,10},{3,11},{4,12},{5,13},{6,14},{7,15},{8,0},{9,1},... | collective-permute-start | bytes 245768 | tf_op jit(solution)/shard_map/ppermute | solution.py:366
  14.6 0.1 collective-permute-start.8
  14.7 0.6 %collective-permute-start.7 = (f32[3,32,128]{2,1,0:T(8,128)S(1)}, f32[3,32,128]{2,1,0:T(8,128)S(1)}, u32[]{:S(2)}, u32[]{:S(2)}) collective-permute-start(f32[3,32,128]{2,1,0:T(8,128)S(1)} %get-tuple-element.26), channel_id=1, source_target_pairs={{0,1},{1,0},{2,3},{3,2},{4,5},{5,4},{6,7},{7,6},{8,9},{9,8},{10,11... | collective-permute-start | bytes 147464 | tf_op jit(solution)/shard_map/ppermute | solution.py:366
  15.3 1.5 %collective-permute-start.6 = (f32[3,32,128]{2,1,0:T(8,128)S(1)}, f32[3,32,128]{2,1,0:T(8,128)S(1)}, u32[]{:S(2)}, u32[]{:S(2)}) collective-permute-start(f32[3,32,128]{2,1,0:T(8,128)S(1)} %get-tuple-element.27), channel_id=1, source_target_pairs={{0,2},{1,3},{2,0},{3,1},{4,6},{5,7},{6,4},{7,5},{8,10},{9,11},{10,... | collective-permute-start | bytes 147464 | tf_op jit(solution)/shard_map/ppermute | solution.py:366
  16.8 1.4 %collective-permute-done.8.rest_9_ = f32[3,32,128]{2,1,0:T(8,128)S(1)} collective-permute-done((f32[3,32,128]{2,1,0:T(8,128)S(1)}, f32[3,32,128]{2,1,0:T(8,128)S(1)}, u32[]{:S(2)}, u32[]{:S(2)}) %collective-permute-start.8) | collective-permute-done | bytes 49184 | tf_op jit(solution)/shard_map/ppermute | solution.py:366
  18.2 0.0 collective-permute-done.7.rest_8_
  18.2 1.2 %collective-permute-done.6.rest_7_ = f32[3,32,128]{2,1,0:T(8,128)S(1)} collective-permute-done((f32[3,32,128]{2,1,0:T(8,128)S(1)}, f32[3,32,128]{2,1,0:T(8,128)S(1)}, u32[]{:S(2)}, u32[]{:S(2)}) %collective-permute-start.6) | collective-permute-done | bytes 49184 | tf_op jit(solution)/shard_map/ppermute | solution.py:366
  19.4 0.0 collective-permute-done.5.rest_6_
  19.4 2.3 %cross_tree.1 = (bf16[16,4096]{1,0:T(8,128)(2,1)}, f32[8,16]{1,0:T(8,128)}) custom-call(s32[8,128]{1,0:T(8,128)S(1)} %get-tuple-element.4.words_ref, f32[22,32,128]{2,1,0:T(8,128)S(1)} %get-tuple-element.5.rest_0_, f32[3,32,128]{2,1,0:T(8,128)S(1)} %collective-permute-done.rest_1_, f32[3,32,128]{2,1,0:T(8,128)S(1)} %collective-permute-done.1.rest_2_, ...), custom_call_target="tpu_custom_call" | custom-call | tf_op jit(solution)/shard_map/cross_tree/pallas_call | solution.py:444
  (8 shorter events, 0.1 us)
Async XLA Ops:
  2.8 10.9 %collective-permute-start.4 = (f32[5,32,128]{2,1,0:T(8,128)S(1)}, f32[5,32,128]{2,1,0:T(8,128)S(1)}, u32[]{:S(2)}, u32[]{:S(2)}) collective-permute-start(f32[5,32,128]{2,1,0:T(8,128)S(1)} %get-tuple-element.10), channel_id=1, source_target_pairs={{0,12},{1,13},{2,14},{3,15},{4,8},{5,9},{6,10},{7,11},{8,4},{9,5},... | collective-permute-start | bytes 245768 | tf_op jit(solution)/shard_map/ppermute | solution.py:366
  7.9 5.8 %collective-permute-start.3 = (f32[5,32,128]{2,1,0:T(8,128)S(1)}, f32[5,32,128]{2,1,0:T(8,128)S(1)}, u32[]{:S(2)}, u32[]{:S(2)}) collective-permute-start(f32[5,32,128]{2,1,0:T(8,128)S(1)} %get-tuple-element.11), channel_id=1, source_target_pairs={{0,4},{1,5},{2,6},{3,7},{4,0},{5,1},{6,2},{7,3},{8,12},{9,13},{10,... | collective-permute-start | bytes 245768 | tf_op jit(solution)/shard_map/ppermute | solution.py:366
  7.9 4.1 %collective-permute-start.2 = (f32[3,32,128]{2,1,0:T(8,128)S(1)}, f32[3,32,128]{2,1,0:T(8,128)S(1)}, u32[]{:S(2)}, u32[]{:S(2)}) collective-permute-start(f32[3,32,128]{2,1,0:T(8,128)S(1)} %get-tuple-element.12), channel_id=1, source_target_pairs={{0,3},{1,2},{2,1},{3,0},{4,7},{5,6},{6,5},{7,4},{8,11},{9,10},{10,... | collective-permute-start | bytes 147464 | tf_op jit(solution)/shard_map/ppermute | solution.py:366
  8.6 3.3 %collective-permute-start.1 = (f32[3,32,128]{2,1,0:T(8,128)S(1)}, f32[3,32,128]{2,1,0:T(8,128)S(1)}, u32[]{:S(2)}, u32[]{:S(2)}) collective-permute-start(f32[3,32,128]{2,1,0:T(8,128)S(1)} %get-tuple-element.13), channel_id=1, source_target_pairs={{0,1},{1,0},{2,3},{3,2},{4,5},{5,4},{6,7},{7,6},{8,9},{9,8},{10,11... | collective-permute-start | bytes 147464 | tf_op jit(solution)/shard_map/ppermute | solution.py:366
  9.6 4.1 %collective-permute-start = (f32[3,32,128]{2,1,0:T(8,128)S(1)}, f32[3,32,128]{2,1,0:T(8,128)S(1)}, u32[]{:S(2)}, u32[]{:S(2)}) collective-permute-start(f32[3,32,128]{2,1,0:T(8,128)S(1)} %get-tuple-element.14), channel_id=1, source_target_pairs={{0,2},{1,3},{2,0},{3,1},{4,6},{5,7},{6,4},{7,5},{8,10},{9,11},{10,... | collective-permute-start | bytes 147464 | tf_op jit(solution)/shard_map/ppermute | solution.py:366
  13.8 5.6 %collective-permute-start.5 = (f32[5,32,128]{2,1,0:T(8,128)S(1)}, f32[5,32,128]{2,1,0:T(8,128)S(1)}, u32[]{:S(2)}, u32[]{:S(2)}) collective-permute-start(f32[5,32,128]{2,1,0:T(8,128)S(1)} %constant_dynamic-update-slice_fusion), channel_id=1, source_target_pairs={{0,8},{1,9},{2,10},{3,11},{4,12},{5,13},{6,14},{7,15},{8,0},{9,1},... | collective-permute-start | bytes 245768 | tf_op jit(solution)/shard_map/ppermute | solution.py:366
  14.6 3.6 %collective-permute-start.8 = (f32[3,32,128]{2,1,0:T(8,128)S(1)}, f32[3,32,128]{2,1,0:T(8,128)S(1)}, u32[]{:S(2)}, u32[]{:S(2)}) collective-permute-start(f32[3,32,128]{2,1,0:T(8,128)S(1)} %get-tuple-element.25), channel_id=1, source_target_pairs={{0,3},{1,2},{2,1},{3,0},{4,7},{5,6},{6,5},{7,4},{8,11},{9,10},{10,... | collective-permute-start | bytes 147464 | tf_op jit(solution)/shard_map/ppermute | solution.py:366
  14.7 3.5 %collective-permute-start.7 = (f32[3,32,128]{2,1,0:T(8,128)S(1)}, f32[3,32,128]{2,1,0:T(8,128)S(1)}, u32[]{:S(2)}, u32[]{:S(2)}) collective-permute-start(f32[3,32,128]{2,1,0:T(8,128)S(1)} %get-tuple-element.26), channel_id=1, source_target_pairs={{0,1},{1,0},{2,3},{3,2},{4,5},{5,4},{6,7},{7,6},{8,9},{9,8},{10,11... | collective-permute-start | bytes 147464 | tf_op jit(solution)/shard_map/ppermute | solution.py:366
  15.3 4.1 %collective-permute-start.6 = (f32[3,32,128]{2,1,0:T(8,128)S(1)}, f32[3,32,128]{2,1,0:T(8,128)S(1)}, u32[]{:S(2)}, u32[]{:S(2)}) collective-permute-start(f32[3,32,128]{2,1,0:T(8,128)S(1)} %get-tuple-element.27), channel_id=1, source_target_pairs={{0,2},{1,3},{2,0},{3,1},{4,6},{5,7},{6,4},{7,5},{8,10},{9,11},{10,... | collective-permute-start | bytes 147464 | tf_op jit(solution)/shard_map/ppermute | solution.py:366

commit v9 on v8

--- a/solution.py
+++ b/solution.py
@@ -43,6 +43,10 @@
 def clear_tail(refs, blocks):
     for ref in refs:
         ref[blocks : blocks + PAD, :] = jnp.zeros((PAD, LANES), jnp.float32)
+
+
+def uppers(refs, trials):
+    return [ref for row, ref in enumerate(refs) if row // trials % 2]
 
 
 def rows_of(ref):
@@ -81,7 +85,7 @@
 
 def local_kernel(
     table_hbm, width_hbm, x_hbm, rows_ref, words_ref,
-    table_ref, width_ref, x_ref, normal, small_sem, x_sem, *single,
+    table_ref, width_ref, x_ref, small_sem, x_sem, *single,
 ):
     channels, length = x_ref.shape
     blocks = length // LANES
@@ -95,10 +99,12 @@
     for copy in copies:
         copy.start()
     lane = lane_index(blocks)
-    flat = normal.reshape(channels * stride, LANES)
-    channel = rows_of(normal)
+    normal, single = single[:groups], single[groups:]
+    channel = [ref.at[pl.ds(row * stride, stride), :] for ref in normal for row in range(16)]
     inner, quads, eights, sixteens, halves = [single[ROWS * level : ROWS * (level + 1)] for level in range(5)]
-    clear_tail(channel[3::4] + list(single), blocks)
+    clear_tail(channel[3::4] + list(inner), blocks)
+    for level, refs in enumerate((quads, eights, sixteens, halves)):
+        clear_tail(uppers(refs, 1 << level), blocks)
 
     def row_of(refs, row):
         return refs[row][0:blocks, :]
@@ -120,8 +126,8 @@
         for block in range(blocks):
             value = (piece(block) - centre) * gain
             for half in range(2):
-                start = (16 * group + 8 * half) * stride + block
-                flat[pl.ds(start, 8, stride=stride), :] = value[8 * half : 8 * half + 8]
+                start = 8 * half * stride + block
+                normal[group][pl.ds(start, 8, stride=stride), :] = value[8 * half : 8 * half + 8]
     shift = table_ref[0]
     partial = []
     for quad in range(ROWS):
@@ -177,9 +183,9 @@
             pltpu.SMEM(shift_table.shape, jnp.int32),
             pltpu.SMEM(box_widths.shape, jnp.int32),
             pltpu.VMEM(filterbank.shape, filterbank.dtype),
-            pltpu.VMEM((channels, blocks + PAD, LANES), jnp.float32),
             pltpu.SemaphoreType.DMA((2,)),
             pltpu.SemaphoreType.DMA,
+            *[pltpu.VMEM((16 * (blocks + PAD), LANES), jnp.float32)] * (channels // 16),
             *[pltpu.VMEM((blocks + PAD, LANES), jnp.float32)] * 5 * ROWS,
         ],
         compiler_params=pltpu.CompilerParams(vmem_limit_bytes=32 << 20),
@@ -301,7 +307,9 @@
     words = [words_ref[0, index] for index in range(2 + WIDTHS // 4)]
     spare, single = single[:4], single[4:]
     buffers = [rows_of(first), single[:ROWS], single[ROWS : 2 * ROWS], single[2 * ROWS :], rows_of(final)]
-    clear_tail([*spare, *buffers[0], *single], blocks)
+    clear_tail(spare, blocks)
+    for level, refs in enumerate(buffers[:4]):
+        clear_tail(uppers(refs, 1 << level), blocks)
     me = lax.axis_index("chan")
     here = me & 15
 

time: 21.9 us -> 21.8 us (level)
  no operation moved by 1% of the time
where the time goes in v9:
time: 21.8 us; the launch traced here: 21.7 us
  starting transfers between devices  10.4 us (48%)
  waiting for transfers between devices  6.11 us (28%)
  Pallas kernels  4.43 us (20%)
  between operations  0.71 us (3%)
    ppermute x9, starting transfers between devices, swapped(): lax.ppermute(block, 'chan', [(device, device ^ distance) for device in ra...  10.4 us
    ppermute x9, waiting for transfers between devices, swapped(): lax.ppermute(block, 'chan', [(device, device ^ distance) for device in ra...  6.11 us
    pallas_call x1, Pallas kernels, shards(): result = call(words, *arrived, mean)  2.34 us
    pallas_call x1, Pallas kernels, local_rows(): pl.pallas_call(local_kernel, out_shape=(jax.ShapeDtypeStruct((4 * SPAN +...  2.09 us
  transfers between devices with their start and end apart: 9, of which 4 were waited for; matrix products, arithmetic and copies ran while one was open for 0% of the time, Pallas kernels for 0%

profile of v9, /device:TPU:0, one launch (start us, length us, event | category | flops | bytes accessed | tf_op | source)
XLA Modules:
  0.0 21.7 jit_solution(18427470740302152596)
XLA Ops:
  0.6 2.1 %local_tree.1 = (f32[22,32,128]{2,1,0:T(8,128)S(1)}, s32[8,128]{1,0:T(8,128)S(1)}) custom-call(s32[511]{0:T(512)} %table_hbm.1, s32[8]{0:T(128)} %width_hbm.1, bf16[64,4096]{1,0:T(8,128)(2,1)} %x_hbm.1), custom_call_target="tpu_custom_call" | custom-call | tf_op jit(solution)/shard_map/local_tree/pallas_call | solution.py:174
  2.7 5.1 %collective-permute-start.4 = (f32[5,32,128]{2,1,0:T(8,128)S(1)}, f32[5,32,128]{2,1,0:T(8,128)S(1)}, u32[]{:S(2)}, u32[]{:S(2)}) collective-permute-start(f32[5,32,128]{2,1,0:T(8,128)S(1)} %get-tuple-element.10), channel_id=1, source_target_pairs={{0,12},{1,13},{2,14},{3,15},{4,8},{5,9},{6,10},{7,11},{8,4},{9,5},... | collective-permute-start | bytes 245768 | tf_op jit(solution)/shard_map/ppermute | solution.py:374
  7.9 0.0 collective-permute-start.3
  7.9 0.7 %collective-permute-start.2 = (f32[3,32,128]{2,1,0:T(8,128)S(1)}, f32[3,32,128]{2,1,0:T(8,128)S(1)}, u32[]{:S(2)}, u32[]{:S(2)}) collective-permute-start(f32[3,32,128]{2,1,0:T(8,128)S(1)} %get-tuple-element.12), channel_id=1, source_target_pairs={{0,3},{1,2},{2,1},{3,0},{4,7},{5,6},{6,5},{7,4},{8,11},{9,10},{10,... | collective-permute-start | bytes 147464 | tf_op jit(solution)/shard_map/ppermute | solution.py:374
  8.6 1.0 %collective-permute-start.1 = (f32[3,32,128]{2,1,0:T(8,128)S(1)}, f32[3,32,128]{2,1,0:T(8,128)S(1)}, u32[]{:S(2)}, u32[]{:S(2)}) collective-permute-start(f32[3,32,128]{2,1,0:T(8,128)S(1)} %get-tuple-element.13), channel_id=1, source_target_pairs={{0,1},{1,0},{2,3},{3,2},{4,5},{5,4},{6,7},{7,6},{8,9},{9,8},{10,11... | collective-permute-start | bytes 147464 | tf_op jit(solution)/shard_map/ppermute | solution.py:374
  9.6 0.5 %collective-permute-start = (f32[3,32,128]{2,1,0:T(8,128)S(1)}, f32[3,32,128]{2,1,0:T(8,128)S(1)}, u32[]{:S(2)}, u32[]{:S(2)}) collective-permute-start(f32[3,32,128]{2,1,0:T(8,128)S(1)} %get-tuple-element.14), channel_id=1, source_target_pairs={{0,2},{1,3},{2,0},{3,1},{4,6},{5,7},{6,4},{7,5},{8,10},{9,11},{10,... | collective-permute-start | bytes 147464 | tf_op jit(solution)/shard_map/ppermute | solution.py:374
  10.1 1.9 %collective-permute-done.2.rest_3_ = f32[3,32,128]{2,1,0:T(8,128)S(1)} collective-permute-done((f32[3,32,128]{2,1,0:T(8,128)S(1)}, f32[3,32,128]{2,1,0:T(8,128)S(1)}, u32[]{:S(2)}, u32[]{:S(2)}) %collective-permute-start.2) | collective-permute-done | bytes 49184 | tf_op jit(solution)/shard_map/ppermute | solution.py:374
  11.9 0.0 collective-permute-done.1.rest_2_
  11.9 1.7 %collective-permute-done.rest_1_ = f32[3,32,128]{2,1,0:T(8,128)S(1)} collective-permute-done((f32[3,32,128]{2,1,0:T(8,128)S(1)}, f32[3,32,128]{2,1,0:T(8,128)S(1)}, u32[]{:S(2)}, u32[]{:S(2)}) %collective-permute-start) | collective-permute-done | bytes 49184 | tf_op jit(solution)/shard_map/ppermute | solution.py:374
  13.6 0.0 collective-permute-done.4.rest_5_
  13.6 0.0 collective-permute-done.3.rest_4_
  13.7 0.8 %collective-permute-start.5 = (f32[5,32,128]{2,1,0:T(8,128)S(1)}, f32[5,32,128]{2,1,0:T(8,128)S(1)}, u32[]{:S(2)}, u32[]{:S(2)}) collective-permute-start(f32[5,32,128]{2,1,0:T(8,128)S(1)} %constant_dynamic-update-slice_fusion), channel_id=1, source_target_pairs={{0,8},{1,9},{2,10},{3,11},{4,12},{5,13},{6,14},{7,15},{8,0},{9,1},... | collective-permute-start | bytes 245768 | tf_op jit(solution)/shard_map/ppermute | solution.py:374
  14.6 0.1 collective-permute-start.8
  14.7 0.6 %collective-permute-start.7 = (f32[3,32,128]{2,1,0:T(8,128)S(1)}, f32[3,32,128]{2,1,0:T(8,128)S(1)}, u32[]{:S(2)}, u32[]{:S(2)}) collective-permute-start(f32[3,32,128]{2,1,0:T(8,128)S(1)} %get-tuple-element.26), channel_id=1, source_target_pairs={{0,1},{1,0},{2,3},{3,2},{4,5},{5,4},{6,7},{7,6},{8,9},{9,8},{10,11... | collective-permute-start | bytes 147464 | tf_op jit(solution)/shard_map/ppermute | solution.py:374
  15.2 1.5 %collective-permute-start.6 = (f32[3,32,128]{2,1,0:T(8,128)S(1)}, f32[3,32,128]{2,1,0:T(8,128)S(1)}, u32[]{:S(2)}, u32[]{:S(2)}) collective-permute-start(f32[3,32,128]{2,1,0:T(8,128)S(1)} %get-tuple-element.27), channel_id=1, source_target_pairs={{0,2},{1,3},{2,0},{3,1},{4,6},{5,7},{6,4},{7,5},{8,10},{9,11},{10,... | collective-permute-start | bytes 147464 | tf_op jit(solution)/shard_map/ppermute | solution.py:374
  16.8 1.4 %collective-permute-done.8.rest_9_ = f32[3,32,128]{2,1,0:T(8,128)S(1)} collective-permute-done((f32[3,32,128]{2,1,0:T(8,128)S(1)}, f32[3,32,128]{2,1,0:T(8,128)S(1)}, u32[]{:S(2)}, u32[]{:S(2)}) %collective-permute-start.8) | collective-permute-done | bytes 49184 | tf_op jit(solution)/shard_map/ppermute | solution.py:374
  18.2 0.0 collective-permute-done.7.rest_8_
  18.2 1.2 %collective-permute-done.6.rest_7_ = f32[3,32,128]{2,1,0:T(8,128)S(1)} collective-permute-done((f32[3,32,128]{2,1,0:T(8,128)S(1)}, f32[3,32,128]{2,1,0:T(8,128)S(1)}, u32[]{:S(2)}, u32[]{:S(2)}) %collective-permute-start.6) | collective-permute-done | bytes 49184 | tf_op jit(solution)/shard_map/ppermute | solution.py:374
  19.3 0.0 collective-permute-done.5.rest_6_
  19.3 2.3 %cross_tree.1 = (bf16[16,4096]{1,0:T(8,128)(2,1)}, f32[8,16]{1,0:T(8,128)}) custom-call(s32[8,128]{1,0:T(8,128)S(1)} %get-tuple-element.4.words_ref, f32[22,32,128]{2,1,0:T(8,128)S(1)} %get-tuple-element.5.rest_0_, f32[3,32,128]{2,1,0:T(8,128)S(1)} %collective-permute-done.rest_1_, f32[3,32,128]{2,1,0:T(8,128)S(1)} %collective-permute-done.1.rest_2_, ...), custom_call_target="tpu_custom_call" | custom-call | tf_op jit(solution)/shard_map/cross_tree/pallas_call | solution.py:452
  (8 shorter events, 0.1 us)
Async XLA Ops:
  2.7 10.9 %collective-permute-start.4 = (f32[5,32,128]{2,1,0:T(8,128)S(1)}, f32[5,32,128]{2,1,0:T(8,128)S(1)}, u32[]{:S(2)}, u32[]{:S(2)}) collective-permute-start(f32[5,32,128]{2,1,0:T(8,128)S(1)} %get-tuple-element.10), channel_id=1, source_target_pairs={{0,12},{1,13},{2,14},{3,15},{4,8},{5,9},{6,10},{7,11},{8,4},{9,5},... | collective-permute-start | bytes 245768 | tf_op jit(solution)/shard_map/ppermute | solution.py:374
  7.9 5.8 %collective-permute-start.3 = (f32[5,32,128]{2,1,0:T(8,128)S(1)}, f32[5,32,128]{2,1,0:T(8,128)S(1)}, u32[]{:S(2)}, u32[]{:S(2)}) collective-permute-start(f32[5,32,128]{2,1,0:T(8,128)S(1)} %get-tuple-element.11), channel_id=1, source_target_pairs={{0,4},{1,5},{2,6},{3,7},{4,0},{5,1},{6,2},{7,3},{8,12},{9,13},{10,... | collective-permute-start | bytes 245768 | tf_op jit(solution)/shard_map/ppermute | solution.py:374
  7.9 4.1 %collective-permute-start.2 = (f32[3,32,128]{2,1,0:T(8,128)S(1)}, f32[3,32,128]{2,1,0:T(8,128)S(1)}, u32[]{:S(2)}, u32[]{:S(2)}) collective-permute-start(f32[3,32,128]{2,1,0:T(8,128)S(1)} %get-tuple-element.12), channel_id=1, source_target_pairs={{0,3},{1,2},{2,1},{3,0},{4,7},{5,6},{6,5},{7,4},{8,11},{9,10},{10,... | collective-permute-start | bytes 147464 | tf_op jit(solution)/shard_map/ppermute | solution.py:374
  8.6 3.3 %collective-permute-start.1 = (f32[3,32,128]{2,1,0:T(8,128)S(1)}, f32[3,32,128]{2,1,0:T(8,128)S(1)}, u32[]{:S(2)}, u32[]{:S(2)}) collective-permute-start(f32[3,32,128]{2,1,0:T(8,128)S(1)} %get-tuple-element.13), channel_id=1, source_target_pairs={{0,1},{1,0},{2,3},{3,2},{4,5},{5,4},{6,7},{7,6},{8,9},{9,8},{10,11... | collective-permute-start | bytes 147464 | tf_op jit(solution)/shard_map/ppermute | solution.py:374
  9.6 4.1 %collective-permute-start = (f32[3,32,128]{2,1,0:T(8,128)S(1)}, f32[3,32,128]{2,1,0:T(8,128)S(1)}, u32[]{:S(2)}, u32[]{:S(2)}) collective-permute-start(f32[3,32,128]{2,1,0:T(8,128)S(1)} %get-tuple-element.14), channel_id=1, source_target_pairs={{0,2},{1,3},{2,0},{3,1},{4,6},{5,7},{6,4},{7,5},{8,10},{9,11},{10,... | collective-permute-start | bytes 147464 | tf_op jit(solution)/shard_map/ppermute | solution.py:374
  13.7 5.6 %collective-permute-start.5 = (f32[5,32,128]{2,1,0:T(8,128)S(1)}, f32[5,32,128]{2,1,0:T(8,128)S(1)}, u32[]{:S(2)}, u32[]{:S(2)}) collective-permute-start(f32[5,32,128]{2,1,0:T(8,128)S(1)} %constant_dynamic-update-slice_fusion), channel_id=1, source_target_pairs={{0,8},{1,9},{2,10},{3,11},{4,12},{5,13},{6,14},{7,15},{8,0},{9,1},... | collective-permute-start | bytes 245768 | tf_op jit(solution)/shard_map/ppermute | solution.py:374
  14.6 3.6 %collective-permute-start.8 = (f32[3,32,128]{2,1,0:T(8,128)S(1)}, f32[3,32,128]{2,1,0:T(8,128)S(1)}, u32[]{:S(2)}, u32[]{:S(2)}) collective-permute-start(f32[3,32,128]{2,1,0:T(8,128)S(1)} %get-tuple-element.25), channel_id=1, source_target_pairs={{0,3},{1,2},{2,1},{3,0},{4,7},{5,6},{6,5},{7,4},{8,11},{9,10},{10,... | collective-permute-start | bytes 147464 | tf_op jit(solution)/shard_map/ppermute | solution.py:374
  14.7 3.5 %collective-permute-start.7 = (f32[3,32,128]{2,1,0:T(8,128)S(1)}, f32[3,32,128]{2,1,0:T(8,128)S(1)}, u32[]{:S(2)}, u32[]{:S(2)}) collective-permute-start(f32[3,32,128]{2,1,0:T(8,128)S(1)} %get-tuple-element.26), channel_id=1, source_target_pairs={{0,1},{1,0},{2,3},{3,2},{4,5},{5,4},{6,7},{7,6},{8,9},{9,8},{10,11... | collective-permute-start | bytes 147464 | tf_op jit(solution)/shard_map/ppermute | solution.py:374
  15.2 4.1 %collective-permute-start.6 = (f32[3,32,128]{2,1,0:T(8,128)S(1)}, f32[3,32,128]{2,1,0:T(8,128)S(1)}, u32[]{:S(2)}, u32[]{:S(2)}) collective-permute-start(f32[3,32,128]{2,1,0:T(8,128)S(1)} %get-tuple-element.27), channel_id=1, source_target_pairs={{0,2},{1,3},{2,0},{3,1},{4,6},{5,7},{6,4},{7,5},{8,10},{9,11},{10,... | collective-permute-start | bytes 147464 | tf_op jit(solution)/shard_map/ppermute | solution.py:374

commit v10 on v9

--- a/solution.py
+++ b/solution.py
@@ -195,17 +195,15 @@
 
 def mean_path(mean, word, scratch, blocks, lane, row):
     value = mean
-    for step in range(0, len(PATH), 2):
-        shifts = []
-        for trials, spot in PATH[step : step + 2]:
+    for step in range(0, len(PATH), 3):
+        moves = []
+        for trials, spot in PATH[step : step + 3]:
             index = row >> (ROWS // trials).bit_length() - 1
-            shifts.append(2 * index + (word >> spot & 1))
-        ref = scratch[step // 2]
+            shift = 2 * index + (word >> spot & 1)
+            moves = moves + [shift] + [other + shift for other in moves]
+        ref = scratch[step // 3]
         ref[0:blocks, :] = value
-        near, far = shifts
-        value = (value + later(ref, blocks, lane, near)) + (
-            later(ref, blocks, lane, far) + later(ref, blocks, lane, near + far)
-        )
+        value = value + spread_sum(later(ref, blocks, lane, move) for move in moves)
     return value
 
 

time: 21.8 us -> 21.8 us (level)
  no operation moved by 1% of the time
where the time goes in v10:
time: 21.8 us; the launch traced here: 21.6 us
  starting transfers between devices  10.4 us (48%)
  waiting for transfers between devices  6.11 us (28%)
  Pallas kernels  4.36 us (20%)
  between operations  0.71 us (3%)
    ppermute x9, starting transfers between devices, swapped(): lax.ppermute(block, 'chan', [(device, device ^ distance) for device in ra...  10.4 us
    ppermute x9, waiting for transfers between devices, swapped(): lax.ppermute(block, 'chan', [(device, device ^ distance) for device in ra...  6.11 us
    pallas_call x1, Pallas kernels, shards(): result = call(words, *arrived, mean)  2.27 us
    pallas_call x1, Pallas kernels, local_rows(): pl.pallas_call(local_kernel, out_shape=(jax.ShapeDtypeStruct((4 * SPAN +...  2.09 us
  transfers between devices with their start and end apart: 9, of which 4 were waited for; matrix products, arithmetic and copies ran while one was open for 0% of the time, Pallas kernels for 0%

profile of v10, /device:TPU:0, one launch (start us, length us, event | category | flops | bytes accessed | tf_op | source)
XLA Modules:
  0.0 21.6 jit_solution(13386091336008709749)
XLA Ops:
  0.6 2.1 %local_tree.1 = (f32[22,32,128]{2,1,0:T(8,128)S(1)}, s32[8,128]{1,0:T(8,128)S(1)}) custom-call(s32[511]{0:T(512)} %table_hbm.1, s32[8]{0:T(128)} %width_hbm.1, bf16[64,4096]{1,0:T(8,128)(2,1)} %x_hbm.1), custom_call_target="tpu_custom_call" | custom-call | tf_op jit(solution)/shard_map/local_tree/pallas_call | solution.py:174
  2.7 5.1 %collective-permute-start.4 = (f32[5,32,128]{2,1,0:T(8,128)S(1)}, f32[5,32,128]{2,1,0:T(8,128)S(1)}, u32[]{:S(2)}, u32[]{:S(2)}) collective-permute-start(f32[5,32,128]{2,1,0:T(8,128)S(1)} %get-tuple-element.10), channel_id=1, source_target_pairs={{0,12},{1,13},{2,14},{3,15},{4,8},{5,9},{6,10},{7,11},{8,4},{9,5},... | collective-permute-start | bytes 245768 | tf_op jit(solution)/shard_map/ppermute | solution.py:372
  7.9 0.0 collective-permute-start.3
  7.9 0.7 %collective-permute-start.2 = (f32[3,32,128]{2,1,0:T(8,128)S(1)}, f32[3,32,128]{2,1,0:T(8,128)S(1)}, u32[]{:S(2)}, u32[]{:S(2)}) collective-permute-start(f32[3,32,128]{2,1,0:T(8,128)S(1)} %get-tuple-element.12), channel_id=1, source_target_pairs={{0,3},{1,2},{2,1},{3,0},{4,7},{5,6},{6,5},{7,4},{8,11},{9,10},{10,... | collective-permute-start | bytes 147464 | tf_op jit(solution)/shard_map/ppermute | solution.py:372
  8.6 1.0 %collective-permute-start.1 = (f32[3,32,128]{2,1,0:T(8,128)S(1)}, f32[3,32,128]{2,1,0:T(8,128)S(1)}, u32[]{:S(2)}, u32[]{:S(2)}) collective-permute-start(f32[3,32,128]{2,1,0:T(8,128)S(1)} %get-tuple-element.13), channel_id=1, source_target_pairs={{0,1},{1,0},{2,3},{3,2},{4,5},{5,4},{6,7},{7,6},{8,9},{9,8},{10,11... | collective-permute-start | bytes 147464 | tf_op jit(solution)/shard_map/ppermute | solution.py:372
  9.6 0.5 %collective-permute-start = (f32[3,32,128]{2,1,0:T(8,128)S(1)}, f32[3,32,128]{2,1,0:T(8,128)S(1)}, u32[]{:S(2)}, u32[]{:S(2)}) collective-permute-start(f32[3,32,128]{2,1,0:T(8,128)S(1)} %get-tuple-element.14), channel_id=1, source_target_pairs={{0,2},{1,3},{2,0},{3,1},{4,6},{5,7},{6,4},{7,5},{8,10},{9,11},{10,... | collective-permute-start | bytes 147464 | tf_op jit(solution)/shard_map/ppermute | solution.py:372
  10.1 1.9 %collective-permute-done.2.rest_3_ = f32[3,32,128]{2,1,0:T(8,128)S(1)} collective-permute-done((f32[3,32,128]{2,1,0:T(8,128)S(1)}, f32[3,32,128]{2,1,0:T(8,128)S(1)}, u32[]{:S(2)}, u32[]{:S(2)}) %collective-permute-start.2) | collective-permute-done | bytes 49184 | tf_op jit(solution)/shard_map/ppermute | solution.py:372
  11.9 0.0 collective-permute-done.1.rest_2_
  11.9 1.7 %collective-permute-done.rest_1_ = f32[3,32,128]{2,1,0:T(8,128)S(1)} collective-permute-done((f32[3,32,128]{2,1,0:T(8,128)S(1)}, f32[3,32,128]{2,1,0:T(8,128)S(1)}, u32[]{:S(2)}, u32[]{:S(2)}) %collective-permute-start) | collective-permute-done | bytes 49184 | tf_op jit(solution)/shard_map/ppermute | solution.py:372
  13.6 0.0 collective-permute-done.4.rest_5_
  13.6 0.0 collective-permute-done.3.rest_4_
  13.7 0.8 %collective-permute-start.5 = (f32[5,32,128]{2,1,0:T(8,128)S(1)}, f32[5,32,128]{2,1,0:T(8,128)S(1)}, u32[]{:S(2)}, u32[]{:S(2)}) collective-permute-start(f32[5,32,128]{2,1,0:T(8,128)S(1)} %constant_dynamic-update-slice_fusion), channel_id=1, source_target_pairs={{0,8},{1,9},{2,10},{3,11},{4,12},{5,13},{6,14},{7,15},{8,0},{9,1},... | collective-permute-start | bytes 245768 | tf_op jit(solution)/shard_map/ppermute | solution.py:372
  14.6 0.1 collective-permute-start.8
  14.7 0.6 %collective-permute-start.7 = (f32[3,32,128]{2,1,0:T(8,128)S(1)}, f32[3,32,128]{2,1,0:T(8,128)S(1)}, u32[]{:S(2)}, u32[]{:S(2)}) collective-permute-start(f32[3,32,128]{2,1,0:T(8,128)S(1)} %get-tuple-element.26), channel_id=1, source_target_pairs={{0,1},{1,0},{2,3},{3,2},{4,5},{5,4},{6,7},{7,6},{8,9},{9,8},{10,11... | collective-permute-start | bytes 147464 | tf_op jit(solution)/shard_map/ppermute | solution.py:372
  15.2 1.5 %collective-permute-start.6 = (f32[3,32,128]{2,1,0:T(8,128)S(1)}, f32[3,32,128]{2,1,0:T(8,128)S(1)}, u32[]{:S(2)}, u32[]{:S(2)}) collective-permute-start(f32[3,32,128]{2,1,0:T(8,128)S(1)} %get-tuple-element.27), channel_id=1, source_target_pairs={{0,2},{1,3},{2,0},{3,1},{4,6},{5,7},{6,4},{7,5},{8,10},{9,11},{10,... | collective-permute-start | bytes 147464 | tf_op jit(solution)/shard_map/ppermute | solution.py:372
  16.8 1.4 %collective-permute-done.8.rest_9_ = f32[3,32,128]{2,1,0:T(8,128)S(1)} collective-permute-done((f32[3,32,128]{2,1,0:T(8,128)S(1)}, f32[3,32,128]{2,1,0:T(8,128)S(1)}, u32[]{:S(2)}, u32[]{:S(2)}) %collective-permute-start.8) | collective-permute-done | bytes 49184 | tf_op jit(solution)/shard_map/ppermute | solution.py:372
  18.2 0.0 collective-permute-done.7.rest_8_
  18.2 1.2 %collective-permute-done.6.rest_7_ = f32[3,32,128]{2,1,0:T(8,128)S(1)} collective-permute-done((f32[3,32,128]{2,1,0:T(8,128)S(1)}, f32[3,32,128]{2,1,0:T(8,128)S(1)}, u32[]{:S(2)}, u32[]{:S(2)}) %collective-permute-start.6) | collective-permute-done | bytes 49184 | tf_op jit(solution)/shard_map/ppermute | solution.py:372
  19.3 0.0 collective-permute-done.5.rest_6_
  19.3 2.3 %cross_tree.1 = (bf16[16,4096]{1,0:T(8,128)(2,1)}, f32[8,16]{1,0:T(8,128)}) custom-call(s32[8,128]{1,0:T(8,128)S(1)} %get-tuple-element.4.words_ref, f32[22,32,128]{2,1,0:T(8,128)S(1)} %get-tuple-element.5.rest_0_, f32[3,32,128]{2,1,0:T(8,128)S(1)} %collective-permute-done.rest_1_, f32[3,32,128]{2,1,0:T(8,128)S(1)} %collective-permute-done.1.rest_2_, ...), custom_call_target="tpu_custom_call" | custom-call | tf_op jit(solution)/shard_map/cross_tree/pallas_call | solution.py:450
  (8 shorter events, 0.1 us)
Async XLA Ops:
  2.7 10.9 %collective-permute-start.4 = (f32[5,32,128]{2,1,0:T(8,128)S(1)}, f32[5,32,128]{2,1,0:T(8,128)S(1)}, u32[]{:S(2)}, u32[]{:S(2)}) collective-permute-start(f32[5,32,128]{2,1,0:T(8,128)S(1)} %get-tuple-element.10), channel_id=1, source_target_pairs={{0,12},{1,13},{2,14},{3,15},{4,8},{5,9},{6,10},{7,11},{8,4},{9,5},... | collective-permute-start | bytes 245768 | tf_op jit(solution)/shard_map/ppermute | solution.py:372
  7.9 5.8 %collective-permute-start.3 = (f32[5,32,128]{2,1,0:T(8,128)S(1)}, f32[5,32,128]{2,1,0:T(8,128)S(1)}, u32[]{:S(2)}, u32[]{:S(2)}) collective-permute-start(f32[5,32,128]{2,1,0:T(8,128)S(1)} %get-tuple-element.11), channel_id=1, source_target_pairs={{0,4},{1,5},{2,6},{3,7},{4,0},{5,1},{6,2},{7,3},{8,12},{9,13},{10,... | collective-permute-start | bytes 245768 | tf_op jit(solution)/shard_map/ppermute | solution.py:372
  7.9 4.1 %collective-permute-start.2 = (f32[3,32,128]{2,1,0:T(8,128)S(1)}, f32[3,32,128]{2,1,0:T(8,128)S(1)}, u32[]{:S(2)}, u32[]{:S(2)}) collective-permute-start(f32[3,32,128]{2,1,0:T(8,128)S(1)} %get-tuple-element.12), channel_id=1, source_target_pairs={{0,3},{1,2},{2,1},{3,0},{4,7},{5,6},{6,5},{7,4},{8,11},{9,10},{10,... | collective-permute-start | bytes 147464 | tf_op jit(solution)/shard_map/ppermute | solution.py:372
  8.6 3.3 %collective-permute-start.1 = (f32[3,32,128]{2,1,0:T(8,128)S(1)}, f32[3,32,128]{2,1,0:T(8,128)S(1)}, u32[]{:S(2)}, u32[]{:S(2)}) collective-permute-start(f32[3,32,128]{2,1,0:T(8,128)S(1)} %get-tuple-element.13), channel_id=1, source_target_pairs={{0,1},{1,0},{2,3},{3,2},{4,5},{5,4},{6,7},{7,6},{8,9},{9,8},{10,11... | collective-permute-start | bytes 147464 | tf_op jit(solution)/shard_map/ppermute | solution.py:372
  9.6 4.1 %collective-permute-start = (f32[3,32,128]{2,1,0:T(8,128)S(1)}, f32[3,32,128]{2,1,0:T(8,128)S(1)}, u32[]{:S(2)}, u32[]{:S(2)}) collective-permute-start(f32[3,32,128]{2,1,0:T(8,128)S(1)} %get-tuple-element.14), channel_id=1, source_target_pairs={{0,2},{1,3},{2,0},{3,1},{4,6},{5,7},{6,4},{7,5},{8,10},{9,11},{10,... | collective-permute-start | bytes 147464 | tf_op jit(solution)/shard_map/ppermute | solution.py:372
  13.7 5.6 %collective-permute-start.5 = (f32[5,32,128]{2,1,0:T(8,128)S(1)}, f32[5,32,128]{2,1,0:T(8,128)S(1)}, u32[]{:S(2)}, u32[]{:S(2)}) collective-permute-start(f32[5,32,128]{2,1,0:T(8,128)S(1)} %constant_dynamic-update-slice_fusion), channel_id=1, source_target_pairs={{0,8},{1,9},{2,10},{3,11},{4,12},{5,13},{6,14},{7,15},{8,0},{9,1},... | collective-permute-start | bytes 245768 | tf_op jit(solution)/shard_map/ppermute | solution.py:372
  14.6 3.6 %collective-permute-start.8 = (f32[3,32,128]{2,1,0:T(8,128)S(1)}, f32[3,32,128]{2,1,0:T(8,128)S(1)}, u32[]{:S(2)}, u32[]{:S(2)}) collective-permute-start(f32[3,32,128]{2,1,0:T(8,128)S(1)} %get-tuple-element.25), channel_id=1, source_target_pairs={{0,3},{1,2},{2,1},{3,0},{4,7},{5,6},{6,5},{7,4},{8,11},{9,10},{10,... | collective-permute-start | bytes 147464 | tf_op jit(solution)/shard_map/ppermute | solution.py:372
  14.7 3.5 %collective-permute-start.7 = (f32[3,32,128]{2,1,0:T(8,128)S(1)}, f32[3,32,128]{2,1,0:T(8,128)S(1)}, u32[]{:S(2)}, u32[]{:S(2)}) collective-permute-start(f32[3,32,128]{2,1,0:T(8,128)S(1)} %get-tuple-element.26), channel_id=1, source_target_pairs={{0,1},{1,0},{2,3},{3,2},{4,5},{5,4},{6,7},{7,6},{8,9},{9,8},{10,11... | collective-permute-start | bytes 147464 | tf_op jit(solution)/shard_map/ppermute | solution.py:372
  15.2 4.1 %collective-permute-start.6 = (f32[3,32,128]{2,1,0:T(8,128)S(1)}, f32[3,32,128]{2,1,0:T(8,128)S(1)}, u32[]{:S(2)}, u32[]{:S(2)}) collective-permute-start(f32[3,32,128]{2,1,0:T(8,128)S(1)} %get-tuple-element.27), channel_id=1, source_target_pairs={{0,2},{1,3},{2,0},{3,1},{4,6},{5,7},{6,4},{7,5},{8,10},{9,11},{10,... | collective-permute-start | bytes 147464 | tf_op jit(solution)/shard_map/ppermute | solution.py:372

commit v11 on v10

--- a/solution.py
+++ b/solution.py
@@ -231,7 +231,7 @@
         bands, trials = bands // 2, fresh
 
 
-def finish(rows, widths, out_ref, peaks_ref, values, prefix, split):
+def finish(rows, widths, out_ref, peaks_ref, values, prefix, *split):
     stride = rows.shape[1]
     blocks = stride - PAD
     length = blocks * LANES
@@ -246,22 +246,24 @@
         values[block] = value
         high = value.astype(jnp.bfloat16)
         rest = (value - high.astype(jnp.float32)).astype(jnp.bfloat16)
-        split[pl.ds(block * ROWS, ROWS), pl.ds(0, LANES)] = high
-        split[pl.ds(block * ROWS, ROWS), pl.ds(LANES, LANES)] = rest
+        ref, spot = split[block * 4 // blocks], block % (blocks // 4) * ROWS
+        ref[pl.ds(spot, ROWS), pl.ds(0, LANES)] = high
+        ref[pl.ds(spot, ROWS), pl.ds(LANES, LANES)] = rest
         total.append(value)
     centre = jnp.sum(spread_sum(total), axis=1, keepdims=True) / length
     centre = jnp.broadcast_to(centre, (ROWS, LANES))
     above = lax.broadcasted_iota(jnp.int32, (2 * LANES, 2 * LANES), 0) & 127
     across = lax.broadcasted_iota(jnp.int32, (2 * LANES, 2 * LANES), 1)
     weights = jnp.where(above <= across, 1.0, 0.0).astype(jnp.bfloat16)
-    sums = jnp.dot(split[...], weights, preferred_element_type=jnp.float32)
+    sums = [jnp.dot(ref[...], weights, preferred_element_type=jnp.float32) for ref in split]
     carry = jnp.zeros((ROWS, LANES), jnp.float32)
     prefix[0] = carry
     prefix[1] = carry
     ramp = centre * (lane + 1).astype(jnp.float32)
     drop = centre * LANES
     for block in range(blocks):
-        part = sums[block * ROWS : (block + 1) * ROWS]
+        spot = block % (blocks // 4) * ROWS
+        part = sums[block * 4 // blocks][spot : spot + ROWS]
         prefix[2 + block] = (part[:, :LANES] - ramp) + carry
         carry = carry + (part[:, LANES:] - drop)
 
@@ -299,7 +301,7 @@
     blocks = mean_ref.shape[1]
     lane = lane_index(blocks)
     if finishing:
-        out_ref, peaks_ref, first, final, *single, values, prefix, split = rest
+        out_ref, peaks_ref, first, final, *single, values, prefix, s0, s1, s2, s3 = rest
     else:
         series_ref, first, final, *single = rest
     words = [words_ref[0, index] for index in range(2 + WIDTHS // 4)]
@@ -330,7 +332,7 @@
     mean = mean / (channels * count)
     cross_tree(me, mean, words, buffers, spare, blocks, lane)
     if finishing:
-        finish(final, unpacked_widths(words), out_ref, peaks_ref, values, prefix, split)
+        finish(final, unpacked_widths(words), out_ref, peaks_ref, values, prefix, s0, s1, s2, s3)
     else:
         for trial in range(ROWS):
             series_ref[trial] = final[trial, pl.ds(0, blocks), :]
@@ -356,7 +358,7 @@
     return [
         pltpu.VMEM((blocks, ROWS, LANES), jnp.float32),
         pltpu.VMEM((blocks + 2, ROWS, LANES), jnp.float32),
-        pltpu.VMEM((blocks * ROWS, 2 * LANES), jnp.bfloat16),
+        *[pltpu.VMEM((blocks // 4 * ROWS, 2 * LANES), jnp.bfloat16)] * 4,
     ]
 
 

time: 21.8 us -> 21.8 us (level)
  no operation moved by 1% of the time
where the time goes in v11:
time: 21.8 us; the launch traced here: 21.6 us
  starting transfers between devices  10.4 us (48%)
  waiting for transfers between devices  6.11 us (28%)
  Pallas kernels  4.35 us (20%)
  between operations  0.71 us (3%)
    ppermute x9, starting transfers between devices, swapped(): lax.ppermute(block, 'chan', [(device, device ^ distance) for device in ra...  10.4 us
    ppermute x9, waiting for transfers between devices, swapped(): lax.ppermute(block, 'chan', [(device, device ^ distance) for device in ra...  6.11 us
    pallas_call x1, Pallas kernels, shards(): result = call(words, *arrived, mean)  2.26 us
    pallas_call x1, Pallas kernels, local_rows(): pl.pallas_call(local_kernel, out_shape=(jax.ShapeDtypeStruct((4 * SPAN +...  2.09 us
  transfers between devices with their start and end apart: 9, of which 4 were waited for; matrix products, arithmetic and copies ran while one was open for 0% of the time, Pallas kernels for 0%

profile of v11, /device:TPU:0, one launch (start us, length us, event | category | flops | bytes accessed | tf_op | source)
XLA Modules:
  0.0 21.6 jit_solution(17200676701380789199)
XLA Ops:
  0.6 2.1 %local_tree.1 = (f32[22,32,128]{2,1,0:T(8,128)S(1)}, s32[8,128]{1,0:T(8,128)S(1)}) custom-call(s32[511]{0:T(512)} %table_hbm.1, s32[8]{0:T(128)} %width_hbm.1, bf16[64,4096]{1,0:T(8,128)(2,1)} %x_hbm.1), custom_call_target="tpu_custom_call" | custom-call | tf_op jit(solution)/shard_map/local_tree/pallas_call | solution.py:174
  2.7 5.1 %collective-permute-start.4 = (f32[5,32,128]{2,1,0:T(8,128)S(1)}, f32[5,32,128]{2,1,0:T(8,128)S(1)}, u32[]{:S(2)}, u32[]{:S(2)}) collective-permute-start(f32[5,32,128]{2,1,0:T(8,128)S(1)} %get-tuple-element.10), channel_id=1, source_target_pairs={{0,12},{1,13},{2,14},{3,15},{4,8},{5,9},{6,10},{7,11},{8,4},{9,5},... | collective-permute-start | bytes 245768 | tf_op jit(solution)/shard_map/ppermute | solution.py:374
  7.9 0.0 collective-permute-start.3
  7.9 0.7 %collective-permute-start.2 = (f32[3,32,128]{2,1,0:T(8,128)S(1)}, f32[3,32,128]{2,1,0:T(8,128)S(1)}, u32[]{:S(2)}, u32[]{:S(2)}) collective-permute-start(f32[3,32,128]{2,1,0:T(8,128)S(1)} %get-tuple-element.12), channel_id=1, source_target_pairs={{0,3},{1,2},{2,1},{3,0},{4,7},{5,6},{6,5},{7,4},{8,11},{9,10},{10,... | collective-permute-start | bytes 147464 | tf_op jit(solution)/shard_map/ppermute | solution.py:374
  8.6 1.0 %collective-permute-start.1 = (f32[3,32,128]{2,1,0:T(8,128)S(1)}, f32[3,32,128]{2,1,0:T(8,128)S(1)}, u32[]{:S(2)}, u32[]{:S(2)}) collective-permute-start(f32[3,32,128]{2,1,0:T(8,128)S(1)} %get-tuple-element.13), channel_id=1, source_target_pairs={{0,1},{1,0},{2,3},{3,2},{4,5},{5,4},{6,7},{7,6},{8,9},{9,8},{10,11... | collective-permute-start | bytes 147464 | tf_op jit(solution)/shard_map/ppermute | solution.py:374
  9.6 0.5 %collective-permute-start = (f32[3,32,128]{2,1,0:T(8,128)S(1)}, f32[3,32,128]{2,1,0:T(8,128)S(1)}, u32[]{:S(2)}, u32[]{:S(2)}) collective-permute-start(f32[3,32,128]{2,1,0:T(8,128)S(1)} %get-tuple-element.14), channel_id=1, source_target_pairs={{0,2},{1,3},{2,0},{3,1},{4,6},{5,7},{6,4},{7,5},{8,10},{9,11},{10,... | collective-permute-start | bytes 147464 | tf_op jit(solution)/shard_map/ppermute | solution.py:374
  10.1 1.9 %collective-permute-done.2.rest_3_ = f32[3,32,128]{2,1,0:T(8,128)S(1)} collective-permute-done((f32[3,32,128]{2,1,0:T(8,128)S(1)}, f32[3,32,128]{2,1,0:T(8,128)S(1)}, u32[]{:S(2)}, u32[]{:S(2)}) %collective-permute-start.2) | collective-permute-done | bytes 49184 | tf_op jit(solution)/shard_map/ppermute | solution.py:374
  11.9 0.0 collective-permute-done.1.rest_2_
  11.9 1.7 %collective-permute-done.rest_1_ = f32[3,32,128]{2,1,0:T(8,128)S(1)} collective-permute-done((f32[3,32,128]{2,1,0:T(8,128)S(1)}, f32[3,32,128]{2,1,0:T(8,128)S(1)}, u32[]{:S(2)}, u32[]{:S(2)}) %collective-permute-start) | collective-permute-done | bytes 49184 | tf_op jit(solution)/shard_map/ppermute | solution.py:374
  13.6 0.0 collective-permute-done.4.rest_5_
  13.6 0.0 collective-permute-done.3.rest_4_
  13.7 0.8 %collective-permute-start.5 = (f32[5,32,128]{2,1,0:T(8,128)S(1)}, f32[5,32,128]{2,1,0:T(8,128)S(1)}, u32[]{:S(2)}, u32[]{:S(2)}) collective-permute-start(f32[5,32,128]{2,1,0:T(8,128)S(1)} %constant_dynamic-update-slice_fusion), channel_id=1, source_target_pairs={{0,8},{1,9},{2,10},{3,11},{4,12},{5,13},{6,14},{7,15},{8,0},{9,1},... | collective-permute-start | bytes 245768 | tf_op jit(solution)/shard_map/ppermute | solution.py:374
  14.6 0.1 collective-permute-start.8
  14.7 0.6 %collective-permute-start.7 = (f32[3,32,128]{2,1,0:T(8,128)S(1)}, f32[3,32,128]{2,1,0:T(8,128)S(1)}, u32[]{:S(2)}, u32[]{:S(2)}) collective-permute-start(f32[3,32,128]{2,1,0:T(8,128)S(1)} %get-tuple-element.26), channel_id=1, source_target_pairs={{0,1},{1,0},{2,3},{3,2},{4,5},{5,4},{6,7},{7,6},{8,9},{9,8},{10,11... | collective-permute-start | bytes 147464 | tf_op jit(solution)/shard_map/ppermute | solution.py:374
  15.2 1.5 %collective-permute-start.6 = (f32[3,32,128]{2,1,0:T(8,128)S(1)}, f32[3,32,128]{2,1,0:T(8,128)S(1)}, u32[]{:S(2)}, u32[]{:S(2)}) collective-permute-start(f32[3,32,128]{2,1,0:T(8,128)S(1)} %get-tuple-element.27), channel_id=1, source_target_pairs={{0,2},{1,3},{2,0},{3,1},{4,6},{5,7},{6,4},{7,5},{8,10},{9,11},{10,... | collective-permute-start | bytes 147464 | tf_op jit(solution)/shard_map/ppermute | solution.py:374
  16.8 1.4 %collective-permute-done.8.rest_9_ = f32[3,32,128]{2,1,0:T(8,128)S(1)} collective-permute-done((f32[3,32,128]{2,1,0:T(8,128)S(1)}, f32[3,32,128]{2,1,0:T(8,128)S(1)}, u32[]{:S(2)}, u32[]{:S(2)}) %collective-permute-start.8) | collective-permute-done | bytes 49184 | tf_op jit(solution)/shard_map/ppermute | solution.py:374
  18.2 0.0 collective-permute-done.7.rest_8_
  18.2 1.2 %collective-permute-done.6.rest_7_ = f32[3,32,128]{2,1,0:T(8,128)S(1)} collective-permute-done((f32[3,32,128]{2,1,0:T(8,128)S(1)}, f32[3,32,128]{2,1,0:T(8,128)S(1)}, u32[]{:S(2)}, u32[]{:S(2)}) %collective-permute-start.6) | collective-permute-done | bytes 49184 | tf_op jit(solution)/shard_map/ppermute | solution.py:374
  19.3 0.0 collective-permute-done.5.rest_6_
  19.3 2.3 %cross_tree.1 = (bf16[16,4096]{1,0:T(8,128)(2,1)}, f32[8,16]{1,0:T(8,128)}) custom-call(s32[8,128]{1,0:T(8,128)S(1)} %get-tuple-element.4.words_ref, f32[22,32,128]{2,1,0:T(8,128)S(1)} %get-tuple-element.5.rest_0_, f32[3,32,128]{2,1,0:T(8,128)S(1)} %collective-permute-done.rest_1_, f32[3,32,128]{2,1,0:T(8,128)S(1)} %collective-permute-done.1.rest_2_, ...), custom_call_target="tpu_custom_call" | custom-call | tf_op jit(solution)/shard_map/cross_tree/pallas_call | solution.py:452
  (8 shorter events, 0.1 us)
Async XLA Ops:
  2.7 10.9 %collective-permute-start.4 = (f32[5,32,128]{2,1,0:T(8,128)S(1)}, f32[5,32,128]{2,1,0:T(8,128)S(1)}, u32[]{:S(2)}, u32[]{:S(2)}) collective-permute-start(f32[5,32,128]{2,1,0:T(8,128)S(1)} %get-tuple-element.10), channel_id=1, source_target_pairs={{0,12},{1,13},{2,14},{3,15},{4,8},{5,9},{6,10},{7,11},{8,4},{9,5},... | collective-permute-start | bytes 245768 | tf_op jit(solution)/shard_map/ppermute | solution.py:374
  7.9 5.8 %collective-permute-start.3 = (f32[5,32,128]{2,1,0:T(8,128)S(1)}, f32[5,32,128]{2,1,0:T(8,128)S(1)}, u32[]{:S(2)}, u32[]{:S(2)}) collective-permute-start(f32[5,32,128]{2,1,0:T(8,128)S(1)} %get-tuple-element.11), channel_id=1, source_target_pairs={{0,4},{1,5},{2,6},{3,7},{4,0},{5,1},{6,2},{7,3},{8,12},{9,13},{10,... | collective-permute-start | bytes 245768 | tf_op jit(solution)/shard_map/ppermute | solution.py:374
  7.9 4.1 %collective-permute-start.2 = (f32[3,32,128]{2,1,0:T(8,128)S(1)}, f32[3,32,128]{2,1,0:T(8,128)S(1)}, u32[]{:S(2)}, u32[]{:S(2)}) collective-permute-start(f32[3,32,128]{2,1,0:T(8,128)S(1)} %get-tuple-element.12), channel_id=1, source_target_pairs={{0,3},{1,2},{2,1},{3,0},{4,7},{5,6},{6,5},{7,4},{8,11},{9,10},{10,... | collective-permute-start | bytes 147464 | tf_op jit(solution)/shard_map/ppermute | solution.py:374
  8.6 3.3 %collective-permute-start.1 = (f32[3,32,128]{2,1,0:T(8,128)S(1)}, f32[3,32,128]{2,1,0:T(8,128)S(1)}, u32[]{:S(2)}, u32[]{:S(2)}) collective-permute-start(f32[3,32,128]{2,1,0:T(8,128)S(1)} %get-tuple-element.13), channel_id=1, source_target_pairs={{0,1},{1,0},{2,3},{3,2},{4,5},{5,4},{6,7},{7,6},{8,9},{9,8},{10,11... | collective-permute-start | bytes 147464 | tf_op jit(solution)/shard_map/ppermute | solution.py:374
  9.6 4.1 %collective-permute-start = (f32[3,32,128]{2,1,0:T(8,128)S(1)}, f32[3,32,128]{2,1,0:T(8,128)S(1)}, u32[]{:S(2)}, u32[]{:S(2)}) collective-permute-start(f32[3,32,128]{2,1,0:T(8,128)S(1)} %get-tuple-element.14), channel_id=1, source_target_pairs={{0,2},{1,3},{2,0},{3,1},{4,6},{5,7},{6,4},{7,5},{8,10},{9,11},{10,... | collective-permute-start | bytes 147464 | tf_op jit(solution)/shard_map/ppermute | solution.py:374
  13.7 5.6 %collective-permute-start.5 = (f32[5,32,128]{2,1,0:T(8,128)S(1)}, f32[5,32,128]{2,1,0:T(8,128)S(1)}, u32[]{:S(2)}, u32[]{:S(2)}) collective-permute-start(f32[5,32,128]{2,1,0:T(8,128)S(1)} %constant_dynamic-update-slice_fusion), channel_id=1, source_target_pairs={{0,8},{1,9},{2,10},{3,11},{4,12},{5,13},{6,14},{7,15},{8,0},{9,1},... | collective-permute-start | bytes 245768 | tf_op jit(solution)/shard_map/ppermute | solution.py:374
  14.6 3.6 %collective-permute-start.8 = (f32[3,32,128]{2,1,0:T(8,128)S(1)}, f32[3,32,128]{2,1,0:T(8,128)S(1)}, u32[]{:S(2)}, u32[]{:S(2)}) collective-permute-start(f32[3,32,128]{2,1,0:T(8,128)S(1)} %get-tuple-element.25), channel_id=1, source_target_pairs={{0,3},{1,2},{2,1},{3,0},{4,7},{5,6},{6,5},{7,4},{8,11},{9,10},{10,... | collective-permute-start | bytes 147464 | tf_op jit(solution)/shard_map/ppermute | solution.py:374
  14.7 3.5 %collective-permute-start.7 = (f32[3,32,128]{2,1,0:T(8,128)S(1)}, f32[3,32,128]{2,1,0:T(8,128)S(1)}, u32[]{:S(2)}, u32[]{:S(2)}) collective-permute-start(f32[3,32,128]{2,1,0:T(8,128)S(1)} %get-tuple-element.26), channel_id=1, source_target_pairs={{0,1},{1,0},{2,3},{3,2},{4,5},{5,4},{6,7},{7,6},{8,9},{9,8},{10,11... | collective-permute-start | bytes 147464 | tf_op jit(solution)/shard_map/ppermute | solution.py:374
  15.2 4.1 %collective-permute-start.6 = (f32[3,32,128]{2,1,0:T(8,128)S(1)}, f32[3,32,128]{2,1,0:T(8,128)S(1)}, u32[]{:S(2)}, u32[]{:S(2)}) collective-permute-start(f32[3,32,128]{2,1,0:T(8,128)S(1)} %get-tuple-element.27), channel_id=1, source_target_pairs={{0,2},{1,3},{2,0},{3,1},{4,6},{5,7},{6,4},{7,5},{8,10},{9,11},{10,... | collective-permute-start | bytes 147464 | tf_op jit(solution)/shard_map/ppermute | solution.py:374
